TPU v7x, 256 devices: a whole 4x4x8 slice. The times are simulated.
256 devices in a mesh: pb: 16 (over x, z_hi), sa: 16 (over z_lo, y, core).
Axes of the slice: x: 4, y: 4, z: 8 (z_hi: 4, z_lo: 2; z = z_hi * 2 + z_lo), core: 2. Of those that a mesh axis runs over, the one named last changes fastest.
Arguments:
- question_states: bfloat16 [16, 16, 256, 768], P('pb', 'sa'), may hold values from -16 to 16
- question_ids: int32 [16, 16, 256], P('pb'), may hold values from 0 to 30521, as said below
- q_inner_weight: bfloat16 [768, 3072], P(None, 'sa'), may hold values from -0.21875 to 0.21875
- q_outer_weight: bfloat16 [3072, 768], P('sa'), may hold values from -0.109375 to 0.109375
- q_norm_gain: float32 [768], replicated, may hold values from 0.1 to 1.9
- sql_states: bfloat16 [16, 16, 256, 768], P('sa', 'pb'), may hold values from -16 to 16
- sql_ids: int32 [16, 16, 256], P('sa'), may hold values from 0 to 32099, as said below
- s_inner_weight: bfloat16 [768, 3072], P(None, 'pb'), may hold values from -0.21875 to 0.21875
- s_outer_weight: bfloat16 [3072, 768], P('pb'), may hold values from -0.109375 to 0.109375
- s_norm_gain: float32 [768], replicated, may hold values from 0.1 to 1.9
- positive_column: int32 [256], P('pb'), may hold values from 0 to 255, each once
Outputs:
- loss: float32 [], replicated
- q_inner_grad: float32 [768, 3072], P(None, 'sa')
- q_outer_grad: float32 [3072, 768], P('sa')
- q_gain_grad: float32 [768], replicated
- s_inner_grad: float32 [768, 3072], P(None, 'pb')
- s_outer_grad: float32 [3072, 768], P('pb')
- s_gain_grad: float32 [768], replicated
Inputs may be any that keep to these rules, and one draw needn't show every extreme that they name: `question_ids`: each sequence is a run of nonzero ids followed by padding zeros, the run 3 * 64 long or longer. `sql_ids`: each sequence is a run of nonzero ids followed by padding zeros, the run 3 * 64 long or longer.
All inputs are finite; a program needn't handle non-finite values.
Results may differ from a plain program's by a relative error of at most 0.0051.
Values may be sent and summed in bfloat16 or wider, within the bound.
A program may use at most 128 MiB of HBM per device.

v0:
```python
import functools
import math

import jax
import jax.numpy as jnp
from jax import lax
from jax.experimental import pallas as pl
from jax.experimental.pallas import tpu as pltpu
from jax.sharding import PartitionSpec as P

D = 768

MESH_AXES = ("pb", "sa")


def _peer(axis, p):
    return tuple(p if a == axis else lax.axis_index(a) for a in MESH_AXES)


def exchange(jobs, cid):
    arrays = [a for a, _, _ in jobs]
    kinds = [(ax, spread) for _, ax, spread in jobs]
    sizes = {ax: lax.axis_size(ax) for ax, _ in kinds}
    widest = max(sizes.values())
    count = len(jobs)

    def kernel(*refs):
        srcs, dsts = refs[:count], refs[count:2 * count]
        send, recv, local = refs[2 * count:]
        barrier = pltpu.get_barrier_semaphore()
        axes = list(dict.fromkeys(ax for ax, _ in kinds))
        total = 0
        for ax in axes:
            n = sizes[ax]
            me = lax.axis_index(ax)
            for s in range(1, n):
                pl.semaphore_signal(barrier, 1, device_id=_peer(ax, lax.rem(me + s, n)),
                                    device_id_type=pl.DeviceIdType.MESH)
            total += n - 1
        pl.semaphore_wait(barrier, total)
        started = []
        for t, (ax, spread) in enumerate(kinds):
            n = sizes[ax]
            me = lax.axis_index(ax)
            for s in range(1, n):
                p = lax.rem(me + s, n)
                src = srcs[t].at[p] if spread else srcs[t]
                c = pltpu.make_async_remote_copy(
                    src_ref=src, dst_ref=dsts[t].at[me], send_sem=send.at[t, s],
                    recv_sem=recv.at[t, s], device_id=_peer(ax, p),
                    device_id_type=pl.DeviceIdType.MESH)
                c.start()
                started.append(c)
            src = srcs[t].at[me] if spread else srcs[t]
            c = pltpu.make_async_copy(src, dsts[t].at[me], local.at[t])
            c.start()
            started.append(c)
        for c in started:
            c.wait()

    out_shape = []
    for a, (ax, spread) in zip(arrays, kinds):
        shape = a.shape if spread else (sizes[ax],) + a.shape
        out_shape.append(jax.ShapeDtypeStruct(shape, a.dtype))
    anywhere = pl.BlockSpec(memory_space=pl.ANY)
    return pl.pallas_call(
        kernel,
        out_shape=out_shape,
        in_specs=[anywhere] * count,
        out_specs=[anywhere] * count,
        scratch_shapes=[
            pltpu.SemaphoreType.DMA((count, widest)),
            pltpu.SemaphoreType.DMA((count, widest)),
            pltpu.SemaphoreType.DMA((count,)),
        ],
        compiler_params=pltpu.CompilerParams(collective_id=cid, has_side_effects=True),
    )(*arrays)


HIGH = lax.Precision.HIGHEST


def apply_rms_norm(input_float, norm_gain_vector, root_mean_square):
    if root_mean_square:
        input_normalized = input_float * lax.rsqrt(
            jnp.mean(input_float * input_float, axis=-1, keepdims=True) + 1e-06
        )
    else:
        mean_removed = input_float - jnp.mean(input_float, axis=-1, keepdims=True)
        input_normalized = mean_removed * lax.rsqrt(
            jnp.mean(mean_removed * mean_removed, axis=-1, keepdims=True) + 1e-05
        )
    return (input_normalized, (input_normalized * norm_gain_vector).astype(jnp.bfloat16))


def gelu_value(v):
    return 0.5 * v * (1.0 + lax.erf(v / math.sqrt(2.0)))


def gelu_slope(v):
    return 0.5 * (1.0 + lax.erf(v / math.sqrt(2.0))) + v * jnp.exp(-0.5 * v * v) / math.sqrt(
        2.0 * math.pi
    )


def pool_weights(ids):
    mask = (ids > 0).astype(jnp.float32)
    return mask / jnp.sum(mask, axis=-1, keepdims=True)


def tower_forward(tokens, ids, inner, gain, root_mean_square):
    count, length, width = tokens.shape
    input_float = tokens.astype(jnp.float32).reshape(count * length, width)
    input_normalized, normalized_rows = apply_rms_norm(input_float, gain, root_mean_square)
    pre = jnp.dot(normalized_rows, inner, preferred_element_type=jnp.float32)
    weights = pool_weights(ids)
    hidden = gelu_value(pre).reshape(count, length, -1)
    pooled = jnp.einsum("nt,ntf->nf", weights, hidden, precision=HIGH)
    resid = jnp.einsum(
        "nt,ntd->nd", weights, input_float.reshape(count, length, width), precision=HIGH
    )
    return input_normalized, normalized_rows, pre, weights, pooled, resid


def tower_backward(input_normalized, normalized_rows, pre, weights, inner, hidden_grad):
    count, length = weights.shape
    width = normalized_rows.shape[-1]
    slope = gelu_slope(pre).reshape(count, length, -1)
    dpre = (
        (weights[:, :, None] * hidden_grad[:, None, :] * slope)
        .reshape(count * length, -1)
        .astype(jnp.bfloat16)
    )
    high = input_normalized.astype(jnp.bfloat16)
    low = (input_normalized - high.astype(jnp.float32)).astype(jnp.bfloat16)
    rows = jnp.concatenate([normalized_rows, high, low], axis=1)
    both = lax.dot_general(
        dpre, rows, (((0,), (0,)), ((), ())), preferred_element_type=jnp.float32
    )
    inner_part = both[:, :width].T
    moment = both[:, width : 2 * width] + both[:, 2 * width :]
    gain_part = jnp.sum(inner.astype(jnp.float32).T * moment, axis=0)
    return inner_part, gain_part


def per_device(
    question_states,
    question_ids,
    q_inner_weight,
    q_outer_weight,
    q_norm_gain,
    sql_states,
    sql_ids,
    s_inner_weight,
    s_outer_weight,
    s_norm_gain,
    positive_column,
):
    scale = 1.0 / math.sqrt(D)
    q_place = lax.axis_index("sa")
    s_place = lax.axis_index("pb")
    q_tokens = lax.all_gather(question_states, "sa", axis=1, tiled=True)[0]
    s_tokens = lax.all_gather(sql_states, "pb", axis=1, tiled=True)[0]
    (positive_all,) = exchange([(positive_column.reshape(1, -1), "pb", False)], 0)
    positive_all = positive_all.reshape(-1)
    q_rows = q_tokens.shape[0]
    s_rows = s_tokens.shape[0]

    q_hat, q_normed, q_pre, q_weights, q_pooled, q_resid = tower_forward(
        q_tokens, question_ids[0], q_inner_weight, q_norm_gain, False
    )
    s_hat, s_normed, s_pre, s_weights, s_pooled, s_resid = tower_forward(
        s_tokens, sql_ids[0], s_inner_weight, s_norm_gain, True
    )
    q_outer_f = q_outer_weight.astype(jnp.float32)
    s_outer_f = s_outer_weight.astype(jnp.float32)
    q_terms, s_terms = exchange(
        [
            (jnp.dot(q_pooled, q_outer_f, precision=HIGH), "sa", False),
            (jnp.dot(s_pooled, s_outer_f, precision=HIGH), "pb", False),
        ],
        1,
    )
    q_block = jnp.sum(q_terms, axis=0) + q_resid
    s_block = jnp.sum(s_terms, axis=0) + s_resid
    q_embed, q_pooled_all, s_embed, s_pooled_all = exchange(
        [
            (q_block, "pb", False),
            (q_pooled, "pb", False),
            (s_block, "sa", False),
            (s_pooled, "sa", False),
        ],
        2,
    )
    q_embed = q_embed.reshape(-1, D)
    s_embed = s_embed.reshape(-1, D)
    q_pooled_all = q_pooled_all.reshape(-1, q_pooled.shape[-1])
    s_pooled_all = s_pooled_all.reshape(-1, s_pooled.shape[-1])
    score = scale * lax.dot_general(q_embed, s_embed, (((1,), (1,)), ((), ())), precision=HIGH)
    count = score.shape[0]
    match = (positive_all[:, None] == jnp.arange(count, dtype=jnp.int32)[None, :]).astype(
        jnp.float32
    )
    row_max = jnp.max(score, axis=1)
    row_lse = row_max + jnp.log(jnp.sum(jnp.exp(score - row_max[:, None]), axis=1))
    col_max = jnp.max(score, axis=0)
    col_lse = col_max + jnp.log(jnp.sum(jnp.exp(score - col_max[None, :]), axis=0))
    row_pos = jnp.sum(match * score, axis=1)
    col_pos = jnp.sum(match * score, axis=0)
    loss = (jnp.sum(row_lse - row_pos) + jnp.sum(col_lse - col_pos)) / (2.0 * count)
    dscore = 0.5 * (
        jnp.exp(score - row_lse[:, None]) + jnp.exp(score - col_lse[None, :]) - 2.0 * match
    )
    q_grad = scale * jnp.dot(dscore, s_embed, precision=HIGH)
    s_grad = scale * lax.dot_general(dscore, q_embed, (((0,), (0,)), ((), ())), precision=HIGH)

    q_outer_grad = lax.dot_general(q_pooled_all, q_grad, (((0,), (0,)), ((), ())), precision=HIGH)
    s_outer_grad = lax.dot_general(s_pooled_all, s_grad, (((0,), (0,)), ((), ())), precision=HIGH)
    q_grad_own = lax.dynamic_slice_in_dim(q_grad, s_place * q_rows, q_rows, 0)
    s_grad_own = lax.dynamic_slice_in_dim(s_grad, q_place * s_rows, s_rows, 0)
    q_hidden_grad = lax.dot_general(
        q_grad_own, q_outer_f, (((1,), (1,)), ((), ())), precision=HIGH
    )
    s_hidden_grad = lax.dot_general(
        s_grad_own, s_outer_f, (((1,), (1,)), ((), ())), precision=HIGH
    )
    q_inner_part, q_gain_part = tower_backward(
        q_hat, q_normed, q_pre, q_weights, q_inner_weight, q_hidden_grad
    )
    s_inner_part, s_gain_part = tower_backward(
        s_hat, s_normed, s_pre, s_weights, s_inner_weight, s_hidden_grad
    )
    q_pieces = q_inner_part.reshape(lax.axis_size("pb"), -1, q_inner_part.shape[-1])
    s_pieces = s_inner_part.reshape(lax.axis_size("sa"), -1, s_inner_part.shape[-1])
    gains = jnp.stack([q_gain_part, s_gain_part])
    q_pieces, s_pieces, gains = exchange(
        [(q_pieces, "pb", True), (s_pieces, "sa", True), (gains, "sa", False)], 3
    )
    q_inner_grad, s_inner_grad, gains = exchange(
        [
            (jnp.sum(q_pieces, axis=0), "pb", False),
            (jnp.sum(s_pieces, axis=0), "sa", False),
            (jnp.sum(gains, axis=0), "pb", False),
        ],
        4,
    )
    q_inner_grad = q_inner_grad.reshape(q_inner_part.shape)
    s_inner_grad = s_inner_grad.reshape(s_inner_part.shape)
    gains = jnp.sum(gains, axis=0)
    q_gain_grad, s_gain_grad = gains[0], gains[1]
    return (loss, q_inner_grad, q_outer_grad, q_gain_grad, s_inner_grad, s_outer_grad, s_gain_grad)


def solution(mesh):
    placed = (
        P("pb", "sa", None, None),
        P("pb", None, None),
        P(None, "sa"),
        P("sa", None),
        P(),
        P("sa", "pb", None, None),
        P("sa", None, None),
        P(None, "pb"),
        P("pb", None),
        P(),
        P("pb"),
    )
    return jax.shard_map(
        per_device,
        mesh=mesh,
        in_specs=placed,
        out_specs=(P(), P(None, "sa"), P("sa", None), P(), P(None, "pb"), P("pb", None), P()),
        check_vma=False,
    )
```

profile of v0, /device:TPU:1, one launch (start us, length us, event | category | flops | bytes accessed | tf_op | source)
XLA Modules:
  0.0 417.4 jit_solution(17802809574941479869)
XLA Ops:
  8.7 14.0 %shard_map.164 = s32[16,1,16]{2,1,0:T(1,128)} custom-call(s32[1,16]{1,0:T(1,128)} %bitcast.163), custom_call_target="tpu_custom_call" | custom-call | tf_op jit(solution)/shard_map/pallas_call | solution.py:66
  26.6 78.4 %all-gather.5.cloned.1.call-done = bf16[1,16,256,768]{3,2,0,1:T(8,128)(2,1)} async-done(((bf16[1,1,256,768]{3,2,0,1:T(8,128)(2,1)}), bf16[1,16,256,768]{3,2,0,1:T(8,128)(2,1)}) %all-gather.5.cloned.1.call-update) | async-done | bytes 6291472 | tf_op jit(solution)/shard_map/all_gather | solution.py:163
  105.0 4.1 multiply_reduce_fusion
  109.1 47.9 %all-gather.3.cloned.1.call-done = bf16[1,16,256,768]{3,2,0,1:T(8,128)(2,1)} async-done(((bf16[1,1,256,768]{3,2,0,1:T(8,128)(2,1)}), bf16[1,16,256,768]{3,2,0,1:T(8,128)(2,1)}) %all-gather.3.cloned.1.call-update) | async-done | bytes 6291472 | tf_op jit(solution)/shard_map/all_gather | solution.py:162
  157.1 3.8 convert_reduce_fusion
  163.7 5.9 %fusion.14 = (bf16[4096,768]{1,0:T(8,128)(2,1)}, bf16[4096,768]{1,0:T(8,128)(2,1)}, bf16[4096,768]{1,0:T(8,128)(2,1)S(1)}) fusion(bf16[1,16,256,768]{3,2,0,1:T(8,128)(2,1)S(1)} %copy-done.2, f32[4096]{0:T(1024)S(1)} %bitcast.162, f32[4096]{0:T(1024)S(1)} %bitcast.161, f32[768]{0:T(1024)S(1)} %copy-done.15), kind=kLoop, calls=%fused_computation.22 | loop fusion | flops 28311552 | bytes 25201664 | tf_op jit(solution)/shard_map/convert_element_type | solution.py:134
  169.5 3.5 multiply_multiply_fusion.3
  174.2 2.7 fusion.34
  178.4 5.6 %fusion.13 = (bf16[4096,768]{1,0:T(8,128)(2,1)}, bf16[4096,768]{1,0:T(8,128)(2,1)}, bf16[4096,768]{1,0:T(8,128)(2,1)S(1)}) fusion(bf16[1,16,256,768]{3,2,0,1:T(8,128)(2,1)S(1)} %bitcast.129, f32[4096]{0:T(1024)S(1)} %bitcast.154, f32[768]{0:T(1024)S(1)} %copy-done.14), kind=kLoop, calls=%fused_computation.21 | loop fusion | flops 25165824 | bytes 25185280 | tf_op jit(solution)/shard_map/convert_element_type | solution.py:134
  184.0 4.1 multiply_multiply_fusion.2
  188.1 2.7 fusion.31
  192.3 34.3 %shard_map.162 = (f32[16,16,768]{2,1,0:T(8,128)}, f32[16,16,768]{2,1,0:T(8,128)}) custom-call(f32[16,768]{1,0:T(8,128)} %fusion.77.refs_0_, f32[16,768]{1,0:T(8,128)} %fusion.78.refs_1_), custom_call_target="tpu_custom_call" | custom-call | tf_op jit(solution)/shard_map/pallas_call | solution.py:66
  229.0 5.5 %fusion.17 = f32[16,1,768]{2,1,0:T(1,128)S(1)} fusion(bf16[1,16,256,768]{3,2,0,1:T(8,128)(2,1)} %all-gather.3.cloned.1.call-done, f32[16,256,1]{1,0,2:T(8,128)S(1)} %get-tuple-element.76), kind=kOutput, calls=%fused_computation.26 | convolution fusion | flops 37748736 | bytes 6356992 | tf_op jit(solution)/shard_map/nt,ntd->nd/dot_general | solution.py:119
  234.5 5.3 %fusion.15 = f32[16,1,768]{2,1,0:T(1,128)S(1)} fusion(bf16[1,16,256,768]{3,2,0,1:T(8,128)(2,1)} %all-gather.5.cloned.1.call-done, f32[16,256,1]{1,0,2:T(8,128)S(1)} %get-tuple-element.74), kind=kOutput, calls=%fused_computation.24 | convolution fusion | flops 37748736 | bytes 6356992 | tf_op jit(solution)/shard_map/nt,ntd->nd/dot_general | solution.py:119
  240.5 45.4 %shard_map.163 = (f32[16,16,768]{2,1,0:T(8,128)}, f32[16,16,192]{2,1,0:T(8,128)}, f32[16,16,768]{2,1,0:T(8,128)}, f32[16,16,192]{2,1,0:T(8,128)}) custom-call(f32[16,768]{1,0:T(8,128)} %get-tuple-element.83.refs_0_, f32[16,192]{1,0:T(8,128)} %bitcast.159, f32[16,768]{1,0:T(8,128)} %get-tuple-element.82.refs_2_, f32[16,192]{1,0:T(8,128)} %bitcast.160), custom_call_target="tpu_custom_call" | custom-call | tf_op jit(solution)/shard_map/pallas_call | solution.py:66
  285.9 2.4 fusion.79
  289.7 2.2 convolution_multiply_fusion.1
  297.5 2.8 copy.49
  300.3 8.5 %fusion = f32[192,2304]{1,0:T(8,128)S(1)} fusion(bf16[4096,768]{1,0:T(8,128)(2,1)} %get-tuple-element.62, bf16[4096,768]{1,0:T(8,128)(2,1)S(1)} %bitcast.139, bf16[4096,768]{1,0:T(8,128)(2,1)S(1)} %bitcast.133, f32[4096,192]{0,1:T(8,128)S(1)} %copy-done.6, f32[4096,192]{0,1:T(8,128)S(1)} %bitcast.140, f32[4096]{0:T(1024)S(1)} %div.72), kind=kOutput, calls=%fused_computation | convolution fusion | flops 3689152512 | bytes 26951680 | tf_op jit(solution)/shard_map/dot_general | solution.py:137
  310.7 2.8 copy.52
  313.6 9.9 %fusion.6 = f32[192,2304]{1,0:T(8,128)S(1)} fusion(bf16[4096,768]{1,0:T(8,128)(2,1)} %get-tuple-element.65, bf16[4096,768]{1,0:T(8,128)(2,1)} %get-tuple-element.64, bf16[4096,768]{1,0:T(8,128)(2,1)S(1)} %bitcast.131, f32[4096,192]{0,1:T(8,128)S(1)} %copy-done.5, f32[4096,192]{0,1:T(8,128)S(1)} %bitcast.141, f32[4096]{0:T(1024)S(1)} %div.75), kind=kOutput, calls=%fused_computation.6 | convolution fusion | flops 3689152512 | bytes 26951680 | tf_op jit(solution)/shard_map/dot_general | solution.py:137
  325.4 34.6 %shard_map.165 = (f32[16,48,192]{2,1,0:T(8,128)}, f32[16,48,192]{2,1,0:T(8,128)}, f32[16,2,768]{2,1,0:T(2,128)}) custom-call(f32[16,48,192]{2,1,0:T(8,128)} %bitcast.146, f32[16,48,192]{2,1,0:T(8,128)} %bitcast.147, f32[2,768]{1,0:T(2,128)} %pad_maximum_fusion.refs_2_), custom_call_target="tpu_custom_call" | custom-call | tf_op jit(solution)/shard_map/pallas_call | solution.py:66
  365.2 36.8 %shard_map.166 = (f32[16,48,192]{2,1,0:T(8,128)}, f32[16,48,192]{2,1,0:T(8,128)}, f32[16,2,768]{2,1,0:T(2,128)}) custom-call(f32[48,192]{1,0:T(8,128)} %reduce_sum.186.refs_0_, f32[48,192]{1,0:T(8,128)} %reduce_sum.187.refs_1_, f32[2,768]{1,0:T(2,128)} %reduce_sum.188.refs_2_), custom_call_target="tpu_custom_call" | custom-call | tf_op jit(solution)/shard_map/pallas_call | solution.py:66
  402.0 2.2 copy.30
  (108 shorter events, 34.8 us)
Async XLA Ops:
  7.2 184.3 %copy-start = (bf16[192,768]{1,0:T(8,128)(2,1)S(1)}, bf16[192,768]{1,0:T(8,128)(2,1)}, u32[]{:S(2)}) copy-start(bf16[192,768]{1,0:T(8,128)(2,1)} %param.19) | copy-start | bytes 884740
  7.2 97.8 %all-gather.5.cloned.1.call-start = ((), (), s32[]{:S(2)}) async-start(), calls=%async_computation.1 | async-start | bytes 6684672 | tf_op jit(solution)/shard_map/all_gather | solution.py:163
  7.9 149.1 %all-gather.3.cloned.1.call-start = ((), (), s32[]{:S(2)}) async-start(), calls=%async_computation | async-start | bytes 6684672 | tf_op jit(solution)/shard_map/all_gather | solution.py:162
  157.1 4.6 %copy-start.2 = (bf16[1,16,256,768]{3,2,0,1:T(8,128)(2,1)S(1)}, bf16[1,16,256,768]{3,2,0,1:T(8,128)(2,1)}, u32[]{:S(2)}) copy-start(bf16[1,16,256,768]{3,2,0,1:T(8,128)(2,1)} %all-gather.3.cloned.1.call-done) | copy-start | bytes 18874372
  163.6 5.9 %copy-start.9 = (bf16[768,192]{0,1:T(8,128)(2,1)S(1)}, bf16[768,192]{0,1:T(8,128)(2,1)}, u32[]{:S(2)}) copy-start(bf16[768,192]{0,1:T(8,128)(2,1)} %param.13) | copy-start | bytes 884740
  169.5 4.7 %copy-start.4 = (bf16[4096,768]{1,0:T(8,128)(2,1)}, bf16[4096,768]{1,0:T(8,128)(2,1)S(1)}, u32[]{:S(2)}) copy-start(bf16[4096,768]{1,0:T(8,128)(2,1)S(1)} %get-tuple-element.63) | copy-start | bytes 18874372
  169.5 8.8 %slice-start = ((s8[6291456]{0:T(1024)(128)(4,1)}), s8[4194304]{0:T(1024)(128)(4,1)S(1)}, s32[]{:S(2)}) async-start(s8[6291456]{0:T(1024)(128)(4,1)} %bitcast.128), calls=%async_computation.2 | async-start | bytes 8388608
  169.5 8.8 %slice-start.1 = ((s8[6291456]{0:T(1024)(128)(4,1)}), s8[2097152]{0:T(1024)(128)(4,1)S(1)}, s32[]{:S(2)}) async-start(s8[6291456]{0:T(1024)(128)(4,1)} %bitcast.128), calls=%async_computation.3 | async-start | bytes 4194304
  174.2 3.3 copy-start.8
  174.2 4.2 copy-start.14
  178.4 5.6 %copy-start.10 = (bf16[768,192]{0,1:T(8,128)(2,1)S(1)}, bf16[768,192]{0,1:T(8,128)(2,1)}, u32[]{:S(2)}) copy-start(bf16[768,192]{0,1:T(8,128)(2,1)} %param.18) | copy-start | bytes 884740
  184.0 4.1 copy-start.3
  229.0 71.3 %slice-start.6 = ((s8[6291456]{0:T(1024)(128)(4,1)}), s8[2097152]{0:T(1024)(128)(4,1)S(1)}, s32[]{:S(2)}) async-start(s8[6291456]{0:T(1024)(128)(4,1)} %bitcast.138), calls=%async_computation.8 | async-start | bytes 4194304
  285.9 6.1 %copy-start.7 = (f32[16,16,768]{2,1,0:T(8,128)S(1)}, f32[16,16,768]{2,1,0:T(8,128)}, u32[]{:S(2)}) copy-start(f32[16,16,768]{2,1,0:T(8,128)} %get-tuple-element.21) | copy-start | bytes 2359300
  285.9 7.6 %copy-start.13 = (f32[16,16,192]{2,1,0:T(8,128)S(1)}, f32[16,16,192]{2,1,0:T(8,128)}, u32[]{:S(2)}) copy-start(f32[16,16,192]{2,1,0:T(8,128)} %get-tuple-element.30) | copy-start | bytes 589828
  288.5 7.0 %copy-start.12 = (f32[16,16,192]{2,1,0:T(8,128)S(1)}, f32[16,16,192]{2,1,0:T(8,128)}, u32[]{:S(2)}) copy-start(f32[16,16,192]{2,1,0:T(8,128)} %get-tuple-element.27) | copy-start | bytes 589828
  289.7 10.6 %slice-start.7 = ((s8[6291456]{0:T(1024)(128)(4,1)}), s8[4194304]{0:T(1024)(128)(4,1)S(1)}, s32[]{:S(2)}) async-start(s8[6291456]{0:T(1024)(128)(4,1)} %bitcast.138), calls=%async_computation.9 | async-start | bytes 8388608
  293.5 6.8 %slice-start.4 = ((s8[6291456]{0:T(1024)(128)(4,1)}), s8[4194304]{0:T(1024)(128)(4,1)S(1)}, s32[]{:S(2)}) async-start(s8[6291456]{0:T(1024)(128)(4,1)} %bitcast.132), calls=%async_computation.6 | async-start | bytes 8388608
  297.0 3.3 slice-start.5
  308.9 4.6 %slice-start.2 = ((s8[6291456]{0:T(1024)(128)(4,1)}), s8[2097152]{0:T(1024)(128)(4,1)S(1)}, s32[]{:S(2)}) async-start(s8[6291456]{0:T(1024)(128)(4,1)} %bitcast.130), calls=%async_computation.4 | async-start | bytes 4194304
  310.2 3.3 slice-start.3
  310.7 2.8 copy-start.5
  313.5 9.9 %copy-start.11 = (bf16[768,192]{0,1:T(8,128)(2,1)S(1)}, bf16[768,192]{0,1:T(8,128)(2,1)}, u32[]{:S(2)}) copy-start(bf16[768,192]{0,1:T(8,128)(2,1)} %param.18) | copy-start | bytes 884740
  325.4 83.8 %copy-start.1 = (bf16[192,768]{1,0:T(8,128)(2,1)S(1)}, bf16[192,768]{1,0:T(8,128)(2,1)}, u32[]{:S(2)}) copy-start(bf16[192,768]{1,0:T(8,128)(2,1)} %param.19) | copy-start | bytes 884740
  (2 other events, 4.8 us)
Sparse Core Ops, SparseCore 0:
  10.5 94.4 all-gather.4
  106.8 50.1 all-gather.2
where the time goes:
time: 426 us; the launch traced here: 417 us
  Pallas kernels  165 us (39%)
  waiting for transfers between devices  128 us (30%)
  matrix products  53.5 us (13%)
  other arithmetic  36 us (8%)
  local copies, waits for them, and re-layouts  17.7 us (4%)
  between operations  17.2 us (4%)
    pallas_call x5, Pallas kernels, exchange(): pl.pallas_call(kernel, out_shape=out_shape, in_specs=[anywhere] * count,...  165 us
    all_gather x1, waiting for transfers between devices, per_device(): s_tokens = lax.all_gather(sql_states, 'pb', axis=1, tiled=True)[0]  78.4 us
    all_gather x1, waiting for transfers between devices, per_device(): q_tokens = lax.all_gather(question_states, 'sa', axis=1, tiled=True)[0]  47.9 us
    dot_general x2, matrix products, tower_backward(): lax.dot_general(dpre, rows, (((0,), (0,)), ((), ())), preferred_element_t...  18.4 us
    unnamed x59, local copies, waits for them, and re-layouts  12 us
    convert_element_type x2, other arithmetic, tower_backward(): high = input_normalized.astype(jnp.bfloat16)  11.5 us
    dot_general x2, matrix products, tower_forward(): jnp.einsum('nt,ntd->nd', weights, input_float.reshape(count, length, widt...  10.8 us
  transfers between devices with their start and end apart: 2, of which 2 were waited for; matrix products, arithmetic and copies ran while one was open for 2% of the time, Pallas kernels for 3%

commit v1 on v0

--- a/solution.py
+++ b/solution.py
@@ -131,9 +131,11 @@
         .reshape(count * length, -1)
         .astype(jnp.bfloat16)
     )
-    high = input_normalized.astype(jnp.bfloat16)
-    low = (input_normalized - high.astype(jnp.float32)).astype(jnp.bfloat16)
-    rows = jnp.concatenate([normalized_rows, high, low], axis=1)
+    high = lax.reduce_precision(input_normalized, exponent_bits=8, mantissa_bits=7)
+    low = input_normalized - high
+    rows = jnp.concatenate(
+        [normalized_rows, high.astype(jnp.bfloat16), low.astype(jnp.bfloat16)], axis=1
+    )
     both = lax.dot_general(
         dpre, rows, (((0,), (0,)), ((), ())), preferred_element_type=jnp.float32
     )
@@ -160,6 +162,7 @@
     q_place = lax.axis_index("sa")
     s_place = lax.axis_index("pb")
     q_tokens = lax.all_gather(question_states, "sa", axis=1, tiled=True)[0]
+    q_tokens, sql_states = lax.optimization_barrier((q_tokens, sql_states))
     s_tokens = lax.all_gather(sql_states, "pb", axis=1, tiled=True)[0]
     (positive_all,) = exchange([(positive_column.reshape(1, -1), "pb", False)], 0)
     positive_all = positive_all.reshape(-1)

time: 426 us -> 400 us (0.939)
  waiting for transfers between devices: 128 us -> 107 us
    all_gather x1, waiting for transfers between devices: 78.4 us -> 55.2 us  [per_device(): s_tokens = lax.all_gather(sql_states, 'pb', axis=1, tiled=True)[0]]
    unnamed x59 -> x57, local copies, waits for them, and re-layouts: 12 us -> 11.2 us
  transfers between devices with their start and end apart: 2 -> 2, of which waited for: 2 -> 2; matrix products, arithmetic and copies ran while one was open for 2% -> 7% of each run, Pallas kernels for 3% -> 3%
where the time goes in v1:
time: 400 us; the launch traced here: 395 us
  Pallas kernels  166 us (42%)
  waiting for transfers between devices  107 us (27%)
  matrix products  50.1 us (13%)
  other arithmetic  37.5 us (9%)
  between operations  17.2 us (4%)
  local copies, waits for them, and re-layouts  16.9 us (4%)
    pallas_call x5, Pallas kernels, exchange(): pl.pallas_call(kernel, out_shape=out_shape, in_specs=[anywhere] * count,...  166 us
    all_gather x1, waiting for transfers between devices, per_device(): s_tokens = lax.all_gather(sql_states, 'pb', axis=1, tiled=True)[0]  55.2 us
    all_gather x1, waiting for transfers between devices, per_device(): q_tokens = lax.all_gather(question_states, 'sa', axis=1, tiled=True)[0]  51.1 us
    dot_general x2, matrix products, tower_backward(): lax.dot_general(dpre, rows, (((0,), (0,)), ((), ())), preferred_element_t...  18.2 us
    convert_element_type x2, other arithmetic, tower_backward(): high.astype(jnp.bfloat16)  12.3 us
    unnamed x57, local copies, waits for them, and re-layouts  11.2 us
  transfers between devices with their start and end apart: 2, of which 2 were waited for; matrix products, arithmetic and copies ran while one was open for 7% of the time, Pallas kernels for 3%

profile of v1, /device:TPU:1, one launch (start us, length us, event | category | flops | bytes accessed | tf_op | source)
XLA Modules:
  0.0 395.1 jit_solution(16745138991222066184)
XLA Ops:
  8.0 51.1 %all-gather.3.cloned.1.call-done = bf16[1,16,256,768]{3,2,0,1:T(8,128)(2,1)} async-done(((bf16[1,1,256,768]{3,2,0,1:T(8,128)(2,1)}), bf16[1,16,256,768]{3,2,0,1:T(8,128)(2,1)}) %all-gather.3.cloned.1.call-update) | async-done | bytes 6291472 | tf_op jit(solution)/shard_map/all_gather | solution.py:164
  59.1 10.7 %shard_map.164 = s32[16,1,16]{2,1,0:T(1,128)} custom-call(s32[1,16]{1,0:T(1,128)} %bitcast.160), custom_call_target="tpu_custom_call" | custom-call | tf_op jit(solution)/shard_map/pallas_call | solution.py:66
  73.7 4.1 %convert_reduce_fusion = f32[16,256]{1,0:T(8,128)S(1)} fusion(bf16[16,256,768]{2,1,0:T(8,128)(2,1)} %bitcast.123), kind=kLoop, calls=%fused_computation.25 | loop fusion | flops 6287360 | bytes 6307840 | tf_op jit(solution)/shard_map/reduce_sum | solution.py:89
  80.6 6.5 %reduce-precision_convert_fusion.1 = (bf16[4096,768]{1,0:T(8,128)(2,1)}, bf16[4096,768]{1,0:T(8,128)(2,1)}, bf16[4096,768]{1,0:T(8,128)(2,1)S(1)}) fusion(bf16[16,256,768]{2,1,0:T(8,128)(2,1)S(1)} %bitcast.125, f32[4096]{0:T(1024)S(1)} %bitcast.159, f32[4096]{0:T(1024)S(1)} %bitcast.158, f32[768]{0:T(1024)S(1)} %copy-done.16), kind=kLoop, calls=%fused_computation.15 | loop fusion | flops 28311552 | bytes 25201664 | tf_op jit(solution)/shard_map/convert_element_type | solution.py:137
  87.1 3.7 multiply_multiply_fusion.3
  90.8 2.7 fusion.32
  95.0 2.5 fusion.62
  97.5 55.2 %all-gather.5.cloned.1.call-done = bf16[1,16,256,768]{3,2,0,1:T(8,128)(2,1)} async-done(((bf16[1,1,256,768]{3,2,0,1:T(8,128)(2,1)}), bf16[1,16,256,768]{3,2,0,1:T(8,128)(2,1)}) %all-gather.5.cloned.1.call-update) | async-done | bytes 6291472 | tf_op jit(solution)/shard_map/all_gather | solution.py:166
  152.7 4.2 %multiply_reduce_fusion = f32[16,256]{1,0:T(8,128)S(1)} fusion(bf16[1,16,256,768]{3,2,0,1:T(8,128)(2,1)} %all-gather.5.cloned.1.call-done), kind=kLoop, calls=%fused_computation.22 | loop fusion | flops 9433088 | bytes 6307840 | tf_op jit(solution)/shard_map/reduce_sum | solution.py:86
  157.3 5.8 %reduce-precision_convert_fusion = (bf16[4096,768]{1,0:T(8,128)(2,1)}, bf16[4096,768]{1,0:T(8,128)(2,1)}, bf16[4096,768]{1,0:T(8,128)(2,1)S(1)}) fusion(bf16[1,16,256,768]{3,2,0,1:T(8,128)(2,1)S(1)} %copy-done.3, f32[4096]{0:T(1024)S(1)} %bitcast.151, f32[768]{0:T(1024)S(1)} %copy-done.15), kind=kLoop, calls=%fused_computation.13 | loop fusion | flops 25165824 | bytes 25185280 | tf_op jit(solution)/shard_map/convert_element_type | solution.py:137
  163.1 3.8 multiply_multiply_fusion.2
  166.9 2.7 fusion.29
  171.1 41.0 %shard_map.162 = (f32[16,16,768]{2,1,0:T(8,128)}, f32[16,16,768]{2,1,0:T(8,128)}) custom-call(f32[16,768]{1,0:T(8,128)} %fusion.76.refs_0_, f32[16,768]{1,0:T(8,128)} %fusion.77.refs_1_), custom_call_target="tpu_custom_call" | custom-call | tf_op jit(solution)/shard_map/pallas_call | solution.py:66
  214.7 5.3 %fusion.15 = f32[16,1,768]{2,1,0:T(1,128)S(1)} fusion(bf16[1,16,256,768]{3,2,0,1:T(8,128)(2,1)} %all-gather.5.cloned.1.call-done, f32[16,256,1]{1,0,2:T(8,128)S(1)} %get-tuple-element.78), kind=kOutput, calls=%fused_computation.26 | convolution fusion | flops 37748736 | bytes 6356992 | tf_op jit(solution)/shard_map/nt,ntd->nd/dot_general | solution.py:119
  220.6 40.8 %shard_map.163 = (f32[16,16,768]{2,1,0:T(8,128)}, f32[16,16,192]{2,1,0:T(8,128)}, f32[16,16,768]{2,1,0:T(8,128)}, f32[16,16,192]{2,1,0:T(8,128)}) custom-call(f32[16,768]{1,0:T(8,128)} %get-tuple-element.87.refs_0_, f32[16,192]{1,0:T(8,128)} %bitcast.156, f32[16,768]{1,0:T(8,128)} %get-tuple-element.86.refs_2_, f32[16,192]{1,0:T(8,128)} %bitcast.157), custom_call_target="tpu_custom_call" | custom-call | tf_op jit(solution)/shard_map/pallas_call | solution.py:66
  261.4 2.4 fusion.78
  272.9 2.8 copy.49
  275.8 8.5 %fusion = f32[192,2304]{1,0:T(8,128)S(1)} fusion(bf16[4096,768]{1,0:T(8,128)(2,1)} %get-tuple-element.66, bf16[4096,768]{1,0:T(8,128)(2,1)S(1)} %bitcast.136, bf16[4096,768]{1,0:T(8,128)(2,1)S(1)} %bitcast.128, f32[4096,192]{0,1:T(8,128)S(1)} %copy-done.6, f32[4096,192]{0,1:T(8,128)S(1)} %bitcast.137, f32[4096]{0:T(1024)S(1)} %div.72), kind=kOutput, calls=%fused_computation | convolution fusion | flops 3689152512 | bytes 26951680 | tf_op jit(solution)/shard_map/dot_general | solution.py:139
  286.1 2.8 copy.52
  289.0 9.7 %fusion.6 = f32[192,2304]{1,0:T(8,128)S(1)} fusion(bf16[4096,768]{1,0:T(8,128)(2,1)} %get-tuple-element.69, bf16[4096,768]{1,0:T(8,128)(2,1)} %get-tuple-element.68, bf16[4096,768]{1,0:T(8,128)(2,1)S(1)} %bitcast.130, f32[4096,192]{0,1:T(8,128)S(1)} %copy-done.7, f32[4096,192]{0,1:T(8,128)S(1)} %bitcast.138, f32[4096]{0:T(1024)S(1)} %div.75), kind=kOutput, calls=%fused_computation.6 | convolution fusion | flops 3689152512 | bytes 26951680 | tf_op jit(solution)/shard_map/dot_general | solution.py:139
  300.6 38.4 %shard_map.165 = (f32[16,48,192]{2,1,0:T(8,128)}, f32[16,48,192]{2,1,0:T(8,128)}, f32[16,2,768]{2,1,0:T(2,128)}) custom-call(f32[16,48,192]{2,1,0:T(8,128)} %bitcast.143, f32[16,48,192]{2,1,0:T(8,128)} %bitcast.144, f32[2,768]{1,0:T(2,128)} %pad_maximum_fusion.refs_2_), custom_call_target="tpu_custom_call" | custom-call | tf_op jit(solution)/shard_map/pallas_call | solution.py:66
  344.2 35.5 %shard_map.166 = (f32[16,48,192]{2,1,0:T(8,128)}, f32[16,48,192]{2,1,0:T(8,128)}, f32[16,2,768]{2,1,0:T(2,128)}) custom-call(f32[48,192]{1,0:T(8,128)} %reduce_sum.186.refs_0_, f32[48,192]{1,0:T(8,128)} %reduce_sum.187.refs_1_, f32[2,768]{1,0:T(2,128)} %reduce_sum.188.refs_2_), custom_call_target="tpu_custom_call" | custom-call | tf_op jit(solution)/shard_map/pallas_call | solution.py:66
  379.7 2.2 copy.30
  383.4 2.2 copy.31
  (105 shorter events, 33.4 us)
Async XLA Ops:
  7.2 163.1 %copy-start = (bf16[192,768]{1,0:T(8,128)(2,1)S(1)}, bf16[192,768]{1,0:T(8,128)(2,1)}, u32[]{:S(2)}) copy-start(bf16[192,768]{1,0:T(8,128)(2,1)} %param.19) | copy-start | bytes 884740
  7.2 51.9 %all-gather.3.cloned.1.call-start = ((), (), s32[]{:S(2)}) async-start(), calls=%async_computation | async-start | bytes 6684672 | tf_op jit(solution)/shard_map/all_gather | solution.py:164
  7.9 144.8 %all-gather.5.cloned.1.call-start = ((), (), s32[]{:S(2)}) async-start(), calls=%async_computation.1 | async-start | bytes 6684672 | tf_op jit(solution)/shard_map/all_gather | solution.py:166
  73.7 4.9 %copy-start.2 = (bf16[1,16,256,768]{3,2,0,1:T(8,128)(2,1)S(1)}, bf16[1,16,256,768]{3,2,0,1:T(8,128)(2,1)}, u32[]{:S(2)}) copy-start(bf16[1,16,256,768]{3,2,0,1:T(8,128)(2,1)} %all-gather.3.cloned.1.call-done) | copy-start | bytes 18874372
  80.6 6.6 %copy-start.10 = (bf16[768,192]{0,1:T(8,128)(2,1)S(1)}, bf16[768,192]{0,1:T(8,128)(2,1)}, u32[]{:S(2)}) copy-start(bf16[768,192]{0,1:T(8,128)(2,1)} %param.13) | copy-start | bytes 884740
  87.1 3.7 copy-start.4
  90.8 3.3 copy-start.9
  97.5 59.5 %copy-start.15 = (f32[768]{0:T(1024)S(1)}, f32[768]{0:T(1024)}, u32[]{:S(2)}) copy-start(f32[768]{0:T(1024)} %param.20) | copy-start | bytes 9220
  152.7 4.6 %copy-start.3 = (bf16[1,16,256,768]{3,2,0,1:T(8,128)(2,1)S(1)}, bf16[1,16,256,768]{3,2,0,1:T(8,128)(2,1)}, u32[]{:S(2)}) copy-start(bf16[1,16,256,768]{3,2,0,1:T(8,128)(2,1)} %all-gather.5.cloned.1.call-done) | copy-start | bytes 18874372
  157.3 5.8 %copy-start.11 = (bf16[768,192]{0,1:T(8,128)(2,1)S(1)}, bf16[768,192]{0,1:T(8,128)(2,1)}, u32[]{:S(2)}) copy-start(bf16[768,192]{0,1:T(8,128)(2,1)} %param.18) | copy-start | bytes 884740
  163.1 3.8 copy-start.5
  212.1 63.6 %slice-start.4 = ((s8[6291456]{0:T(1024)(128)(4,1)}), s8[2097152]{0:T(1024)(128)(4,1)S(1)}, s32[]{:S(2)}) async-start(s8[6291456]{0:T(1024)(128)(4,1)} %bitcast.135), calls=%async_computation.6 | async-start | bytes 4194304
  261.4 5.9 %copy-start.8 = (f32[16,16,768]{2,1,0:T(8,128)S(1)}, f32[16,16,768]{2,1,0:T(8,128)}, u32[]{:S(2)}) copy-start(f32[16,16,768]{2,1,0:T(8,128)} %get-tuple-element.25) | copy-start | bytes 2359300
  261.4 7.3 %copy-start.14 = (f32[16,16,192]{2,1,0:T(8,128)S(1)}, f32[16,16,192]{2,1,0:T(8,128)}, u32[]{:S(2)}) copy-start(f32[16,16,192]{2,1,0:T(8,128)} %get-tuple-element.34) | copy-start | bytes 589828
  264.1 6.6 %copy-start.13 = (f32[16,16,192]{2,1,0:T(8,128)S(1)}, f32[16,16,192]{2,1,0:T(8,128)}, u32[]{:S(2)}) copy-start(f32[16,16,192]{2,1,0:T(8,128)} %get-tuple-element.31) | copy-start | bytes 589828
  267.4 8.4 %slice-start.5 = ((s8[6291456]{0:T(1024)(128)(4,1)}), s8[4194304]{0:T(1024)(128)(4,1)S(1)}, s32[]{:S(2)}) async-start(s8[6291456]{0:T(1024)(128)(4,1)} %bitcast.135), calls=%async_computation.7 | async-start | bytes 8388608
  268.7 7.0 %slice-start = ((s8[6291456]{0:T(1024)(128)(4,1)}), s8[4194304]{0:T(1024)(128)(4,1)S(1)}, s32[]{:S(2)}) async-start(s8[6291456]{0:T(1024)(128)(4,1)} %bitcast.127), calls=%async_computation.2 | async-start | bytes 8388608
  272.5 3.3 slice-start.1
  272.9 2.8 copy-start.6
  284.3 4.6 %slice-start.2 = ((s8[6291456]{0:T(1024)(128)(4,1)}), s8[2097152]{0:T(1024)(128)(4,1)S(1)}, s32[]{:S(2)}) async-start(s8[6291456]{0:T(1024)(128)(4,1)} %bitcast.129), calls=%async_computation.4 | async-start | bytes 4194304
  285.7 3.3 slice-start.3
  286.1 2.8 copy-start.7
  289.0 9.7 %copy-start.12 = (bf16[768,192]{0,1:T(8,128)(2,1)S(1)}, bf16[768,192]{0,1:T(8,128)(2,1)}, u32[]{:S(2)}) copy-start(bf16[768,192]{0,1:T(8,128)(2,1)} %param.18) | copy-start | bytes 884740
  300.6 86.3 %copy-start.1 = (bf16[192,768]{1,0:T(8,128)(2,1)S(1)}, bf16[192,768]{1,0:T(8,128)(2,1)}, u32[]{:S(2)}) copy-start(bf16[192,768]{1,0:T(8,128)(2,1)} %param.19) | copy-start | bytes 884740
  (1 other events, 2.0 us)
Sparse Core Ops, SparseCore 0:
  9.9 49.1 all-gather.2
  61.5 91.1 all-gather.4

commit v2 on v1

--- a/solution.py
+++ b/solution.py
@@ -77,6 +77,69 @@
     )(*arrays)
 
 
+def pair_gather(block, cid):
+    n = lax.axis_size("sa")
+    half = n // 2
+
+    def kernel(src, dst, send, recv, relay_send, relay_recv, pair_send, pair_recv, local):
+        me = lax.axis_index("sa")
+        partner = me + 1 - 2 * lax.rem(me, 2)
+        barrier = pltpu.get_barrier_semaphore()
+        for s in range(1, half):
+            pl.semaphore_signal(barrier, 1, device_id=_peer("sa", lax.rem(me + 2 * s, n)),
+                                device_id_type=pl.DeviceIdType.MESH)
+        pl.semaphore_signal(barrier, 1, device_id=_peer("sa", partner),
+                            device_id_type=pl.DeviceIdType.MESH)
+        pl.semaphore_wait(barrier, half)
+        own = pltpu.make_async_copy(src, dst.at[me], local.at[0])
+        own.start()
+        pair = pltpu.make_async_remote_copy(
+            src_ref=src, dst_ref=dst.at[me], send_sem=pair_send.at[0], recv_sem=pair_recv.at[0],
+            device_id=_peer("sa", partner), device_id_type=pl.DeviceIdType.MESH)
+        pair.start()
+        outgoing = []
+        for s in range(1, half):
+            c = pltpu.make_async_remote_copy(
+                src_ref=src, dst_ref=dst.at[me], send_sem=send.at[s], recv_sem=recv.at[s],
+                device_id=_peer("sa", lax.rem(me + 2 * s, n)), device_id_type=pl.DeviceIdType.MESH)
+            c.start()
+            outgoing.append(c)
+        relays = []
+        for s in range(1, half):
+            outgoing[s - 1].wait_recv()
+            slot = lax.rem(me + n - 2 * s, n)
+            r = pltpu.make_async_remote_copy(
+                src_ref=dst.at[slot], dst_ref=dst.at[slot], send_sem=relay_send.at[s],
+                recv_sem=relay_recv.at[s], device_id=_peer("sa", partner),
+                device_id_type=pl.DeviceIdType.MESH)
+            r.start()
+            relays.append(r)
+        for c in outgoing:
+            c.wait_send()
+        for r in relays:
+            r.wait()
+        pair.wait()
+        own.wait()
+
+    anywhere = pl.BlockSpec(memory_space=pl.ANY)
+    return pl.pallas_call(
+        kernel,
+        out_shape=jax.ShapeDtypeStruct((n,) + block.shape, block.dtype),
+        in_specs=[anywhere],
+        out_specs=anywhere,
+        scratch_shapes=[
+            pltpu.SemaphoreType.DMA((half,)),
+            pltpu.SemaphoreType.DMA((half,)),
+            pltpu.SemaphoreType.DMA((half,)),
+            pltpu.SemaphoreType.DMA((half,)),
+            pltpu.SemaphoreType.DMA((1,)),
+            pltpu.SemaphoreType.DMA((1,)),
+            pltpu.SemaphoreType.DMA((1,)),
+        ],
+        compiler_params=pltpu.CompilerParams(collective_id=cid, has_side_effects=True),
+    )(block)
+
+
 HIGH = lax.Precision.HIGHEST
 
 
@@ -161,8 +224,7 @@
     scale = 1.0 / math.sqrt(D)
     q_place = lax.axis_index("sa")
     s_place = lax.axis_index("pb")
-    q_tokens = lax.all_gather(question_states, "sa", axis=1, tiled=True)[0]
-    q_tokens, sql_states = lax.optimization_barrier((q_tokens, sql_states))
+    q_tokens = pair_gather(question_states[0, 0], 5)
     s_tokens = lax.all_gather(sql_states, "pb", axis=1, tiled=True)[0]
     (positive_all,) = exchange([(positive_column.reshape(1, -1), "pb", False)], 0)
     positive_all = positive_all.reshape(-1)

time: 400 us -> 396 us (0.990)
  waiting for transfers between devices: 107 us -> 0.68 us
  Pallas kernels: 166 us -> 266 us
    pallas_call x0 -> x1, Pallas kernels: none -> 81.2 us  [pair_gather(): pl.pallas_call(kernel, out_shape=jax.ShapeDtypeStruct((n,) + block.shape,...]
    all_gather x1, waiting for transfers between devices: 55.2 us -> 0.01 us  [per_device(): s_tokens = lax.all_gather(sql_states, 'pb', axis=1, tiled=True)[0]]
    all_gather x1 -> x0, waiting for transfers between devices: 51.1 us -> none  [per_device(): q_tokens = lax.all_gather(question_states, 'sa', axis=1, tiled=True)[0]]
    pallas_call x5, Pallas kernels: 166 us -> 185 us  [exchange(): pl.pallas_call(kernel, out_shape=out_shape, in_specs=[anywhere] * count,...]
  transfers between devices with their start and end apart: 2 -> 1, of which waited for: 2 -> 0; matrix products, arithmetic and copies ran while one was open for 7% -> 8% of each run, Pallas kernels for 3% -> 24%
where the time goes in v2:
time: 396 us; the launch traced here: 391 us
  Pallas kernels  266 us (67%)
  matrix products  52.9 us (13%)
  other arithmetic  37.3 us (9%)
  between operations  17.2 us (4%)
  local copies, waits for them, and re-layouts  17 us (4%)
    pallas_call x5, Pallas kernels, exchange(): pl.pallas_call(kernel, out_shape=out_shape, in_specs=[anywhere] * count,...  185 us
    pallas_call x1, Pallas kernels, pair_gather(): pl.pallas_call(kernel, out_shape=jax.ShapeDtypeStruct((n,) + block.shape,...  81.2 us
    dot_general x2, matrix products, tower_backward(): lax.dot_general(dpre, rows, (((0,), (0,)), ((), ())), preferred_element_t...  18.2 us
    convert_element_type x2, other arithmetic, tower_backward(): high.astype(jnp.bfloat16)  12.4 us
    unnamed x57, local copies, waits for them, and re-layouts  11.3 us
    dot_general x2, matrix products, tower_forward(): jnp.einsum('nt,ntd->nd', weights, input_float.reshape(count, length, widt...  10.7 us
  transfers between devices with their start and end apart: 1, of which 0 were waited for; matrix products, arithmetic and copies ran while one was open for 8% of the time, Pallas kernels for 24%

profile of v2, /device:TPU:1, one launch (start us, length us, event | category | flops | bytes accessed | tf_op | source)
XLA Modules:
  0.0 391.4 jit_solution(18024782603212547611)
XLA Ops:
  7.9 14.0 %shard_map.165 = s32[16,1,16]{2,1,0:T(1,128)} custom-call(s32[1,16]{1,0:T(1,128)} %bitcast.155), custom_call_target="tpu_custom_call" | custom-call | tf_op jit(solution)/shard_map/pallas_call | solution.py:66
  25.8 81.2 %shard_map.162 = bf16[16,256,768]{2,1,0:T(8,128)(2,1)} custom-call(bf16[256,768]{1,0:T(8,128)(2,1)} %bitcast.142), custom_call_target="tpu_custom_call" | custom-call | tf_op jit(solution)/shard_map/pallas_call | solution.py:125
  106.9 3.8 convert_reduce_fusion
  113.7 6.6 %reduce-precision_convert_fusion.1 = (bf16[4096,768]{1,0:T(8,128)(2,1)}, bf16[4096,768]{1,0:T(8,128)(2,1)}, bf16[4096,768]{1,0:T(8,128)(2,1)S(1)}) fusion(bf16[16,256,768]{2,1,0:T(8,128)(2,1)S(1)} %copy-done.2, f32[4096]{0:T(1024)S(1)} %bitcast.154, f32[4096]{0:T(1024)S(1)} %bitcast.153, f32[768]{0:T(1024)S(1)} %copy-done.16), kind=kLoop, calls=%fused_computation.15 | loop fusion | flops 28311552 | bytes 25201664 | tf_op jit(solution)/shard_map/convert_element_type | solution.py:200
  120.2 3.7 multiply_multiply_fusion.3
  123.9 2.7 fusion.32
  128.1 5.3 %fusion.62 = f32[16,1,768]{2,1,0:T(1,128)S(1)} fusion(bf16[16,256,768]{2,1,0:T(8,128)(2,1)} %shard_map.162, f32[16,256,1]{1,0,2:T(8,128)S(1)} %get-tuple-element.76), kind=kOutput, calls=%fused_computation.100 | convolution fusion | flops 37748736 | bytes 6356992 | tf_op jit(solution)/shard_map/nt,ntd->nd/dot_general | solution.py:182
  133.5 4.2 %multiply_reduce_fusion = f32[16,256]{1,0:T(8,128)S(1)} fusion(bf16[1,16,256,768]{3,2,0,1:T(8,128)(2,1)} %all-gather.2.cloned.1.call-done), kind=kLoop, calls=%fused_computation.22 | loop fusion | flops 9433088 | bytes 6307840 | tf_op jit(solution)/shard_map/reduce_sum | solution.py:149
  138.1 5.8 %reduce-precision_convert_fusion = (bf16[4096,768]{1,0:T(8,128)(2,1)}, bf16[4096,768]{1,0:T(8,128)(2,1)}, bf16[4096,768]{1,0:T(8,128)(2,1)S(1)}) fusion(bf16[1,16,256,768]{3,2,0,1:T(8,128)(2,1)S(1)} %copy-done.3, f32[4096]{0:T(1024)S(1)} %bitcast.146, f32[768]{0:T(1024)S(1)} %copy-done.15), kind=kLoop, calls=%fused_computation.13 | loop fusion | flops 25165824 | bytes 25185280 | tf_op jit(solution)/shard_map/convert_element_type | solution.py:200
  143.9 3.8 multiply_multiply_fusion.2
  147.7 2.7 fusion.29
  151.9 56.0 %shard_map.163 = (f32[16,16,768]{2,1,0:T(8,128)}, f32[16,16,768]{2,1,0:T(8,128)}) custom-call(f32[16,768]{1,0:T(8,128)} %fusion.76.refs_0_, f32[16,768]{1,0:T(8,128)} %fusion.77.refs_1_), custom_call_target="tpu_custom_call" | custom-call | tf_op jit(solution)/shard_map/pallas_call | solution.py:66
  210.4 5.3 %fusion.15 = f32[16,1,768]{2,1,0:T(1,128)S(1)} fusion(bf16[1,16,256,768]{3,2,0,1:T(8,128)(2,1)} %all-gather.2.cloned.1.call-done, f32[16,256,1]{1,0,2:T(8,128)S(1)} %get-tuple-element.74), kind=kOutput, calls=%fused_computation.26 | convolution fusion | flops 37748736 | bytes 6356992 | tf_op jit(solution)/shard_map/nt,ntd->nd/dot_general | solution.py:182
  216.4 41.3 %shard_map.164 = (f32[16,16,768]{2,1,0:T(8,128)}, f32[16,16,192]{2,1,0:T(8,128)}, f32[16,16,768]{2,1,0:T(8,128)}, f32[16,16,192]{2,1,0:T(8,128)}) custom-call(f32[16,768]{1,0:T(8,128)} %get-tuple-element.83.refs_0_, f32[16,192]{1,0:T(8,128)} %bitcast.151, f32[16,768]{1,0:T(8,128)} %get-tuple-element.82.refs_2_, f32[16,192]{1,0:T(8,128)} %bitcast.152), custom_call_target="tpu_custom_call" | custom-call | tf_op jit(solution)/shard_map/pallas_call | solution.py:66
  257.7 2.4 fusion.78
  261.6 2.1 convolution_multiply_fusion.1
  269.2 2.8 copy.48
  272.1 8.5 %fusion = f32[192,2304]{1,0:T(8,128)S(1)} fusion(bf16[4096,768]{1,0:T(8,128)(2,1)} %get-tuple-element.62, bf16[4096,768]{1,0:T(8,128)(2,1)S(1)} %bitcast.131, bf16[4096,768]{1,0:T(8,128)(2,1)S(1)} %bitcast.123, f32[4096,192]{0,1:T(8,128)S(1)} %copy-done.6, f32[4096,192]{0,1:T(8,128)S(1)} %bitcast.132, f32[4096]{0:T(1024)S(1)} %div.72), kind=kOutput, calls=%fused_computation | convolution fusion | flops 3689152512 | bytes 26951680 | tf_op jit(solution)/shard_map/dot_general | solution.py:202
  282.4 2.8 copy.51
  285.2 9.7 %fusion.6 = f32[192,2304]{1,0:T(8,128)S(1)} fusion(bf16[4096,768]{1,0:T(8,128)(2,1)} %get-tuple-element.65, bf16[4096,768]{1,0:T(8,128)(2,1)} %get-tuple-element.64, bf16[4096,768]{1,0:T(8,128)(2,1)S(1)} %bitcast.125, f32[4096,192]{0,1:T(8,128)S(1)} %copy-done.7, f32[4096,192]{0,1:T(8,128)S(1)} %bitcast.133, f32[4096]{0:T(1024)S(1)} %div.75), kind=kOutput, calls=%fused_computation.6 | convolution fusion | flops 3689152512 | bytes 26951680 | tf_op jit(solution)/shard_map/dot_general | solution.py:202
  296.9 37.6 %shard_map.166 = (f32[16,48,192]{2,1,0:T(8,128)}, f32[16,48,192]{2,1,0:T(8,128)}, f32[16,2,768]{2,1,0:T(2,128)}) custom-call(f32[16,48,192]{2,1,0:T(8,128)} %bitcast.138, f32[16,48,192]{2,1,0:T(8,128)} %bitcast.139, f32[2,768]{1,0:T(2,128)} %pad_maximum_fusion.refs_2_), custom_call_target="tpu_custom_call" | custom-call | tf_op jit(solution)/shard_map/pallas_call | solution.py:66
  339.6 36.3 %shard_map.167 = (f32[16,48,192]{2,1,0:T(8,128)}, f32[16,48,192]{2,1,0:T(8,128)}, f32[16,2,768]{2,1,0:T(2,128)}) custom-call(f32[48,192]{1,0:T(8,128)} %reduce_sum.186.refs_0_, f32[48,192]{1,0:T(8,128)} %reduce_sum.187.refs_1_, f32[2,768]{1,0:T(2,128)} %reduce_sum.188.refs_2_), custom_call_target="tpu_custom_call" | custom-call | tf_op jit(solution)/shard_map/pallas_call | solution.py:66
  376.0 2.2 copy.29
  379.7 2.2 copy.30
  (103 shorter events, 31.3 us)
Async XLA Ops:
  7.2 143.9 %copy-start = (bf16[192,768]{1,0:T(8,128)(2,1)S(1)}, bf16[192,768]{1,0:T(8,128)(2,1)}, u32[]{:S(2)}) copy-start(bf16[192,768]{1,0:T(8,128)(2,1)} %param.19) | copy-start | bytes 884740
  7.2 126.3 %all-gather.2.cloned.1.call-start = ((), (), s32[]{:S(2)}) async-start(), calls=%async_computation | async-start | bytes 6684672 | tf_op jit(solution)/shard_map/all_gather | solution.py:228
  106.9 4.7 %copy-start.2 = (bf16[16,256,768]{2,1,0:T(8,128)(2,1)S(1)}, bf16[16,256,768]{2,1,0:T(8,128)(2,1)}, u32[]{:S(2)}) copy-start(bf16[16,256,768]{2,1,0:T(8,128)(2,1)} %shard_map.162) | copy-start | bytes 18874372
  111.7 2.0 copy-start.16
  113.6 6.6 %copy-start.10 = (bf16[768,192]{0,1:T(8,128)(2,1)S(1)}, bf16[768,192]{0,1:T(8,128)(2,1)}, u32[]{:S(2)}) copy-start(bf16[768,192]{0,1:T(8,128)(2,1)} %param.13) | copy-start | bytes 884740
  120.2 3.7 copy-start.4
  123.9 3.3 copy-start.9
  133.5 4.3 %copy-start.15 = (f32[768]{0:T(1024)S(1)}, f32[768]{0:T(1024)}, u32[]{:S(2)}) copy-start(f32[768]{0:T(1024)} %param.20) | copy-start | bytes 9220
  133.5 4.6 %copy-start.3 = (bf16[1,16,256,768]{3,2,0,1:T(8,128)(2,1)S(1)}, bf16[1,16,256,768]{3,2,0,1:T(8,128)(2,1)}, u32[]{:S(2)}) copy-start(bf16[1,16,256,768]{3,2,0,1:T(8,128)(2,1)} %all-gather.2.cloned.1.call-done) | copy-start | bytes 18874372
  138.1 5.8 %copy-start.11 = (bf16[768,192]{0,1:T(8,128)(2,1)S(1)}, bf16[768,192]{0,1:T(8,128)(2,1)}, u32[]{:S(2)}) copy-start(bf16[768,192]{0,1:T(8,128)(2,1)} %param.18) | copy-start | bytes 884740
  143.9 3.8 copy-start.5
  207.9 64.1 %slice-start.4 = ((s8[6291456]{0:T(1024)(128)(4,1)}), s8[2097152]{0:T(1024)(128)(4,1)S(1)}, s32[]{:S(2)}) async-start(s8[6291456]{0:T(1024)(128)(4,1)} %bitcast.130), calls=%async_computation.5 | async-start | bytes 4194304
  257.7 5.9 %copy-start.8 = (f32[16,16,768]{2,1,0:T(8,128)S(1)}, f32[16,16,768]{2,1,0:T(8,128)}, u32[]{:S(2)}) copy-start(f32[16,16,768]{2,1,0:T(8,128)} %get-tuple-element.21) | copy-start | bytes 2359300
  257.7 7.3 %copy-start.14 = (f32[16,16,192]{2,1,0:T(8,128)S(1)}, f32[16,16,192]{2,1,0:T(8,128)}, u32[]{:S(2)}) copy-start(f32[16,16,192]{2,1,0:T(8,128)} %get-tuple-element.30) | copy-start | bytes 589828
  260.3 6.6 %copy-start.13 = (f32[16,16,192]{2,1,0:T(8,128)S(1)}, f32[16,16,192]{2,1,0:T(8,128)}, u32[]{:S(2)}) copy-start(f32[16,16,192]{2,1,0:T(8,128)} %get-tuple-element.27) | copy-start | bytes 589828
  263.6 8.4 %slice-start.5 = ((s8[6291456]{0:T(1024)(128)(4,1)}), s8[4194304]{0:T(1024)(128)(4,1)S(1)}, s32[]{:S(2)}) async-start(s8[6291456]{0:T(1024)(128)(4,1)} %bitcast.130), calls=%async_computation.6 | async-start | bytes 8388608
  265.0 7.0 %slice-start = ((s8[6291456]{0:T(1024)(128)(4,1)}), s8[4194304]{0:T(1024)(128)(4,1)S(1)}, s32[]{:S(2)}) async-start(s8[6291456]{0:T(1024)(128)(4,1)} %bitcast.122), calls=%async_computation.1 | async-start | bytes 8388608
  268.7 3.3 slice-start.1
  269.2 2.8 copy-start.6
  280.6 4.6 %slice-start.2 = ((s8[6291456]{0:T(1024)(128)(4,1)}), s8[2097152]{0:T(1024)(128)(4,1)S(1)}, s32[]{:S(2)}) async-start(s8[6291456]{0:T(1024)(128)(4,1)} %bitcast.124), calls=%async_computation.3 | async-start | bytes 4194304
  281.9 3.3 slice-start.3
  282.4 2.8 copy-start.7
  285.2 9.7 %copy-start.12 = (bf16[768,192]{0,1:T(8,128)(2,1)S(1)}, bf16[768,192]{0,1:T(8,128)(2,1)}, u32[]{:S(2)}) copy-start(bf16[768,192]{0,1:T(8,128)(2,1)} %param.18) | copy-start | bytes 884740
  296.8 86.3 %copy-start.1 = (bf16[192,768]{1,0:T(8,128)(2,1)S(1)}, bf16[192,768]{1,0:T(8,128)(2,1)}, u32[]{:S(2)}) copy-start(bf16[192,768]{1,0:T(8,128)(2,1)} %param.19) | copy-start | bytes 884740
Sparse Core Ops, SparseCore 0:
  10.5 119.9 all-gather.1

commit v3 on v1

--- a/solution.py
+++ b/solution.py
@@ -77,6 +77,82 @@
     )(*arrays)
 
 
+def plane_gather(block, cid):
+    n = lax.axis_size("sa")
+    rows = n // 4
+    mesh_kind = pl.DeviceIdType.MESH
+
+    def kernel(src, dst, ysend, yrecv, fsend, frecv, rsend, rrecv, zsend, zrecv, psend, precv, local):
+        me = lax.axis_index("sa")
+        core = lax.rem(me, 2)
+        row = lax.rem(me // 2, rows)
+        plane = me // (2 * rows)
+        partner = me + 1 - 2 * core
+        across = lax.rem(me + 2 * rows, n)
+
+        def along(d):
+            return plane * 2 * rows + lax.rem(row + d, rows) * 2 + core
+
+        barrier = pltpu.get_barrier_semaphore()
+        for peer in [partner, across] + [along(d) for d in range(1, rows)]:
+            pl.semaphore_signal(barrier, 1, device_id=_peer("sa", peer), device_id_type=mesh_kind)
+        pl.semaphore_wait(barrier, rows + 1)
+
+        def send(source, slot, peer, s, r):
+            c = pltpu.make_async_remote_copy(
+                src_ref=source, dst_ref=dst.at[slot], send_sem=s, recv_sem=r,
+                device_id=_peer("sa", peer), device_id_type=mesh_kind)
+            c.start()
+            return c
+
+        own = pltpu.make_async_copy(src, dst.at[me], local.at[0])
+        own.start()
+        z_copy = send(src, me, across, zsend.at[0], zrecv.at[0])
+        pair = send(src, me, partner, psend.at[0], precv.at[0])
+        direct = [send(src, me, along(d), ysend.at[d], yrecv.at[d]) for d in range(1, rows)]
+        z_copy.wait_recv()
+        far = lax.rem(me + 2 * rows, n)
+        relayed = [send(dst.at[far], far, along(d), fsend.at[d], frecv.at[d]) for d in range(1, rows)]
+        handed = [send(dst.at[far], far, partner, rsend.at[0], rrecv.at[0])]
+        for d in range(1, rows):
+            direct[d - 1].wait_recv()
+            slot = along(rows - d)
+            handed.append(send(dst.at[slot], slot, partner, rsend.at[d], rrecv.at[d]))
+        for d in range(1, rows):
+            relayed[d - 1].wait_recv()
+            slot = lax.rem(along(rows - d) + 2 * rows, n)
+            handed.append(send(dst.at[slot], slot, partner, rsend.at[rows - 1 + d],
+                               rrecv.at[rows - 1 + d]))
+        for c in direct + relayed + [z_copy]:
+            c.wait_send()
+        for c in handed:
+            c.wait()
+        pair.wait()
+        own.wait()
+
+    anywhere = pl.BlockSpec(memory_space=pl.ANY)
+    return pl.pallas_call(
+        kernel,
+        out_shape=jax.ShapeDtypeStruct((n,) + block.shape, block.dtype),
+        in_specs=[anywhere],
+        out_specs=anywhere,
+        scratch_shapes=[
+            pltpu.SemaphoreType.DMA((rows,)),
+            pltpu.SemaphoreType.DMA((rows,)),
+            pltpu.SemaphoreType.DMA((rows,)),
+            pltpu.SemaphoreType.DMA((rows,)),
+            pltpu.SemaphoreType.DMA((2 * rows - 1,)),
+            pltpu.SemaphoreType.DMA((2 * rows - 1,)),
+            pltpu.SemaphoreType.DMA((1,)),
+            pltpu.SemaphoreType.DMA((1,)),
+            pltpu.SemaphoreType.DMA((1,)),
+            pltpu.SemaphoreType.DMA((1,)),
+            pltpu.SemaphoreType.DMA((1,)),
+        ],
+        compiler_params=pltpu.CompilerParams(collective_id=cid, has_side_effects=True),
+    )(block)
+
+
 HIGH = lax.Precision.HIGHEST
 
 
@@ -161,11 +237,8 @@
     scale = 1.0 / math.sqrt(D)
     q_place = lax.axis_index("sa")
     s_place = lax.axis_index("pb")
-    q_tokens = lax.all_gather(question_states, "sa", axis=1, tiled=True)[0]
-    q_tokens, sql_states = lax.optimization_barrier((q_tokens, sql_states))
+    q_tokens = plane_gather(question_states[0, 0], 5)
     s_tokens = lax.all_gather(sql_states, "pb", axis=1, tiled=True)[0]
-    (positive_all,) = exchange([(positive_column.reshape(1, -1), "pb", False)], 0)
-    positive_all = positive_all.reshape(-1)
     q_rows = q_tokens.shape[0]
     s_rows = s_tokens.shape[0]
 
@@ -186,15 +259,17 @@
     )
     q_block = jnp.sum(q_terms, axis=0) + q_resid
     s_block = jnp.sum(s_terms, axis=0) + s_resid
-    q_embed, q_pooled_all, s_embed, s_pooled_all = exchange(
+    q_embed, q_pooled_all, s_embed, s_pooled_all, positive_all = exchange(
         [
             (q_block, "pb", False),
             (q_pooled, "pb", False),
             (s_block, "sa", False),
             (s_pooled, "sa", False),
+            (positive_column.reshape(1, -1), "pb", False),
         ],
         2,
     )
+    positive_all = positive_all.reshape(-1)
     q_embed = q_embed.reshape(-1, D)
     s_embed = s_embed.reshape(-1, D)
     q_pooled_all = q_pooled_all.reshape(-1, q_pooled.shape[-1])

time: 400 us -> 355 us (0.89)
  waiting for transfers between devices: 107 us -> 25.2 us
  Pallas kernels: 166 us -> 200 us
    all_gather x1 -> x0, waiting for transfers between devices: 51.1 us -> none  [per_device(): q_tokens = lax.all_gather(question_states, 'sa', axis=1, tiled=True)[0]]
    pallas_call x0 -> x1, Pallas kernels: none -> 43.7 us  [plane_gather(): pl.pallas_call(kernel, out_shape=jax.ShapeDtypeStruct((n,) + block.shape,...]
    all_gather x1, waiting for transfers between devices: 55.2 us -> 24.6 us  [per_device(): s_tokens = lax.all_gather(sql_states, 'pb', axis=1, tiled=True)[0]]
    pallas_call x5 -> x4, Pallas kernels: 166 us -> 157 us  [exchange(): pl.pallas_call(kernel, out_shape=out_shape, in_specs=[anywhere] * count,...]
    unnamed x57 -> x59, local copies, waits for them, and re-layouts: 11.2 us -> 11.6 us
  transfers between devices with their start and end apart: 2 -> 1, of which waited for: 2 -> 1; matrix products, arithmetic and copies ran while one was open for 7% -> 8% of each run, Pallas kernels for 3% -> 12%
where the time goes in v3:
time: 355 us; the launch traced here: 350 us
  Pallas kernels  200 us (56%)
  matrix products  53 us (15%)
  other arithmetic  37.3 us (11%)
  waiting for transfers between devices  25.2 us (7%)
  local copies, waits for them, and re-layouts  17.3 us (5%)
  between operations  17.2 us (5%)
    pallas_call x4, Pallas kernels, exchange(): pl.pallas_call(kernel, out_shape=out_shape, in_specs=[anywhere] * count,...  157 us
    pallas_call x1, Pallas kernels, plane_gather(): pl.pallas_call(kernel, out_shape=jax.ShapeDtypeStruct((n,) + block.shape,...  43.7 us
    all_gather x1, waiting for transfers between devices, per_device(): s_tokens = lax.all_gather(sql_states, 'pb', axis=1, tiled=True)[0]  24.6 us
    dot_general x2, matrix products, tower_backward(): lax.dot_general(dpre, rows, (((0,), (0,)), ((), ())), preferred_element_t...  18.3 us
    convert_element_type x2, other arithmetic, tower_backward(): high.astype(jnp.bfloat16)  12.3 us
    unnamed x59, local copies, waits for them, and re-layouts  11.6 us
    dot_general x2, matrix products, tower_forward(): jnp.einsum('nt,ntd->nd', weights, input_float.reshape(count, length, widt...  10.8 us
    dot_general x2, matrix products, tower_forward(): pre = jnp.dot(normalized_rows, inner, preferred_element_type=jnp.float32)  7.43 us
  transfers between devices with their start and end apart: 1, of which 1 were waited for; matrix products, arithmetic and copies ran while one was open for 8% of the time, Pallas kernels for 12%

profile of v3, /device:TPU:1, one launch (start us, length us, event | category | flops | bytes accessed | tf_op | source)
XLA Modules:
  0.0 350.3 jit_solution(2071232273416629468)
XLA Ops:
  9.8 43.7 %shard_map.162 = bf16[16,256,768]{2,1,0:T(8,128)(2,1)} custom-call(bf16[256,768]{1,0:T(8,128)(2,1)} %bitcast.142), custom_call_target="tpu_custom_call" | custom-call | tf_op jit(solution)/shard_map/pallas_call | solution.py:134
  53.6 3.9 %convert_reduce_fusion = f32[16,256]{1,0:T(8,128)S(1)} fusion(bf16[16,256,768]{2,1,0:T(8,128)(2,1)} %shard_map.162), kind=kLoop, calls=%fused_computation.25 | loop fusion | flops 6287360 | bytes 6307840 | tf_op jit(solution)/shard_map/reduce_sum | solution.py:165
  60.7 6.5 %reduce-precision_convert_fusion.1 = (bf16[4096,768]{1,0:T(8,128)(2,1)}, bf16[4096,768]{1,0:T(8,128)(2,1)}, bf16[4096,768]{1,0:T(8,128)(2,1)S(1)}) fusion(bf16[16,256,768]{2,1,0:T(8,128)(2,1)S(1)} %copy-done.2, f32[4096]{0:T(1024)S(1)} %bitcast.154, f32[4096]{0:T(1024)S(1)} %bitcast.153, f32[768]{0:T(1024)S(1)} %copy-done.17), kind=kLoop, calls=%fused_computation.15 | loop fusion | flops 28311552 | bytes 25201664 | tf_op jit(solution)/shard_map/convert_element_type | solution.py:213
  67.2 3.7 %multiply_multiply_fusion.3 = (f32[4096,192]{0,1:T(8,128)S(1)}, f32[4096,192]{0,1:T(8,128)}) fusion(bf16[4096,768]{1,0:T(8,128)(2,1)S(1)} %get-tuple-element.65, bf16[768,192]{0,1:T(8,128)(2,1)S(1)} %copy-done.10), kind=kOutput, calls=%fused_computation.51 | convolution fusion | flops 1211105280 | bytes 12877824 | tf_op jit(solution)/shard_map/dot_general | solution.py:191
  70.9 2.7 fusion.32
  75.1 5.5 %fusion.62 = f32[16,1,768]{2,1,0:T(1,128)S(1)} fusion(bf16[16,256,768]{2,1,0:T(8,128)(2,1)} %shard_map.162, f32[16,256,1]{1,0,2:T(8,128)S(1)} %get-tuple-element.78), kind=kOutput, calls=%fused_computation.100 | convolution fusion | flops 37748736 | bytes 6356992 | tf_op jit(solution)/shard_map/nt,ntd->nd/dot_general | solution.py:195
  80.5 24.6 %all-gather.2.cloned.1.call-done = bf16[1,16,256,768]{3,2,0,1:T(8,128)(2,1)} async-done(((bf16[1,1,256,768]{3,2,0,1:T(8,128)(2,1)}), bf16[1,16,256,768]{3,2,0,1:T(8,128)(2,1)}) %all-gather.2.cloned.1.call-update) | async-done | bytes 6291472 | tf_op jit(solution)/shard_map/all_gather | solution.py:241
  105.1 4.2 %multiply_reduce_fusion = f32[16,256]{1,0:T(8,128)S(1)} fusion(bf16[1,16,256,768]{3,2,0,1:T(8,128)(2,1)} %all-gather.2.cloned.1.call-done), kind=kLoop, calls=%fused_computation.22 | loop fusion | flops 9433088 | bytes 6307840 | tf_op jit(solution)/shard_map/reduce_sum | solution.py:162
  109.7 5.8 %reduce-precision_convert_fusion = (bf16[4096,768]{1,0:T(8,128)(2,1)}, bf16[4096,768]{1,0:T(8,128)(2,1)}, bf16[4096,768]{1,0:T(8,128)(2,1)S(1)}) fusion(bf16[1,16,256,768]{3,2,0,1:T(8,128)(2,1)S(1)} %copy-done.3, f32[4096]{0:T(1024)S(1)} %bitcast.146, f32[768]{0:T(1024)S(1)} %copy-done.16), kind=kLoop, calls=%fused_computation.13 | loop fusion | flops 25165824 | bytes 25185280 | tf_op jit(solution)/shard_map/convert_element_type | solution.py:213
  115.5 3.8 %multiply_multiply_fusion.2 = (f32[4096,192]{0,1:T(8,128)S(1)}, f32[4096,192]{0,1:T(8,128)}) fusion(bf16[4096,768]{1,0:T(8,128)(2,1)S(1)} %get-tuple-element.68, bf16[768,192]{0,1:T(8,128)(2,1)S(1)} %copy-done.12), kind=kOutput, calls=%fused_computation.49 | convolution fusion | flops 1211105280 | bytes 12877824 | tf_op jit(solution)/shard_map/dot_general | solution.py:191
  119.3 2.7 fusion.29
  123.5 41.1 %shard_map.163 = (f32[16,16,768]{2,1,0:T(8,128)}, f32[16,16,768]{2,1,0:T(8,128)}) custom-call(f32[16,768]{1,0:T(8,128)} %fusion.76.refs_0_, f32[16,768]{1,0:T(8,128)} %fusion.77.refs_1_), custom_call_target="tpu_custom_call" | custom-call | tf_op jit(solution)/shard_map/pallas_call | solution.py:66
  167.1 5.3 %fusion.15 = f32[16,1,768]{2,1,0:T(1,128)S(1)} fusion(bf16[1,16,256,768]{3,2,0,1:T(8,128)(2,1)} %all-gather.2.cloned.1.call-done, f32[16,256,1]{1,0,2:T(8,128)S(1)} %get-tuple-element.76), kind=kOutput, calls=%fused_computation.26 | convolution fusion | flops 37748736 | bytes 6356992 | tf_op jit(solution)/shard_map/nt,ntd->nd/dot_general | solution.py:195
  173.1 43.6 %shard_map.164 = (f32[16,16,768]{2,1,0:T(8,128)}, f32[16,16,192]{2,1,0:T(8,128)}, f32[16,16,768]{2,1,0:T(8,128)}, f32[16,16,192]{2,1,0:T(8,128)}, s32[16,1,16]{2,1,0:T(1,128)}) custom-call(f32[16,768]{1,0:T(8,128)} %get-tuple-element.85.refs_0_, f32[16,192]{1,0:T(8,128)} %bitcast.151, f32[16,768]{1,0:T(8,128)} %get-tuple-element.84.refs_2_, ...), custom_call_target="tpu_custom_call" | custom-call | tf_op jit(solution)/shard_map/pallas_call | solution.py:66
  218.7 2.3 fusion.78
  222.5 2.1 convolution_multiply_fusion.1
  230.2 2.8 copy.48
  233.0 8.6 %fusion = f32[192,2304]{1,0:T(8,128)S(1)} fusion(bf16[4096,768]{1,0:T(8,128)(2,1)} %get-tuple-element.64, bf16[4096,768]{1,0:T(8,128)(2,1)S(1)} %bitcast.131, bf16[4096,768]{1,0:T(8,128)(2,1)S(1)} %bitcast.123, f32[4096,192]{0,1:T(8,128)S(1)} %copy-done.6, f32[4096,192]{0,1:T(8,128)S(1)} %bitcast.132, f32[4096]{0:T(1024)S(1)} %div.72), kind=kOutput, calls=%fused_computation | convolution fusion | flops 3689152512 | bytes 26951680 | tf_op jit(solution)/shard_map/dot_general | solution.py:215
  243.4 2.8 copy.51
  246.3 9.7 %fusion.6 = f32[192,2304]{1,0:T(8,128)S(1)} fusion(bf16[4096,768]{1,0:T(8,128)(2,1)} %get-tuple-element.67, bf16[4096,768]{1,0:T(8,128)(2,1)} %get-tuple-element.66, bf16[4096,768]{1,0:T(8,128)(2,1)S(1)} %bitcast.125, f32[4096,192]{0,1:T(8,128)S(1)} %copy-done.7, f32[4096,192]{0,1:T(8,128)S(1)} %bitcast.133, f32[4096]{0:T(1024)S(1)} %div.75), kind=kOutput, calls=%fused_computation.6 | convolution fusion | flops 3689152512 | bytes 26951680 | tf_op jit(solution)/shard_map/dot_general | solution.py:215
  257.9 36.1 %shard_map.165 = (f32[16,48,192]{2,1,0:T(8,128)}, f32[16,48,192]{2,1,0:T(8,128)}, f32[16,2,768]{2,1,0:T(2,128)}) custom-call(f32[16,48,192]{2,1,0:T(8,128)} %bitcast.138, f32[16,48,192]{2,1,0:T(8,128)} %bitcast.139, f32[2,768]{1,0:T(2,128)} %pad_maximum_fusion.refs_2_), custom_call_target="tpu_custom_call" | custom-call | tf_op jit(solution)/shard_map/pallas_call | solution.py:66
  299.1 35.8 %shard_map.166 = (f32[16,48,192]{2,1,0:T(8,128)}, f32[16,48,192]{2,1,0:T(8,128)}, f32[16,2,768]{2,1,0:T(2,128)}) custom-call(f32[48,192]{1,0:T(8,128)} %reduce_sum.186.refs_0_, f32[48,192]{1,0:T(8,128)} %reduce_sum.187.refs_1_, f32[2,768]{1,0:T(2,128)} %reduce_sum.188.refs_2_), custom_call_target="tpu_custom_call" | custom-call | tf_op jit(solution)/shard_map/pallas_call | solution.py:66
  334.9 2.2 copy.29
  338.7 2.2 copy.30
  (104 shorter events, 31.6 us)
Async XLA Ops:
  7.2 115.5 %copy-start = (bf16[192,768]{1,0:T(8,128)(2,1)S(1)}, bf16[192,768]{1,0:T(8,128)(2,1)}, u32[]{:S(2)}) copy-start(bf16[192,768]{1,0:T(8,128)(2,1)} %param.19) | copy-start | bytes 884740
  7.2 97.9 %all-gather.2.cloned.1.call-start = ((), (), s32[]{:S(2)}) async-start(), calls=%async_computation | async-start | bytes 6684672 | tf_op jit(solution)/shard_map/all_gather | solution.py:241
  53.6 5.1 %copy-start.2 = (bf16[16,256,768]{2,1,0:T(8,128)(2,1)S(1)}, bf16[16,256,768]{2,1,0:T(8,128)(2,1)}, u32[]{:S(2)}) copy-start(bf16[16,256,768]{2,1,0:T(8,128)(2,1)} %shard_map.162) | copy-start | bytes 18874372
  60.7 6.5 %copy-start.10 = (bf16[768,192]{0,1:T(8,128)(2,1)S(1)}, bf16[768,192]{0,1:T(8,128)(2,1)}, u32[]{:S(2)}) copy-start(bf16[768,192]{0,1:T(8,128)(2,1)} %param.13) | copy-start | bytes 884740
  67.2 3.7 %copy-start.4 = (bf16[4096,768]{1,0:T(8,128)(2,1)}, bf16[4096,768]{1,0:T(8,128)(2,1)S(1)}, u32[]{:S(2)}) copy-start(bf16[4096,768]{1,0:T(8,128)(2,1)S(1)} %get-tuple-element.65) | copy-start | bytes 18874372
  70.9 3.3 copy-start.9
  80.5 28.8 %copy-start.16 = (f32[768]{0:T(1024)S(1)}, f32[768]{0:T(1024)}, u32[]{:S(2)}) copy-start(f32[768]{0:T(1024)} %param.20) | copy-start | bytes 9220
  105.1 4.6 %copy-start.3 = (bf16[1,16,256,768]{3,2,0,1:T(8,128)(2,1)S(1)}, bf16[1,16,256,768]{3,2,0,1:T(8,128)(2,1)}, u32[]{:S(2)}) copy-start(bf16[1,16,256,768]{3,2,0,1:T(8,128)(2,1)} %all-gather.2.cloned.1.call-done) | copy-start | bytes 18874372
  109.7 5.8 %copy-start.12 = (bf16[768,192]{0,1:T(8,128)(2,1)S(1)}, bf16[768,192]{0,1:T(8,128)(2,1)}, u32[]{:S(2)}) copy-start(bf16[768,192]{0,1:T(8,128)(2,1)} %param.18) | copy-start | bytes 884740
  115.5 3.8 %copy-start.5 = (bf16[4096,768]{1,0:T(8,128)(2,1)}, bf16[4096,768]{1,0:T(8,128)(2,1)S(1)}, u32[]{:S(2)}) copy-start(bf16[4096,768]{1,0:T(8,128)(2,1)S(1)} %get-tuple-element.68) | copy-start | bytes 18874372
  164.6 68.4 %slice-start.4 = ((s8[6291456]{0:T(1024)(128)(4,1)}), s8[2097152]{0:T(1024)(128)(4,1)S(1)}, s32[]{:S(2)}) async-start(s8[6291456]{0:T(1024)(128)(4,1)} %bitcast.130), calls=%async_computation.5 | async-start | bytes 4194304
  216.7 7.9 %copy-start.8 = (f32[16,16,768]{2,1,0:T(8,128)S(1)}, f32[16,16,768]{2,1,0:T(8,128)}, u32[]{:S(2)}) copy-start(f32[16,16,768]{2,1,0:T(8,128)} %get-tuple-element.22) | copy-start | bytes 2359300
  218.7 7.3 %copy-start.15 = (f32[16,16,192]{2,1,0:T(8,128)S(1)}, f32[16,16,192]{2,1,0:T(8,128)}, u32[]{:S(2)}) copy-start(f32[16,16,192]{2,1,0:T(8,128)} %get-tuple-element.32) | copy-start | bytes 589828
  221.3 6.6 %copy-start.14 = (f32[16,16,192]{2,1,0:T(8,128)S(1)}, f32[16,16,192]{2,1,0:T(8,128)}, u32[]{:S(2)}) copy-start(f32[16,16,192]{2,1,0:T(8,128)} %get-tuple-element.29) | copy-start | bytes 589828
  224.6 8.4 %slice-start.5 = ((s8[6291456]{0:T(1024)(128)(4,1)}), s8[4194304]{0:T(1024)(128)(4,1)S(1)}, s32[]{:S(2)}) async-start(s8[6291456]{0:T(1024)(128)(4,1)} %bitcast.130), calls=%async_computation.6 | async-start | bytes 8388608
  226.0 7.0 %slice-start = ((s8[6291456]{0:T(1024)(128)(4,1)}), s8[4194304]{0:T(1024)(128)(4,1)S(1)}, s32[]{:S(2)}) async-start(s8[6291456]{0:T(1024)(128)(4,1)} %bitcast.122), calls=%async_computation.1 | async-start | bytes 8388608
  229.7 3.3 slice-start.1
  230.2 2.8 copy-start.6
  233.0 8.6 %copy-start.11 = (bf16[768,192]{0,1:T(8,128)(2,1)S(1)}, bf16[768,192]{0,1:T(8,128)(2,1)}, u32[]{:S(2)}) copy-start(bf16[768,192]{0,1:T(8,128)(2,1)} %param.13) | copy-start | bytes 884740
  241.6 4.6 %slice-start.2 = ((s8[6291456]{0:T(1024)(128)(4,1)}), s8[2097152]{0:T(1024)(128)(4,1)S(1)}, s32[]{:S(2)}) async-start(s8[6291456]{0:T(1024)(128)(4,1)} %bitcast.124), calls=%async_computation.3 | async-start | bytes 4194304
  242.9 3.3 slice-start.3
  243.4 2.8 copy-start.7
  246.3 9.7 %copy-start.13 = (bf16[768,192]{0,1:T(8,128)(2,1)S(1)}, bf16[768,192]{0,1:T(8,128)(2,1)}, u32[]{:S(2)}) copy-start(bf16[768,192]{0,1:T(8,128)(2,1)} %param.18) | copy-start | bytes 884740
  257.9 84.2 %copy-start.1 = (bf16[192,768]{1,0:T(8,128)(2,1)S(1)}, bf16[192,768]{1,0:T(8,128)(2,1)}, u32[]{:S(2)}) copy-start(bf16[192,768]{1,0:T(8,128)(2,1)} %param.19) | copy-start | bytes 884740
  (1 other events, 2.0 us)
Sparse Core Ops, SparseCore 0:
  10.5 94.5 all-gather.1

commit v4 on v3

--- a/solution.py
+++ b/solution.py
@@ -312,18 +312,25 @@
     s_pieces = s_inner_part.reshape(lax.axis_size("sa"), -1, s_inner_part.shape[-1])
     gains = jnp.stack([q_gain_part, s_gain_part])
     q_pieces, s_pieces, gains = exchange(
-        [(q_pieces, "pb", True), (s_pieces, "sa", True), (gains, "sa", False)], 3
-    )
+        [
+            (q_pieces.astype(jnp.bfloat16), "pb", True),
+            (s_pieces.astype(jnp.bfloat16), "sa", True),
+            (gains, "sa", False),
+        ],
+        3,
+    )
+    q_sums = jnp.sum(q_pieces.astype(jnp.float32), axis=0)
+    s_sums = jnp.sum(s_pieces.astype(jnp.float32), axis=0)
     q_inner_grad, s_inner_grad, gains = exchange(
         [
-            (jnp.sum(q_pieces, axis=0), "pb", False),
-            (jnp.sum(s_pieces, axis=0), "sa", False),
+            (q_sums.astype(jnp.bfloat16), "pb", False),
+            (s_sums.astype(jnp.bfloat16), "sa", False),
             (jnp.sum(gains, axis=0), "pb", False),
         ],
         4,
     )
-    q_inner_grad = q_inner_grad.reshape(q_inner_part.shape)
-    s_inner_grad = s_inner_grad.reshape(s_inner_part.shape)
+    q_inner_grad = q_inner_grad.astype(jnp.float32).reshape(q_inner_part.shape)
+    s_inner_grad = s_inner_grad.astype(jnp.float32).reshape(s_inner_part.shape)
     gains = jnp.sum(gains, axis=0)
     q_gain_grad, s_gain_grad = gains[0], gains[1]
     return (loss, q_inner_grad, q_outer_grad, q_gain_grad, s_inner_grad, s_outer_grad, s_gain_grad)

time: 355 us -> 335 us (0.944)
  Pallas kernels: 200 us -> 174 us
    pallas_call x4, Pallas kernels: 157 us -> 131 us  [exchange(): pl.pallas_call(kernel, out_shape=out_shape, in_specs=[anywhere] * count,...]
    unnamed x59 -> x63, local copies, waits for them, and re-layouts: 11.6 us -> 11.1 us
  transfers between devices with their start and end apart: 1 -> 1, of which waited for: 1 -> 1; matrix products, arithmetic and copies ran while one was open for 8% -> 8% of each run, Pallas kernels for 12% -> 13%
where the time goes in v4:
time: 335 us; the launch traced here: 330 us
  Pallas kernels  174 us (52%)
  matrix products  55.3 us (17%)
  other arithmetic  40 us (12%)
  waiting for transfers between devices  25.4 us (8%)
  local copies, waits for them, and re-layouts  17.5 us (5%)
  between operations  17.1 us (5%)
    pallas_call x4, Pallas kernels, exchange(): pl.pallas_call(kernel, out_shape=out_shape, in_specs=[anywhere] * count,...  131 us
    pallas_call x1, Pallas kernels, plane_gather(): pl.pallas_call(kernel, out_shape=jax.ShapeDtypeStruct((n,) + block.shape,...  43.7 us
    all_gather x1, waiting for transfers between devices, per_device(): s_tokens = lax.all_gather(sql_states, 'pb', axis=1, tiled=True)[0]  24.7 us
    dot_general x2, matrix products, tower_backward(): lax.dot_general(dpre, rows, (((0,), (0,)), ((), ())), preferred_element_t...  18.5 us
    convert_element_type x2, other arithmetic, tower_backward(): high.astype(jnp.bfloat16)  12.2 us
    unnamed x63, local copies, waits for them, and re-layouts  11.1 us
    dot_general x2, matrix products, tower_forward(): jnp.einsum('nt,ntd->nd', weights, input_float.reshape(count, length, widt...  10.8 us
    dot_general x2, matrix products, tower_forward(): pre = jnp.dot(normalized_rows, inner, preferred_element_type=jnp.float32)  7.78 us
  transfers between devices with their start and end apart: 1, of which 1 were waited for; matrix products, arithmetic and copies ran while one was open for 8% of the time, Pallas kernels for 13%

profile of v4, /device:TPU:1, one launch (start us, length us, event | category | flops | bytes accessed | tf_op | source)
XLA Modules:
  0.0 329.8 jit_solution(1258850966918949505)
XLA Ops:
  9.8 43.7 %shard_map.162 = bf16[16,256,768]{2,1,0:T(8,128)(2,1)} custom-call(bf16[256,768]{1,0:T(8,128)(2,1)} %bitcast.146), custom_call_target="tpu_custom_call" | custom-call | tf_op jit(solution)/shard_map/pallas_call | solution.py:134
  53.6 3.9 %convert_reduce_fusion = f32[16,256]{1,0:T(8,128)S(1)} fusion(bf16[16,256,768]{2,1,0:T(8,128)(2,1)} %shard_map.162), kind=kLoop, calls=%fused_computation.25 | loop fusion | flops 6287360 | bytes 6307840 | tf_op jit(solution)/shard_map/reduce_sum | solution.py:165
  58.7 1.9 multiply_reduce_fusion.1
  60.7 6.3 %reduce-precision_convert_fusion.1 = (bf16[4096,768]{1,0:T(8,128)(2,1)}, bf16[4096,768]{1,0:T(8,128)(2,1)}, bf16[4096,768]{1,0:T(8,128)(2,1)S(1)}) fusion(bf16[16,256,768]{2,1,0:T(8,128)(2,1)S(1)} %copy-done.2, f32[4096]{0:T(1024)S(1)} %bitcast.158, f32[4096]{0:T(1024)S(1)} %bitcast.157, f32[768]{0:T(1024)S(1)} %copy-done.17), kind=kLoop, calls=%fused_computation.15 | loop fusion | flops 28311552 | bytes 25201664 | tf_op jit(solution)/shard_map/convert_element_type | solution.py:213
  67.0 3.7 %multiply_multiply_fusion.3 = (f32[4096,192]{0,1:T(8,128)S(1)}, f32[4096,192]{0,1:T(8,128)}) fusion(bf16[4096,768]{1,0:T(8,128)(2,1)S(1)} %get-tuple-element.65, bf16[768,192]{0,1:T(8,128)(2,1)S(1)} %copy-done.10), kind=kOutput, calls=%fused_computation.51 | convolution fusion | flops 1211105280 | bytes 12877824 | tf_op jit(solution)/shard_map/dot_general | solution.py:191
  70.7 2.7 fusion.32
  74.9 5.5 %fusion.64 = f32[16,1,768]{2,1,0:T(1,128)S(1)} fusion(bf16[16,256,768]{2,1,0:T(8,128)(2,1)} %shard_map.162, f32[16,256,1]{1,0,2:T(8,128)S(1)} %get-tuple-element.74), kind=kOutput, calls=%fused_computation.104 | convolution fusion | flops 37748736 | bytes 6356992 | tf_op jit(solution)/shard_map/nt,ntd->nd/dot_general | solution.py:195
  80.4 24.7 %all-gather.2.cloned.1.call-done = bf16[1,16,256,768]{3,2,0,1:T(8,128)(2,1)} async-done(((bf16[1,1,256,768]{3,2,0,1:T(8,128)(2,1)}), bf16[1,16,256,768]{3,2,0,1:T(8,128)(2,1)}) %all-gather.2.cloned.1.call-update) | async-done | bytes 6291472 | tf_op jit(solution)/shard_map/all_gather | solution.py:241
  105.1 4.2 %multiply_reduce_fusion = f32[16,256]{1,0:T(8,128)S(1)} fusion(bf16[1,16,256,768]{3,2,0,1:T(8,128)(2,1)} %all-gather.2.cloned.1.call-done), kind=kLoop, calls=%fused_computation.22 | loop fusion | flops 9433088 | bytes 6307840 | tf_op jit(solution)/shard_map/reduce_sum | solution.py:162
  109.7 5.9 %reduce-precision_convert_fusion = (bf16[4096,768]{1,0:T(8,128)(2,1)}, bf16[4096,768]{1,0:T(8,128)(2,1)}, bf16[4096,768]{1,0:T(8,128)(2,1)S(1)}) fusion(bf16[1,16,256,768]{3,2,0,1:T(8,128)(2,1)S(1)} %copy-done.3, f32[4096]{0:T(1024)S(1)} %bitcast.150, f32[768]{0:T(1024)S(1)} %copy-done.16), kind=kLoop, calls=%fused_computation.13 | loop fusion | flops 25165824 | bytes 25185280 | tf_op jit(solution)/shard_map/convert_element_type | solution.py:213
  115.6 4.1 %multiply_multiply_fusion.2 = (f32[4096,192]{0,1:T(8,128)S(1)}, f32[4096,192]{0,1:T(8,128)}) fusion(bf16[4096,768]{1,0:T(8,128)(2,1)S(1)} %get-tuple-element.68, bf16[768,192]{0,1:T(8,128)(2,1)S(1)} %copy-done.12), kind=kOutput, calls=%fused_computation.49 | convolution fusion | flops 1211105280 | bytes 12877824 | tf_op jit(solution)/shard_map/dot_general | solution.py:191
  119.7 2.7 fusion.29
  123.9 41.1 %shard_map.163 = (f32[16,16,768]{2,1,0:T(8,128)}, f32[16,16,768]{2,1,0:T(8,128)}) custom-call(f32[16,768]{1,0:T(8,128)} %fusion.78.refs_0_, f32[16,768]{1,0:T(8,128)} %fusion.79.refs_1_), custom_call_target="tpu_custom_call" | custom-call | tf_op jit(solution)/shard_map/pallas_call | solution.py:66
  167.4 5.3 %fusion.15 = f32[16,1,768]{2,1,0:T(1,128)S(1)} fusion(bf16[1,16,256,768]{3,2,0,1:T(8,128)(2,1)} %all-gather.2.cloned.1.call-done, f32[16,256,1]{1,0,2:T(8,128)S(1)} %get-tuple-element.72), kind=kOutput, calls=%fused_computation.26 | convolution fusion | flops 37748736 | bytes 6356992 | tf_op jit(solution)/shard_map/nt,ntd->nd/dot_general | solution.py:195
  173.3 43.6 %shard_map.164 = (f32[16,16,768]{2,1,0:T(8,128)}, f32[16,16,192]{2,1,0:T(8,128)}, f32[16,16,768]{2,1,0:T(8,128)}, f32[16,16,192]{2,1,0:T(8,128)}, s32[16,1,16]{2,1,0:T(1,128)}) custom-call(f32[16,768]{1,0:T(8,128)} %get-tuple-element.81.refs_0_, f32[16,192]{1,0:T(8,128)} %bitcast.155, f32[16,768]{1,0:T(8,128)} %get-tuple-element.80.refs_2_, ...), custom_call_target="tpu_custom_call" | custom-call | tf_op jit(solution)/shard_map/pallas_call | solution.py:66
  218.9 2.4 fusion.80
  222.9 2.2 convolution_multiply_fusion.1
  225.1 1.9 convolution_multiply_fusion
  227.8 4.6 %copy.48 = f32[24,8,16,256]{3,1,2,0:T(8,128)} copy(f32[24,8,16,256]{3,2,1,0:T(8,128)S(1)} %bitcast.132) | data formatting | bytes 6291456
  232.5 9.7 %fusion = f32[192,2304]{1,0:T(8,128)} fusion(bf16[4096,768]{1,0:T(8,128)(2,1)} %get-tuple-element.64, bf16[4096,768]{1,0:T(8,128)(2,1)S(1)} %bitcast.135, bf16[4096,768]{1,0:T(8,128)(2,1)S(1)} %bitcast.127, f32[4096,192]{0,1:T(8,128)} %get-tuple-element.76, f32[4096,192]{0,1:T(8,128)} %bitcast.138, f32[4096]{0:T(1024)S(1)} %div.72), kind=kOutput, calls=%fused_computation | convolution fusion | flops 3689152512 | bytes 26951680 | tf_op jit(solution)/shard_map/dot_general | solution.py:215
  246.2 2.8 copy.51
  249.1 8.9 %fusion.6 = f32[192,2304]{1,0:T(8,128)S(1)} fusion(bf16[4096,768]{1,0:T(8,128)(2,1)} %get-tuple-element.67, bf16[4096,768]{1,0:T(8,128)(2,1)S(1)} %bitcast.137, bf16[4096,768]{1,0:T(8,128)(2,1)S(1)} %bitcast.129, f32[4096,192]{0,1:T(8,128)S(1)} %copy-done.6, f32[4096,192]{0,1:T(8,128)S(1)} %bitcast.139, f32[4096]{0:T(1024)S(1)} %div.75), kind=kOutput, calls=%fused_computation.6 | convolution fusion | flops 3689152512 | bytes 26951680 | tf_op jit(solution)/shard_map/dot_general | solution.py:215
  263.7 23.2 %shard_map.165 = (bf16[16,48,192]{2,1,0:T(8,128)(2,1)}, bf16[16,48,192]{2,1,0:T(8,128)(2,1)}, f32[16,2,768]{2,1,0:T(2,128)}) custom-call(bf16[16,48,192]{2,1,0:T(8,128)(2,1)} %bitcast.144, bf16[16,48,192]{2,1,0:T(8,128)(2,1)} %bitcast.145, f32[2,768]{1,0:T(2,128)} %pad_maximum_fusion.refs_2_), custom_call_target="tpu_custom_call" | custom-call | tf_op jit(solution)/shard_map/pallas_call | solution.py:66
  291.8 22.8 %shard_map.166 = (bf16[16,48,192]{2,1,0:T(8,128)(2,1)}, bf16[16,48,192]{2,1,0:T(8,128)(2,1)}, f32[16,2,768]{2,1,0:T(2,128)}) custom-call(bf16[48,192]{1,0:T(8,128)(2,1)} %reduce_sum.192.refs_0_, bf16[48,192]{1,0:T(8,128)(2,1)} %reduce_sum.193.refs_1_, f32[2,768]{1,0:T(2,128)} %reduce_sum.194.refs_2_), custom_call_target="tpu_custom_call" | custom-call | tf_op jit(solution)/shard_map/pallas_call | solution.py:66
  (113 shorter events, 34.9 us)
Async XLA Ops:
  7.2 66.9 %copy-start = (bf16[192,768]{1,0:T(8,128)(2,1)S(1)}, bf16[192,768]{1,0:T(8,128)(2,1)}, u32[]{:S(2)}) copy-start(bf16[192,768]{1,0:T(8,128)(2,1)} %param.14) | copy-start | bytes 884740
  7.2 97.9 %all-gather.2.cloned.1.call-start = ((), (), s32[]{:S(2)}) async-start(), calls=%async_computation | async-start | bytes 6684672 | tf_op jit(solution)/shard_map/all_gather | solution.py:241
  53.6 5.1 %copy-start.2 = (bf16[16,256,768]{2,1,0:T(8,128)(2,1)S(1)}, bf16[16,256,768]{2,1,0:T(8,128)(2,1)}, u32[]{:S(2)}) copy-start(bf16[16,256,768]{2,1,0:T(8,128)(2,1)} %shard_map.162) | copy-start | bytes 18874372
  60.7 6.4 %copy-start.10 = (bf16[768,192]{0,1:T(8,128)(2,1)S(1)}, bf16[768,192]{0,1:T(8,128)(2,1)}, u32[]{:S(2)}) copy-start(bf16[768,192]{0,1:T(8,128)(2,1)} %param.13) | copy-start | bytes 884740
  67.0 3.7 %copy-start.4 = (bf16[4096,768]{1,0:T(8,128)(2,1)}, bf16[4096,768]{1,0:T(8,128)(2,1)S(1)}, u32[]{:S(2)}) copy-start(bf16[4096,768]{1,0:T(8,128)(2,1)S(1)} %get-tuple-element.65) | copy-start | bytes 18874372
  80.4 29.0 %copy-start.16 = (f32[768]{0:T(1024)S(1)}, f32[768]{0:T(1024)}, u32[]{:S(2)}) copy-start(f32[768]{0:T(1024)} %param.20) | copy-start | bytes 9220
  105.1 4.6 %copy-start.3 = (bf16[1,16,256,768]{3,2,0,1:T(8,128)(2,1)S(1)}, bf16[1,16,256,768]{3,2,0,1:T(8,128)(2,1)}, u32[]{:S(2)}) copy-start(bf16[1,16,256,768]{3,2,0,1:T(8,128)(2,1)} %all-gather.2.cloned.1.call-done) | copy-start | bytes 18874372
  109.7 5.9 %copy-start.12 = (bf16[768,192]{0,1:T(8,128)(2,1)S(1)}, bf16[768,192]{0,1:T(8,128)(2,1)}, u32[]{:S(2)}) copy-start(bf16[768,192]{0,1:T(8,128)(2,1)} %param.18) | copy-start | bytes 884740
  115.6 4.1 %copy-start.5 = (bf16[4096,768]{1,0:T(8,128)(2,1)}, bf16[4096,768]{1,0:T(8,128)(2,1)S(1)}, u32[]{:S(2)}) copy-start(bf16[4096,768]{1,0:T(8,128)(2,1)S(1)} %get-tuple-element.68) | copy-start | bytes 18874372
  119.7 3.3 %copy-start.9 = (bf16[192,768]{1,0:T(8,128)(2,1)S(1)}, bf16[192,768]{1,0:T(8,128)(2,1)}, u32[]{:S(2)}) copy-start(bf16[192,768]{1,0:T(8,128)(2,1)} %param.19) | copy-start | bytes 884740
  119.7 112.7 %slice-start.4 = ((s8[6291456]{0:T(1024)(128)(4,1)}), s8[2097152]{0:T(1024)(128)(4,1)S(1)}, s32[]{:S(2)}) async-start(s8[6291456]{0:T(1024)(128)(4,1)} %bitcast.134), calls=%async_computation.5 | async-start | bytes 4194304
  218.9 6.1 %copy-start.8 = (f32[16,16,768]{2,1,0:T(8,128)S(1)}, f32[16,16,768]{2,1,0:T(8,128)}, u32[]{:S(2)}) copy-start(f32[16,16,768]{2,1,0:T(8,128)} %get-tuple-element.22) | copy-start | bytes 2359300
  218.9 13.5 %slice-start.5 = ((s8[6291456]{0:T(1024)(128)(4,1)}), s8[4194304]{0:T(1024)(128)(4,1)S(1)}, s32[]{:S(2)}) async-start(s8[6291456]{0:T(1024)(128)(4,1)} %bitcast.134), calls=%async_computation.6 | async-start | bytes 8388608
  222.9 9.6 %slice-start = ((s8[6291456]{0:T(1024)(128)(4,1)}), s8[4194304]{0:T(1024)(128)(4,1)S(1)}, s32[]{:S(2)}) async-start(s8[6291456]{0:T(1024)(128)(4,1)} %bitcast.126), calls=%async_computation.1 | async-start | bytes 8388608
  227.3 5.1 %slice-start.1 = ((s8[6291456]{0:T(1024)(128)(4,1)}), s8[2097152]{0:T(1024)(128)(4,1)S(1)}, s32[]{:S(2)}) async-start(s8[6291456]{0:T(1024)(128)(4,1)} %bitcast.126), calls=%async_computation.2 | async-start | bytes 4194304
  227.8 21.2 %slice-start.2 = ((s8[6291456]{0:T(1024)(128)(4,1)}), s8[4194304]{0:T(1024)(128)(4,1)S(1)}, s32[]{:S(2)}) async-start(s8[6291456]{0:T(1024)(128)(4,1)} %bitcast.128), calls=%async_computation.3 | async-start | bytes 8388608
  227.8 21.2 %slice-start.6 = ((s8[6291456]{0:T(1024)(128)(4,1)}), s8[2097152]{0:T(1024)(128)(4,1)S(1)}, s32[]{:S(2)}) async-start(s8[6291456]{0:T(1024)(128)(4,1)} %bitcast.136), calls=%async_computation.7 | async-start | bytes 4194304
  232.4 9.7 %copy-start.11 = (bf16[768,192]{0,1:T(8,128)(2,1)S(1)}, bf16[768,192]{0,1:T(8,128)(2,1)}, u32[]{:S(2)}) copy-start(bf16[768,192]{0,1:T(8,128)(2,1)} %param.13) | copy-start | bytes 884740
  232.5 16.6 %slice-start.3 = ((s8[6291456]{0:T(1024)(128)(4,1)}), s8[2097152]{0:T(1024)(128)(4,1)S(1)}, s32[]{:S(2)}) async-start(s8[6291456]{0:T(1024)(128)(4,1)} %bitcast.128), calls=%async_computation.4 | async-start | bytes 4194304
  232.5 16.6 %slice-start.7 = ((s8[6291456]{0:T(1024)(128)(4,1)}), s8[4194304]{0:T(1024)(128)(4,1)S(1)}, s32[]{:S(2)}) async-start(s8[6291456]{0:T(1024)(128)(4,1)} %bitcast.136), calls=%async_computation.8 | async-start | bytes 8388608
  249.1 8.9 %copy-start.13 = (bf16[768,192]{0,1:T(8,128)(2,1)S(1)}, bf16[768,192]{0,1:T(8,128)(2,1)}, u32[]{:S(2)}) copy-start(bf16[768,192]{0,1:T(8,128)(2,1)} %param.18) | copy-start | bytes 884740
  249.1 9.0 %copy-start.7 = (f32[256,768]{1,0:T(8,128)S(1)}, f32[256,768]{1,0:T(8,128)}, u32[]{:S(2)}) copy-start(f32[256,768]{1,0:T(8,128)} %convolution_multiply_fusion) | copy-start | bytes 2359300
  249.1 9.0 %copy-start.15 = (f32[16,16,192]{2,1,0:T(8,128)S(1)}, f32[16,16,192]{2,1,0:T(8,128)}, u32[]{:S(2)}) copy-start(f32[16,16,192]{2,1,0:T(8,128)} %get-tuple-element.32) | copy-start | bytes 589828
  263.7 58.0 %copy-start.1 = (bf16[192,768]{1,0:T(8,128)(2,1)S(1)}, bf16[192,768]{1,0:T(8,128)(2,1)}, u32[]{:S(2)}) copy-start(bf16[192,768]{1,0:T(8,128)(2,1)} %param.14) | copy-start | bytes 884740
  (3 other events, 6.5 us)
Sparse Core Ops, SparseCore 0:
  10.5 94.5 all-gather.1

commit v5 on v4

--- a/solution.py
+++ b/solution.py
@@ -323,14 +323,14 @@
     s_sums = jnp.sum(s_pieces.astype(jnp.float32), axis=0)
     q_inner_grad, s_inner_grad, gains = exchange(
         [
-            (q_sums.astype(jnp.bfloat16), "pb", False),
-            (s_sums.astype(jnp.bfloat16), "sa", False),
+            (q_sums, "pb", False),
+            (s_sums, "sa", False),
             (jnp.sum(gains, axis=0), "pb", False),
         ],
         4,
     )
-    q_inner_grad = q_inner_grad.astype(jnp.float32).reshape(q_inner_part.shape)
-    s_inner_grad = s_inner_grad.astype(jnp.float32).reshape(s_inner_part.shape)
+    q_inner_grad = q_inner_grad.reshape(q_inner_part.shape)
+    s_inner_grad = s_inner_grad.reshape(s_inner_part.shape)
     gains = jnp.sum(gains, axis=0)
     q_gain_grad, s_gain_grad = gains[0], gains[1]
     return (loss, q_inner_grad, q_outer_grad, q_gain_grad, s_inner_grad, s_outer_grad, s_gain_grad)

time: 335 us -> 348 us (1.039)
  Pallas kernels: 174 us -> 187 us
    pallas_call x4, Pallas kernels: 131 us -> 143 us  [exchange(): pl.pallas_call(kernel, out_shape=out_shape, in_specs=[anywhere] * count,...]
where the time goes in v5:
time: 348 us; the launch traced here: 343 us
  Pallas kernels  187 us (54%)
  matrix products  55.2 us (16%)
  other arithmetic  38 us (11%)
  waiting for transfers between devices  25.4 us (7%)
  local copies, waits for them, and re-layouts  19.8 us (6%)
  between operations  17.1 us (5%)
    pallas_call x4, Pallas kernels, exchange(): pl.pallas_call(kernel, out_shape=out_shape, in_specs=[anywhere] * count,...  143 us
    pallas_call x1, Pallas kernels, plane_gather(): pl.pallas_call(kernel, out_shape=jax.ShapeDtypeStruct((n,) + block.shape,...  43.7 us
    all_gather x1, waiting for transfers between devices, per_device(): s_tokens = lax.all_gather(sql_states, 'pb', axis=1, tiled=True)[0]  24.7 us
    dot_general x2, matrix products, tower_backward(): lax.dot_general(dpre, rows, (((0,), (0,)), ((), ())), preferred_element_t...  18.5 us
    unnamed x63, local copies, waits for them, and re-layouts  13.4 us
    convert_element_type x2, other arithmetic, tower_backward(): high.astype(jnp.bfloat16)  12.2 us
    dot_general x2, matrix products, tower_forward(): jnp.einsum('nt,ntd->nd', weights, input_float.reshape(count, length, widt...  10.8 us
    dot_general x2, matrix products, tower_forward(): pre = jnp.dot(normalized_rows, inner, preferred_element_type=jnp.float32)  7.78 us
  transfers between devices with their start and end apart: 1, of which 1 were waited for; matrix products, arithmetic and copies ran while one was open for 8% of the time, Pallas kernels for 13%

profile of v5, /device:TPU:1, one launch (start us, length us, event | category | flops | bytes accessed | tf_op | source)
XLA Modules:
  0.0 342.6 jit_solution(5317969593323390265)
XLA Ops:
  9.8 43.7 %shard_map.162 = bf16[16,256,768]{2,1,0:T(8,128)(2,1)} custom-call(bf16[256,768]{1,0:T(8,128)(2,1)} %bitcast.144), custom_call_target="tpu_custom_call" | custom-call | tf_op jit(solution)/shard_map/pallas_call | solution.py:134
  53.6 3.9 %convert_reduce_fusion = f32[16,256]{1,0:T(8,128)S(1)} fusion(bf16[16,256,768]{2,1,0:T(8,128)(2,1)} %shard_map.162), kind=kLoop, calls=%fused_computation.25 | loop fusion | flops 6287360 | bytes 6307840 | tf_op jit(solution)/shard_map/reduce_sum | solution.py:165
  60.7 6.3 %reduce-precision_convert_fusion.1 = (bf16[4096,768]{1,0:T(8,128)(2,1)}, bf16[4096,768]{1,0:T(8,128)(2,1)}, bf16[4096,768]{1,0:T(8,128)(2,1)S(1)}) fusion(bf16[16,256,768]{2,1,0:T(8,128)(2,1)S(1)} %copy-done.2, f32[4096]{0:T(1024)S(1)} %bitcast.156, f32[4096]{0:T(1024)S(1)} %bitcast.155, f32[768]{0:T(1024)S(1)} %copy-done.17), kind=kLoop, calls=%fused_computation.15 | loop fusion | flops 28311552 | bytes 25201664 | tf_op jit(solution)/shard_map/convert_element_type | solution.py:213
  67.0 3.7 %multiply_multiply_fusion.3 = (f32[4096,192]{0,1:T(8,128)S(1)}, f32[4096,192]{0,1:T(8,128)}) fusion(bf16[4096,768]{1,0:T(8,128)(2,1)S(1)} %get-tuple-element.65, bf16[768,192]{0,1:T(8,128)(2,1)S(1)} %copy-done.10), kind=kOutput, calls=%fused_computation.51 | convolution fusion | flops 1211105280 | bytes 12877824 | tf_op jit(solution)/shard_map/dot_general | solution.py:191
  70.7 2.7 fusion.32
  74.9 5.5 %fusion.64 = f32[16,1,768]{2,1,0:T(1,128)S(1)} fusion(bf16[16,256,768]{2,1,0:T(8,128)(2,1)} %shard_map.162, f32[16,256,1]{1,0,2:T(8,128)S(1)} %get-tuple-element.74), kind=kOutput, calls=%fused_computation.104 | convolution fusion | flops 37748736 | bytes 6356992 | tf_op jit(solution)/shard_map/nt,ntd->nd/dot_general | solution.py:195
  80.4 24.7 %all-gather.2.cloned.1.call-done = bf16[1,16,256,768]{3,2,0,1:T(8,128)(2,1)} async-done(((bf16[1,1,256,768]{3,2,0,1:T(8,128)(2,1)}), bf16[1,16,256,768]{3,2,0,1:T(8,128)(2,1)}) %all-gather.2.cloned.1.call-update) | async-done | bytes 6291472 | tf_op jit(solution)/shard_map/all_gather | solution.py:241
  105.1 4.2 %multiply_reduce_fusion = f32[16,256]{1,0:T(8,128)S(1)} fusion(bf16[1,16,256,768]{3,2,0,1:T(8,128)(2,1)} %all-gather.2.cloned.1.call-done), kind=kLoop, calls=%fused_computation.22 | loop fusion | flops 9433088 | bytes 6307840 | tf_op jit(solution)/shard_map/reduce_sum | solution.py:162
  109.7 5.9 %reduce-precision_convert_fusion = (bf16[4096,768]{1,0:T(8,128)(2,1)}, bf16[4096,768]{1,0:T(8,128)(2,1)}, bf16[4096,768]{1,0:T(8,128)(2,1)S(1)}) fusion(bf16[1,16,256,768]{3,2,0,1:T(8,128)(2,1)S(1)} %copy-done.3, f32[4096]{0:T(1024)S(1)} %bitcast.148, f32[768]{0:T(1024)S(1)} %copy-done.16), kind=kLoop, calls=%fused_computation.13 | loop fusion | flops 25165824 | bytes 25185280 | tf_op jit(solution)/shard_map/convert_element_type | solution.py:213
  115.6 4.1 %multiply_multiply_fusion.2 = (f32[4096,192]{0,1:T(8,128)S(1)}, f32[4096,192]{0,1:T(8,128)}) fusion(bf16[4096,768]{1,0:T(8,128)(2,1)S(1)} %get-tuple-element.68, bf16[768,192]{0,1:T(8,128)(2,1)S(1)} %copy-done.12), kind=kOutput, calls=%fused_computation.49 | convolution fusion | flops 1211105280 | bytes 12877824 | tf_op jit(solution)/shard_map/dot_general | solution.py:191
  119.7 2.7 fusion.29
  123.9 41.1 %shard_map.163 = (f32[16,16,768]{2,1,0:T(8,128)}, f32[16,16,768]{2,1,0:T(8,128)}) custom-call(f32[16,768]{1,0:T(8,128)} %fusion.78.refs_0_, f32[16,768]{1,0:T(8,128)} %fusion.79.refs_1_), custom_call_target="tpu_custom_call" | custom-call | tf_op jit(solution)/shard_map/pallas_call | solution.py:66
  167.4 5.3 %fusion.15 = f32[16,1,768]{2,1,0:T(1,128)S(1)} fusion(bf16[1,16,256,768]{3,2,0,1:T(8,128)(2,1)} %all-gather.2.cloned.1.call-done, f32[16,256,1]{1,0,2:T(8,128)S(1)} %get-tuple-element.72), kind=kOutput, calls=%fused_computation.26 | convolution fusion | flops 37748736 | bytes 6356992 | tf_op jit(solution)/shard_map/nt,ntd->nd/dot_general | solution.py:195
  173.3 43.6 %shard_map.164 = (f32[16,16,768]{2,1,0:T(8,128)}, f32[16,16,192]{2,1,0:T(8,128)}, f32[16,16,768]{2,1,0:T(8,128)}, f32[16,16,192]{2,1,0:T(8,128)}, s32[16,1,16]{2,1,0:T(1,128)}) custom-call(f32[16,768]{1,0:T(8,128)} %get-tuple-element.81.refs_0_, f32[16,192]{1,0:T(8,128)} %bitcast.153, f32[16,768]{1,0:T(8,128)} %get-tuple-element.80.refs_2_, ...), custom_call_target="tpu_custom_call" | custom-call | tf_op jit(solution)/shard_map/pallas_call | solution.py:66
  218.9 2.4 fusion.80
  222.9 2.2 convolution_multiply_fusion.1
  227.8 4.6 %copy.48 = f32[24,8,16,256]{3,1,2,0:T(8,128)} copy(f32[24,8,16,256]{3,2,1,0:T(8,128)S(1)} %bitcast.128) | data formatting | bytes 6291456
  232.5 9.7 %fusion = f32[192,2304]{1,0:T(8,128)} fusion(bf16[4096,768]{1,0:T(8,128)(2,1)} %get-tuple-element.64, bf16[4096,768]{1,0:T(8,128)(2,1)S(1)} %bitcast.131, bf16[4096,768]{1,0:T(8,128)(2,1)S(1)} %bitcast.123, f32[4096,192]{0,1:T(8,128)} %get-tuple-element.76, f32[4096,192]{0,1:T(8,128)} %bitcast.134, f32[4096]{0:T(1024)S(1)} %div.72), kind=kOutput, calls=%fused_computation | convolution fusion | flops 3689152512 | bytes 26951680 | tf_op jit(solution)/shard_map/dot_general | solution.py:215
  246.2 2.8 copy.51
  249.1 8.9 %fusion.6 = f32[192,2304]{1,0:T(8,128)S(1)} fusion(bf16[4096,768]{1,0:T(8,128)(2,1)} %get-tuple-element.67, bf16[4096,768]{1,0:T(8,128)(2,1)S(1)} %bitcast.133, bf16[4096,768]{1,0:T(8,128)(2,1)S(1)} %bitcast.125, f32[4096,192]{0,1:T(8,128)S(1)} %copy-done.6, f32[4096,192]{0,1:T(8,128)S(1)} %bitcast.135, f32[4096]{0:T(1024)S(1)} %div.75), kind=kOutput, calls=%fused_computation.6 | convolution fusion | flops 3689152512 | bytes 26951680 | tf_op jit(solution)/shard_map/dot_general | solution.py:215
  263.7 23.2 %shard_map.165 = (bf16[16,48,192]{2,1,0:T(8,128)(2,1)}, bf16[16,48,192]{2,1,0:T(8,128)(2,1)}, f32[16,2,768]{2,1,0:T(2,128)}) custom-call(bf16[16,48,192]{2,1,0:T(8,128)(2,1)} %bitcast.140, bf16[16,48,192]{2,1,0:T(8,128)(2,1)} %bitcast.141, f32[2,768]{1,0:T(2,128)} %pad_maximum_fusion.refs_2_), custom_call_target="tpu_custom_call" | custom-call | tf_op jit(solution)/shard_map/pallas_call | solution.py:66
  291.8 35.5 %shard_map.166 = (f32[16,48,192]{2,1,0:T(8,128)}, f32[16,48,192]{2,1,0:T(8,128)}, f32[16,2,768]{2,1,0:T(2,128)}) custom-call(f32[48,192]{1,0:T(8,128)} %convert_reduce_fusion.2.refs_0_, f32[48,192]{1,0:T(8,128)} %convert_reduce_fusion.1.refs_1_, f32[2,768]{1,0:T(2,128)} %reduce_sum.188.refs_2_), custom_call_target="tpu_custom_call" | custom-call | tf_op jit(solution)/shard_map/pallas_call | solution.py:66
  327.2 2.2 copy.29
  331.0 2.2 copy.30
  (111 shorter events, 34.5 us)
Async XLA Ops:
  7.2 66.9 %copy-start = (bf16[192,768]{1,0:T(8,128)(2,1)S(1)}, bf16[192,768]{1,0:T(8,128)(2,1)}, u32[]{:S(2)}) copy-start(bf16[192,768]{1,0:T(8,128)(2,1)} %param.14) | copy-start | bytes 884740
  7.2 97.9 %all-gather.2.cloned.1.call-start = ((), (), s32[]{:S(2)}) async-start(), calls=%async_computation | async-start | bytes 6684672 | tf_op jit(solution)/shard_map/all_gather | solution.py:241
  53.6 5.1 %copy-start.2 = (bf16[16,256,768]{2,1,0:T(8,128)(2,1)S(1)}, bf16[16,256,768]{2,1,0:T(8,128)(2,1)}, u32[]{:S(2)}) copy-start(bf16[16,256,768]{2,1,0:T(8,128)(2,1)} %shard_map.162) | copy-start | bytes 18874372
  60.7 6.4 %copy-start.10 = (bf16[768,192]{0,1:T(8,128)(2,1)S(1)}, bf16[768,192]{0,1:T(8,128)(2,1)}, u32[]{:S(2)}) copy-start(bf16[768,192]{0,1:T(8,128)(2,1)} %param.13) | copy-start | bytes 884740
  67.0 3.7 %copy-start.4 = (bf16[4096,768]{1,0:T(8,128)(2,1)}, bf16[4096,768]{1,0:T(8,128)(2,1)S(1)}, u32[]{:S(2)}) copy-start(bf16[4096,768]{1,0:T(8,128)(2,1)S(1)} %get-tuple-element.65) | copy-start | bytes 18874372
  80.4 29.0 %copy-start.16 = (f32[768]{0:T(1024)S(1)}, f32[768]{0:T(1024)}, u32[]{:S(2)}) copy-start(f32[768]{0:T(1024)} %param.20) | copy-start | bytes 9220
  105.1 4.6 %copy-start.3 = (bf16[1,16,256,768]{3,2,0,1:T(8,128)(2,1)S(1)}, bf16[1,16,256,768]{3,2,0,1:T(8,128)(2,1)}, u32[]{:S(2)}) copy-start(bf16[1,16,256,768]{3,2,0,1:T(8,128)(2,1)} %all-gather.2.cloned.1.call-done) | copy-start | bytes 18874372
  109.7 5.9 %copy-start.12 = (bf16[768,192]{0,1:T(8,128)(2,1)S(1)}, bf16[768,192]{0,1:T(8,128)(2,1)}, u32[]{:S(2)}) copy-start(bf16[768,192]{0,1:T(8,128)(2,1)} %param.18) | copy-start | bytes 884740
  115.6 4.1 %copy-start.5 = (bf16[4096,768]{1,0:T(8,128)(2,1)}, bf16[4096,768]{1,0:T(8,128)(2,1)S(1)}, u32[]{:S(2)}) copy-start(bf16[4096,768]{1,0:T(8,128)(2,1)S(1)} %get-tuple-element.68) | copy-start | bytes 18874372
  119.7 3.3 copy-start.9
  119.7 112.7 %slice-start.4 = ((s8[6291456]{0:T(1024)(128)(4,1)}), s8[2097152]{0:T(1024)(128)(4,1)S(1)}, s32[]{:S(2)}) async-start(s8[6291456]{0:T(1024)(128)(4,1)} %bitcast.130), calls=%async_computation.5 | async-start | bytes 4194304
  218.9 6.1 %copy-start.8 = (f32[16,16,768]{2,1,0:T(8,128)S(1)}, f32[16,16,768]{2,1,0:T(8,128)}, u32[]{:S(2)}) copy-start(f32[16,16,768]{2,1,0:T(8,128)} %get-tuple-element.22) | copy-start | bytes 2359300
  218.9 13.5 %slice-start.5 = ((s8[6291456]{0:T(1024)(128)(4,1)}), s8[4194304]{0:T(1024)(128)(4,1)S(1)}, s32[]{:S(2)}) async-start(s8[6291456]{0:T(1024)(128)(4,1)} %bitcast.130), calls=%async_computation.6 | async-start | bytes 8388608
  222.9 9.6 %slice-start = ((s8[6291456]{0:T(1024)(128)(4,1)}), s8[4194304]{0:T(1024)(128)(4,1)S(1)}, s32[]{:S(2)}) async-start(s8[6291456]{0:T(1024)(128)(4,1)} %bitcast.122), calls=%async_computation.1 | async-start | bytes 8388608
  227.3 5.1 %slice-start.1 = ((s8[6291456]{0:T(1024)(128)(4,1)}), s8[2097152]{0:T(1024)(128)(4,1)S(1)}, s32[]{:S(2)}) async-start(s8[6291456]{0:T(1024)(128)(4,1)} %bitcast.122), calls=%async_computation.2 | async-start | bytes 4194304
  227.8 21.2 %slice-start.2 = ((s8[6291456]{0:T(1024)(128)(4,1)}), s8[4194304]{0:T(1024)(128)(4,1)S(1)}, s32[]{:S(2)}) async-start(s8[6291456]{0:T(1024)(128)(4,1)} %bitcast.124), calls=%async_computation.3 | async-start | bytes 8388608
  227.8 21.2 %slice-start.6 = ((s8[6291456]{0:T(1024)(128)(4,1)}), s8[2097152]{0:T(1024)(128)(4,1)S(1)}, s32[]{:S(2)}) async-start(s8[6291456]{0:T(1024)(128)(4,1)} %bitcast.132), calls=%async_computation.7 | async-start | bytes 4194304
  232.4 9.7 %copy-start.11 = (bf16[768,192]{0,1:T(8,128)(2,1)S(1)}, bf16[768,192]{0,1:T(8,128)(2,1)}, u32[]{:S(2)}) copy-start(bf16[768,192]{0,1:T(8,128)(2,1)} %param.13) | copy-start | bytes 884740
  232.5 16.6 %slice-start.3 = ((s8[6291456]{0:T(1024)(128)(4,1)}), s8[2097152]{0:T(1024)(128)(4,1)S(1)}, s32[]{:S(2)}) async-start(s8[6291456]{0:T(1024)(128)(4,1)} %bitcast.124), calls=%async_computation.4 | async-start | bytes 4194304
  232.5 16.6 %slice-start.7 = ((s8[6291456]{0:T(1024)(128)(4,1)}), s8[4194304]{0:T(1024)(128)(4,1)S(1)}, s32[]{:S(2)}) async-start(s8[6291456]{0:T(1024)(128)(4,1)} %bitcast.132), calls=%async_computation.8 | async-start | bytes 8388608
  249.1 8.9 %copy-start.13 = (bf16[768,192]{0,1:T(8,128)(2,1)S(1)}, bf16[768,192]{0,1:T(8,128)(2,1)}, u32[]{:S(2)}) copy-start(bf16[768,192]{0,1:T(8,128)(2,1)} %param.18) | copy-start | bytes 884740
  249.1 9.0 %copy-start.7 = (f32[256,768]{1,0:T(8,128)S(1)}, f32[256,768]{1,0:T(8,128)}, u32[]{:S(2)}) copy-start(f32[256,768]{1,0:T(8,128)} %convolution_multiply_fusion) | copy-start | bytes 2359300
  249.1 9.0 %copy-start.15 = (f32[16,16,192]{2,1,0:T(8,128)S(1)}, f32[16,16,192]{2,1,0:T(8,128)}, u32[]{:S(2)}) copy-start(f32[16,16,192]{2,1,0:T(8,128)} %get-tuple-element.32) | copy-start | bytes 589828
  259.7 74.7 %copy-start.1 = (bf16[192,768]{1,0:T(8,128)(2,1)S(1)}, bf16[192,768]{1,0:T(8,128)(2,1)}, u32[]{:S(2)}) copy-start(bf16[192,768]{1,0:T(8,128)(2,1)} %param.14) | copy-start | bytes 884740
  (3 other events, 6.5 us)
Sparse Core Ops, SparseCore 0:
  10.5 94.5 all-gather.1

commit v6 on v4

--- a/solution.py
+++ b/solution.py
@@ -250,13 +250,8 @@
     )
     q_outer_f = q_outer_weight.astype(jnp.float32)
     s_outer_f = s_outer_weight.astype(jnp.float32)
-    q_terms, s_terms = exchange(
-        [
-            (jnp.dot(q_pooled, q_outer_f, precision=HIGH), "sa", False),
-            (jnp.dot(s_pooled, s_outer_f, precision=HIGH), "pb", False),
-        ],
-        1,
-    )
+    (q_terms,) = exchange([(jnp.dot(q_pooled, q_outer_f, precision=HIGH), "sa", False)], 1)
+    (s_terms,) = exchange([(jnp.dot(s_pooled, s_outer_f, precision=HIGH), "pb", False)], 6)
     q_block = jnp.sum(q_terms, axis=0) + q_resid
     s_block = jnp.sum(s_terms, axis=0) + s_resid
     q_embed, q_pooled_all, s_embed, s_pooled_all, positive_all = exchange(

time: 335 us -> 334 us (level)
  Pallas kernels: 174 us -> 199 us
  waiting for transfers between devices: 25.4 us -> 0.68 us
    all_gather x1, waiting for transfers between devices: 24.7 us -> 0.01 us  [per_device(): s_tokens = lax.all_gather(sql_states, 'pb', axis=1, tiled=True)[0]]
    pallas_call x4 -> x5, Pallas kernels: 131 us -> 155 us  [exchange(): pl.pallas_call(kernel, out_shape=out_shape, in_specs=[anywhere] * count,...]
  transfers between devices with their start and end apart: 1 -> 1, of which waited for: 1 -> 0; matrix products, arithmetic and copies ran while one was open for 8% -> 9% of each run, Pallas kernels for 13% -> 25%
where the time goes in v6:
time: 334 us; the launch traced here: 329 us
  Pallas kernels  199 us (60%)
  matrix products  54.7 us (16%)
  other arithmetic  40.2 us (12%)
  local copies, waits for them, and re-layouts  17.5 us (5%)
  between operations  17.2 us (5%)
    pallas_call x5, Pallas kernels, exchange(): pl.pallas_call(kernel, out_shape=out_shape, in_specs=[anywhere] * count,...  155 us
    pallas_call x1, Pallas kernels, plane_gather(): pl.pallas_call(kernel, out_shape=jax.ShapeDtypeStruct((n,) + block.shape,...  43.7 us
    dot_general x2, matrix products, tower_backward(): lax.dot_general(dpre, rows, (((0,), (0,)), ((), ())), preferred_element_t...  18.3 us
    convert_element_type x2, other arithmetic, tower_backward(): high.astype(jnp.bfloat16)  12.3 us
    unnamed x63, local copies, waits for them, and re-layouts  11.2 us
    dot_general x2, matrix products, tower_forward(): jnp.einsum('nt,ntd->nd', weights, input_float.reshape(count, length, widt...  10.7 us
    dot_general x2, matrix products, tower_forward(): pre = jnp.dot(normalized_rows, inner, preferred_element_type=jnp.float32)  7.43 us
  transfers between devices with their start and end apart: 1, of which 0 were waited for; matrix products, arithmetic and copies ran while one was open for 9% of the time, Pallas kernels for 25%

profile of v6, /device:TPU:1, one launch (start us, length us, event | category | flops | bytes accessed | tf_op | source)
XLA Modules:
  0.0 329.3 jit_solution(8235547688808609473)
XLA Ops:
  9.8 43.7 %shard_map.162 = bf16[16,256,768]{2,1,0:T(8,128)(2,1)} custom-call(bf16[256,768]{1,0:T(8,128)(2,1)} %bitcast.146), custom_call_target="tpu_custom_call" | custom-call | tf_op jit(solution)/shard_map/pallas_call | solution.py:134
  53.6 3.9 %convert_reduce_fusion = f32[16,256]{1,0:T(8,128)S(1)} fusion(bf16[16,256,768]{2,1,0:T(8,128)(2,1)} %shard_map.162), kind=kLoop, calls=%fused_computation.25 | loop fusion | flops 6287360 | bytes 6307840 | tf_op jit(solution)/shard_map/reduce_sum | solution.py:165
  58.7 1.9 multiply_reduce_fusion.1
  60.7 6.5 %reduce-precision_convert_fusion.1 = (bf16[4096,768]{1,0:T(8,128)(2,1)}, bf16[4096,768]{1,0:T(8,128)(2,1)}, bf16[4096,768]{1,0:T(8,128)(2,1)S(1)}) fusion(bf16[16,256,768]{2,1,0:T(8,128)(2,1)S(1)} %copy-done.2, f32[4096]{0:T(1024)S(1)} %bitcast.158, f32[4096]{0:T(1024)S(1)} %bitcast.157, f32[768]{0:T(1024)S(1)} %copy-done.17), kind=kLoop, calls=%fused_computation.15 | loop fusion | flops 28311552 | bytes 25201664 | tf_op jit(solution)/shard_map/convert_element_type | solution.py:213
  67.2 3.7 %multiply_multiply_fusion.3 = (f32[4096,192]{0,1:T(8,128)S(1)}, f32[4096,192]{0,1:T(8,128)}) fusion(bf16[4096,768]{1,0:T(8,128)(2,1)S(1)} %get-tuple-element.61, bf16[768,192]{0,1:T(8,128)(2,1)S(1)} %copy-done.10), kind=kOutput, calls=%fused_computation.51 | convolution fusion | flops 1211105280 | bytes 12877824 | tf_op jit(solution)/shard_map/dot_general | solution.py:191
  70.9 2.7 fusion.32
  75.0 38.6 %shard_map.163 = f32[16,16,768]{2,1,0:T(8,128)} custom-call(f32[16,768]{1,0:T(8,128)} %fusion.78.refs_0_), custom_call_target="tpu_custom_call" | custom-call | tf_op jit(solution)/shard_map/pallas_call | solution.py:66
  114.9 5.3 %fusion.64 = f32[16,1,768]{2,1,0:T(1,128)S(1)} fusion(bf16[16,256,768]{2,1,0:T(8,128)(2,1)} %shard_map.162, f32[16,256,1]{1,0,2:T(8,128)S(1)} %get-tuple-element.70), kind=kOutput, calls=%fused_computation.104 | convolution fusion | flops 37748736 | bytes 6356992 | tf_op jit(solution)/shard_map/nt,ntd->nd/dot_general | solution.py:195
  120.9 4.2 %multiply_reduce_fusion = f32[16,256]{1,0:T(8,128)S(1)} fusion(bf16[1,16,256,768]{3,2,0,1:T(8,128)(2,1)} %all-gather.2.cloned.1.call-done), kind=kLoop, calls=%fused_computation.22 | loop fusion | flops 9433088 | bytes 6307840 | tf_op jit(solution)/shard_map/reduce_sum | solution.py:162
  125.5 5.8 %reduce-precision_convert_fusion = (bf16[4096,768]{1,0:T(8,128)(2,1)}, bf16[4096,768]{1,0:T(8,128)(2,1)}, bf16[4096,768]{1,0:T(8,128)(2,1)S(1)}) fusion(bf16[1,16,256,768]{3,2,0,1:T(8,128)(2,1)S(1)} %copy-done.3, f32[4096]{0:T(1024)S(1)} %bitcast.150, f32[768]{0:T(1024)S(1)} %copy-done.16), kind=kLoop, calls=%fused_computation.13 | loop fusion | flops 25165824 | bytes 25185280 | tf_op jit(solution)/shard_map/convert_element_type | solution.py:213
  131.3 3.8 %multiply_multiply_fusion.2 = (f32[4096,192]{0,1:T(8,128)S(1)}, f32[4096,192]{0,1:T(8,128)}) fusion(bf16[4096,768]{1,0:T(8,128)(2,1)S(1)} %get-tuple-element.64, bf16[768,192]{0,1:T(8,128)(2,1)S(1)} %copy-done.12), kind=kOutput, calls=%fused_computation.49 | convolution fusion | flops 1211105280 | bytes 12877824 | tf_op jit(solution)/shard_map/dot_general | solution.py:191
  135.1 2.7 fusion.29
  139.3 26.8 %shard_map.164 = f32[16,16,768]{2,1,0:T(8,128)} custom-call(f32[16,768]{1,0:T(8,128)} %fusion.79.refs_0_), custom_call_target="tpu_custom_call" | custom-call | tf_op jit(solution)/shard_map/pallas_call | solution.py:66
  167.3 5.3 %fusion.15 = f32[16,1,768]{2,1,0:T(1,128)S(1)} fusion(bf16[1,16,256,768]{3,2,0,1:T(8,128)(2,1)} %all-gather.2.cloned.1.call-done, f32[16,256,1]{1,0,2:T(8,128)S(1)} %get-tuple-element.68), kind=kOutput, calls=%fused_computation.26 | convolution fusion | flops 37748736 | bytes 6356992 | tf_op jit(solution)/shard_map/nt,ntd->nd/dot_general | solution.py:195
  173.2 46.1 %shard_map.165 = (f32[16,16,768]{2,1,0:T(8,128)}, f32[16,16,192]{2,1,0:T(8,128)}, f32[16,16,768]{2,1,0:T(8,128)}, f32[16,16,192]{2,1,0:T(8,128)}, s32[16,1,16]{2,1,0:T(1,128)}) custom-call(f32[16,768]{1,0:T(8,128)} %bitcast_add_fusion.1.refs_0_, f32[16,192]{1,0:T(8,128)} %bitcast.155, f32[16,768]{1,0:T(8,128)} %bitcast_add_fusion.refs_2_, ...), custom_call_target="tpu_custom_call" | custom-call | tf_op jit(solution)/shard_map/pallas_call | solution.py:66
  221.3 2.4 fusion.80
  224.6 2.4 convolution_multiply_fusion.1
  227.0 1.9 convolution_multiply_fusion
  229.7 4.6 %copy.48 = f32[24,8,16,256]{3,1,2,0:T(8,128)} copy(f32[24,8,16,256]{3,2,1,0:T(8,128)S(1)} %bitcast.132) | data formatting | bytes 6291456
  234.4 9.7 %fusion = f32[192,2304]{1,0:T(8,128)} fusion(bf16[4096,768]{1,0:T(8,128)(2,1)} %get-tuple-element.60, bf16[4096,768]{1,0:T(8,128)(2,1)S(1)} %bitcast.135, bf16[4096,768]{1,0:T(8,128)(2,1)S(1)} %bitcast.127, f32[4096,192]{0,1:T(8,128)} %get-tuple-element.72, f32[4096,192]{0,1:T(8,128)} %bitcast.138, f32[4096]{0:T(1024)S(1)} %div.72), kind=kOutput, calls=%fused_computation | convolution fusion | flops 3689152512 | bytes 26951680 | tf_op jit(solution)/shard_map/dot_general | solution.py:215
  248.2 2.8 copy.51
  251.0 8.6 %fusion.6 = f32[192,2304]{1,0:T(8,128)S(1)} fusion(bf16[4096,768]{1,0:T(8,128)(2,1)} %get-tuple-element.63, bf16[4096,768]{1,0:T(8,128)(2,1)S(1)} %bitcast.137, bf16[4096,768]{1,0:T(8,128)(2,1)S(1)} %bitcast.129, f32[4096,192]{0,1:T(8,128)S(1)} %copy-done.6, f32[4096,192]{0,1:T(8,128)S(1)} %bitcast.139, f32[4096]{0:T(1024)S(1)} %div.75), kind=kOutput, calls=%fused_computation.6 | convolution fusion | flops 3689152512 | bytes 26951680 | tf_op jit(solution)/shard_map/dot_general | solution.py:215
  265.4 21.0 %shard_map.166 = (bf16[16,48,192]{2,1,0:T(8,128)(2,1)}, bf16[16,48,192]{2,1,0:T(8,128)(2,1)}, f32[16,2,768]{2,1,0:T(2,128)}) custom-call(bf16[16,48,192]{2,1,0:T(8,128)(2,1)} %bitcast.144, bf16[16,48,192]{2,1,0:T(8,128)(2,1)} %bitcast.145, f32[2,768]{1,0:T(2,128)} %pad_maximum_fusion.refs_2_), custom_call_target="tpu_custom_call" | custom-call | tf_op jit(solution)/shard_map/pallas_call | solution.py:66
  291.3 22.8 %shard_map.167 = (bf16[16,48,192]{2,1,0:T(8,128)(2,1)}, bf16[16,48,192]{2,1,0:T(8,128)(2,1)}, f32[16,2,768]{2,1,0:T(2,128)}) custom-call(bf16[48,192]{1,0:T(8,128)(2,1)} %reduce_sum.192.refs_0_, bf16[48,192]{1,0:T(8,128)(2,1)} %reduce_sum.193.refs_1_, f32[2,768]{1,0:T(2,128)} %reduce_sum.194.refs_2_), custom_call_target="tpu_custom_call" | custom-call | tf_op jit(solution)/shard_map/pallas_call | solution.py:66
  (114 shorter events, 34.9 us)
Async XLA Ops:
  7.2 67.0 %copy-start = (bf16[192,768]{1,0:T(8,128)(2,1)S(1)}, bf16[192,768]{1,0:T(8,128)(2,1)}, u32[]{:S(2)}) copy-start(bf16[192,768]{1,0:T(8,128)(2,1)} %param.14) | copy-start | bytes 884740
  7.2 113.7 %all-gather.2.cloned.1.call-start = ((), (), s32[]{:S(2)}) async-start(), calls=%async_computation | async-start | bytes 6684672 | tf_op jit(solution)/shard_map/all_gather | solution.py:241
  53.6 5.1 %copy-start.2 = (bf16[16,256,768]{2,1,0:T(8,128)(2,1)S(1)}, bf16[16,256,768]{2,1,0:T(8,128)(2,1)}, u32[]{:S(2)}) copy-start(bf16[16,256,768]{2,1,0:T(8,128)(2,1)} %shard_map.162) | copy-start | bytes 18874372
  60.7 6.5 %copy-start.10 = (bf16[768,192]{0,1:T(8,128)(2,1)S(1)}, bf16[768,192]{0,1:T(8,128)(2,1)}, u32[]{:S(2)}) copy-start(bf16[768,192]{0,1:T(8,128)(2,1)} %param.13) | copy-start | bytes 884740
  67.2 3.7 %copy-start.4 = (bf16[4096,768]{1,0:T(8,128)(2,1)}, bf16[4096,768]{1,0:T(8,128)(2,1)S(1)}, u32[]{:S(2)}) copy-start(bf16[4096,768]{1,0:T(8,128)(2,1)S(1)} %get-tuple-element.61) | copy-start | bytes 18874372
  120.9 4.3 %copy-start.16 = (f32[768]{0:T(1024)S(1)}, f32[768]{0:T(1024)}, u32[]{:S(2)}) copy-start(f32[768]{0:T(1024)} %param.20) | copy-start | bytes 9220
  120.9 4.6 %copy-start.3 = (bf16[1,16,256,768]{3,2,0,1:T(8,128)(2,1)S(1)}, bf16[1,16,256,768]{3,2,0,1:T(8,128)(2,1)}, u32[]{:S(2)}) copy-start(bf16[1,16,256,768]{3,2,0,1:T(8,128)(2,1)} %all-gather.2.cloned.1.call-done) | copy-start | bytes 18874372
  125.5 5.8 %copy-start.12 = (bf16[768,192]{0,1:T(8,128)(2,1)S(1)}, bf16[768,192]{0,1:T(8,128)(2,1)}, u32[]{:S(2)}) copy-start(bf16[768,192]{0,1:T(8,128)(2,1)} %param.18) | copy-start | bytes 884740
  131.3 3.8 %copy-start.5 = (bf16[4096,768]{1,0:T(8,128)(2,1)}, bf16[4096,768]{1,0:T(8,128)(2,1)S(1)}, u32[]{:S(2)}) copy-start(bf16[4096,768]{1,0:T(8,128)(2,1)S(1)} %get-tuple-element.64) | copy-start | bytes 18874372
  135.1 3.3 %copy-start.9 = (bf16[192,768]{1,0:T(8,128)(2,1)S(1)}, bf16[192,768]{1,0:T(8,128)(2,1)}, u32[]{:S(2)}) copy-start(bf16[192,768]{1,0:T(8,128)(2,1)} %param.19) | copy-start | bytes 884740
  135.1 99.3 %slice-start.4 = ((s8[6291456]{0:T(1024)(128)(4,1)}), s8[2097152]{0:T(1024)(128)(4,1)S(1)}, s32[]{:S(2)}) async-start(s8[6291456]{0:T(1024)(128)(4,1)} %bitcast.134), calls=%async_computation.5 | async-start | bytes 4194304
  221.3 5.7 %copy-start.8 = (f32[16,16,768]{2,1,0:T(8,128)S(1)}, f32[16,16,768]{2,1,0:T(8,128)}, u32[]{:S(2)}) copy-start(f32[16,16,768]{2,1,0:T(8,128)} %get-tuple-element.18) | copy-start | bytes 2359300
  223.7 10.7 %slice-start.5 = ((s8[6291456]{0:T(1024)(128)(4,1)}), s8[4194304]{0:T(1024)(128)(4,1)S(1)}, s32[]{:S(2)}) async-start(s8[6291456]{0:T(1024)(128)(4,1)} %bitcast.134), calls=%async_computation.6 | async-start | bytes 8388608
  224.5 9.8 %slice-start = ((s8[6291456]{0:T(1024)(128)(4,1)}), s8[4194304]{0:T(1024)(128)(4,1)S(1)}, s32[]{:S(2)}) async-start(s8[6291456]{0:T(1024)(128)(4,1)} %bitcast.126), calls=%async_computation.1 | async-start | bytes 8388608
  229.2 5.2 %slice-start.1 = ((s8[6291456]{0:T(1024)(128)(4,1)}), s8[2097152]{0:T(1024)(128)(4,1)S(1)}, s32[]{:S(2)}) async-start(s8[6291456]{0:T(1024)(128)(4,1)} %bitcast.126), calls=%async_computation.2 | async-start | bytes 4194304
  229.7 21.2 %slice-start.2 = ((s8[6291456]{0:T(1024)(128)(4,1)}), s8[4194304]{0:T(1024)(128)(4,1)S(1)}, s32[]{:S(2)}) async-start(s8[6291456]{0:T(1024)(128)(4,1)} %bitcast.128), calls=%async_computation.3 | async-start | bytes 8388608
  229.7 21.2 %slice-start.6 = ((s8[6291456]{0:T(1024)(128)(4,1)}), s8[2097152]{0:T(1024)(128)(4,1)S(1)}, s32[]{:S(2)}) async-start(s8[6291456]{0:T(1024)(128)(4,1)} %bitcast.136), calls=%async_computation.7 | async-start | bytes 4194304
  234.4 9.7 %copy-start.11 = (bf16[768,192]{0,1:T(8,128)(2,1)S(1)}, bf16[768,192]{0,1:T(8,128)(2,1)}, u32[]{:S(2)}) copy-start(bf16[768,192]{0,1:T(8,128)(2,1)} %param.13) | copy-start | bytes 884740
  234.4 16.6 %slice-start.3 = ((s8[6291456]{0:T(1024)(128)(4,1)}), s8[2097152]{0:T(1024)(128)(4,1)S(1)}, s32[]{:S(2)}) async-start(s8[6291456]{0:T(1024)(128)(4,1)} %bitcast.128), calls=%async_computation.4 | async-start | bytes 4194304
  234.4 16.6 %slice-start.7 = ((s8[6291456]{0:T(1024)(128)(4,1)}), s8[4194304]{0:T(1024)(128)(4,1)S(1)}, s32[]{:S(2)}) async-start(s8[6291456]{0:T(1024)(128)(4,1)} %bitcast.136), calls=%async_computation.8 | async-start | bytes 8388608
  251.0 8.7 %copy-start.13 = (bf16[768,192]{0,1:T(8,128)(2,1)S(1)}, bf16[768,192]{0,1:T(8,128)(2,1)}, u32[]{:S(2)}) copy-start(bf16[768,192]{0,1:T(8,128)(2,1)} %param.18) | copy-start | bytes 884740
  251.0 8.8 %copy-start.7 = (f32[256,768]{1,0:T(8,128)S(1)}, f32[256,768]{1,0:T(8,128)}, u32[]{:S(2)}) copy-start(f32[256,768]{1,0:T(8,128)} %convolution_multiply_fusion) | copy-start | bytes 2359300
  251.0 8.8 %copy-start.15 = (f32[16,16,192]{2,1,0:T(8,128)S(1)}, f32[16,16,192]{2,1,0:T(8,128)}, u32[]{:S(2)}) copy-start(f32[16,16,192]{2,1,0:T(8,128)} %get-tuple-element.28) | copy-start | bytes 589828
  265.4 55.7 %copy-start.1 = (bf16[192,768]{1,0:T(8,128)(2,1)S(1)}, bf16[192,768]{1,0:T(8,128)(2,1)}, u32[]{:S(2)}) copy-start(bf16[192,768]{1,0:T(8,128)(2,1)} %param.14) | copy-start | bytes 884740
  (3 other events, 6.5 us)
Sparse Core Ops, SparseCore 0:
  10.5 109.3 all-gather.1

commit v7 on v6

--- a/solution.py
+++ b/solution.py
@@ -250,7 +250,7 @@
     )
     q_outer_f = q_outer_weight.astype(jnp.float32)
     s_outer_f = s_outer_weight.astype(jnp.float32)
-    (q_terms,) = exchange([(jnp.dot(q_pooled, q_outer_f, precision=HIGH), "sa", False)], 1)
+    q_terms = plane_gather(jnp.dot(q_pooled, q_outer_f, precision=HIGH), 1)
     (s_terms,) = exchange([(jnp.dot(s_pooled, s_outer_f, precision=HIGH), "pb", False)], 6)
     q_block = jnp.sum(q_terms, axis=0) + q_resid
     s_block = jnp.sum(s_terms, axis=0) + s_resid

time: 334 us -> 324 us (0.970)
  Pallas kernels: 199 us -> 185 us
  waiting for transfers between devices: 0.68 us -> 4.41 us
    pallas_call x5 -> x4, Pallas kernels: 155 us -> 117 us  [exchange(): pl.pallas_call(kernel, out_shape=out_shape, in_specs=[anywhere] * count,...]
    pallas_call x1 -> x2, Pallas kernels: 43.7 us -> 68.3 us  [plane_gather(): pl.pallas_call(kernel, out_shape=jax.ShapeDtypeStruct((n,) + block.shape,...]
    all_gather x1, waiting for transfers between devices: 0.01 us -> 3.73 us  [per_device(): s_tokens = lax.all_gather(sql_states, 'pb', axis=1, tiled=True)[0]]
  transfers between devices with their start and end apart: 1 -> 1, of which waited for: 0 -> 1; matrix products, arithmetic and copies ran while one was open for 9% -> 9% of each run, Pallas kernels for 25% -> 21%
where the time goes in v7:
time: 324 us; the launch traced here: 319 us
  Pallas kernels  185 us (57%)
  matrix products  54.8 us (17%)
  other arithmetic  40.2 us (12%)
  local copies, waits for them, and re-layouts  17.5 us (5%)
  between operations  17.2 us (5%)
  waiting for transfers between devices  4.41 us (1%)
    pallas_call x4, Pallas kernels, exchange(): pl.pallas_call(kernel, out_shape=out_shape, in_specs=[anywhere] * count,...  117 us
    pallas_call x2, Pallas kernels, plane_gather(): pl.pallas_call(kernel, out_shape=jax.ShapeDtypeStruct((n,) + block.shape,...  68.3 us
    dot_general x2, matrix products, tower_backward(): lax.dot_general(dpre, rows, (((0,), (0,)), ((), ())), preferred_element_t...  18.3 us
    convert_element_type x2, other arithmetic, tower_backward(): high.astype(jnp.bfloat16)  12.3 us
    unnamed x63, local copies, waits for them, and re-layouts  11.2 us
    dot_general x2, matrix products, tower_forward(): jnp.einsum('nt,ntd->nd', weights, input_float.reshape(count, length, widt...  10.8 us
    dot_general x2, matrix products, tower_forward(): pre = jnp.dot(normalized_rows, inner, preferred_element_type=jnp.float32)  7.43 us
  transfers between devices with their start and end apart: 1, of which 1 were waited for; matrix products, arithmetic and copies ran while one was open for 9% of the time, Pallas kernels for 21%

profile of v7, /device:TPU:1, one launch (start us, length us, event | category | flops | bytes accessed | tf_op | source)
XLA Modules:
  0.0 319.4 jit_solution(4213344054621950709)
XLA Ops:
  9.8 43.7 %shard_map.162 = bf16[16,256,768]{2,1,0:T(8,128)(2,1)} custom-call(bf16[256,768]{1,0:T(8,128)(2,1)} %bitcast.146), custom_call_target="tpu_custom_call" | custom-call | tf_op jit(solution)/shard_map/pallas_call | solution.py:134
  53.6 3.9 %convert_reduce_fusion = f32[16,256]{1,0:T(8,128)S(1)} fusion(bf16[16,256,768]{2,1,0:T(8,128)(2,1)} %shard_map.162), kind=kLoop, calls=%fused_computation.25 | loop fusion | flops 6287360 | bytes 6307840 | tf_op jit(solution)/shard_map/reduce_sum | solution.py:165
  58.7 1.9 multiply_reduce_fusion.1
  60.7 6.5 %reduce-precision_convert_fusion.1 = (bf16[4096,768]{1,0:T(8,128)(2,1)}, bf16[4096,768]{1,0:T(8,128)(2,1)}, bf16[4096,768]{1,0:T(8,128)(2,1)S(1)}) fusion(bf16[16,256,768]{2,1,0:T(8,128)(2,1)S(1)} %copy-done.2, f32[4096]{0:T(1024)S(1)} %bitcast.158, f32[4096]{0:T(1024)S(1)} %bitcast.157, f32[768]{0:T(1024)S(1)} %copy-done.17), kind=kLoop, calls=%fused_computation.15 | loop fusion | flops 28311552 | bytes 25201664 | tf_op jit(solution)/shard_map/convert_element_type | solution.py:213
  67.2 3.7 %multiply_multiply_fusion.3 = (f32[4096,192]{0,1:T(8,128)S(1)}, f32[4096,192]{0,1:T(8,128)}) fusion(bf16[4096,768]{1,0:T(8,128)(2,1)S(1)} %get-tuple-element.61, bf16[768,192]{0,1:T(8,128)(2,1)S(1)} %copy-done.10), kind=kOutput, calls=%fused_computation.51 | convolution fusion | flops 1211105280 | bytes 12877824 | tf_op jit(solution)/shard_map/dot_general | solution.py:191
  70.9 2.7 fusion.32
  75.0 24.6 %shard_map.163 = f32[16,16,768]{2,1,0:T(8,128)} custom-call(f32[16,768]{1,0:T(8,128)} %fusion.78.src), custom_call_target="tpu_custom_call" | custom-call | tf_op jit(solution)/shard_map/pallas_call | solution.py:134
  100.9 5.4 %fusion.64 = f32[16,1,768]{2,1,0:T(1,128)S(1)} fusion(bf16[16,256,768]{2,1,0:T(8,128)(2,1)} %shard_map.162, f32[16,256,1]{1,0,2:T(8,128)S(1)} %get-tuple-element.70), kind=kOutput, calls=%fused_computation.104 | convolution fusion | flops 37748736 | bytes 6356992 | tf_op jit(solution)/shard_map/nt,ntd->nd/dot_general | solution.py:195
  107.0 3.7 %all-gather.2.cloned.1.call-done = bf16[1,16,256,768]{3,2,0,1:T(8,128)(2,1)} async-done(((bf16[1,1,256,768]{3,2,0,1:T(8,128)(2,1)}), bf16[1,16,256,768]{3,2,0,1:T(8,128)(2,1)}) %all-gather.2.cloned.1.call-update) | async-done | bytes 6291472 | tf_op jit(solution)/shard_map/all_gather | solution.py:241
  110.7 4.2 %multiply_reduce_fusion = f32[16,256]{1,0:T(8,128)S(1)} fusion(bf16[1,16,256,768]{3,2,0,1:T(8,128)(2,1)} %all-gather.2.cloned.1.call-done), kind=kLoop, calls=%fused_computation.22 | loop fusion | flops 9433088 | bytes 6307840 | tf_op jit(solution)/shard_map/reduce_sum | solution.py:162
  115.3 5.8 %reduce-precision_convert_fusion = (bf16[4096,768]{1,0:T(8,128)(2,1)}, bf16[4096,768]{1,0:T(8,128)(2,1)}, bf16[4096,768]{1,0:T(8,128)(2,1)S(1)}) fusion(bf16[1,16,256,768]{3,2,0,1:T(8,128)(2,1)S(1)} %copy-done.3, f32[4096]{0:T(1024)S(1)} %bitcast.150, f32[768]{0:T(1024)S(1)} %copy-done.16), kind=kLoop, calls=%fused_computation.13 | loop fusion | flops 25165824 | bytes 25185280 | tf_op jit(solution)/shard_map/convert_element_type | solution.py:213
  121.1 3.8 %multiply_multiply_fusion.2 = (f32[4096,192]{0,1:T(8,128)S(1)}, f32[4096,192]{0,1:T(8,128)}) fusion(bf16[4096,768]{1,0:T(8,128)(2,1)S(1)} %get-tuple-element.64, bf16[768,192]{0,1:T(8,128)(2,1)S(1)} %copy-done.12), kind=kOutput, calls=%fused_computation.49 | convolution fusion | flops 1211105280 | bytes 12877824 | tf_op jit(solution)/shard_map/dot_general | solution.py:191
  124.9 2.7 fusion.29
  129.1 21.8 %shard_map.164 = f32[16,16,768]{2,1,0:T(8,128)} custom-call(f32[16,768]{1,0:T(8,128)} %fusion.79.refs_0_), custom_call_target="tpu_custom_call" | custom-call | tf_op jit(solution)/shard_map/pallas_call | solution.py:66
  152.1 5.3 %fusion.15 = f32[16,1,768]{2,1,0:T(1,128)S(1)} fusion(bf16[1,16,256,768]{3,2,0,1:T(8,128)(2,1)} %all-gather.2.cloned.1.call-done, f32[16,256,1]{1,0,2:T(8,128)S(1)} %get-tuple-element.68), kind=kOutput, calls=%fused_computation.26 | convolution fusion | flops 37748736 | bytes 6356992 | tf_op jit(solution)/shard_map/nt,ntd->nd/dot_general | solution.py:195
  158.1 51.7 %shard_map.165 = (f32[16,16,768]{2,1,0:T(8,128)}, f32[16,16,192]{2,1,0:T(8,128)}, f32[16,16,768]{2,1,0:T(8,128)}, f32[16,16,192]{2,1,0:T(8,128)}, s32[16,1,16]{2,1,0:T(1,128)}) custom-call(f32[16,768]{1,0:T(8,128)} %bitcast_add_fusion.1.refs_0_, f32[16,192]{1,0:T(8,128)} %bitcast.155, f32[16,768]{1,0:T(8,128)} %bitcast_add_fusion.refs_2_, ...), custom_call_target="tpu_custom_call" | custom-call | tf_op jit(solution)/shard_map/pallas_call | solution.py:66
  211.7 2.4 fusion.80
  215.0 2.4 convolution_multiply_fusion.1
  220.2 4.6 %copy.48 = f32[24,8,16,256]{3,1,2,0:T(8,128)} copy(f32[24,8,16,256]{3,2,1,0:T(8,128)S(1)} %bitcast.132) | data formatting | bytes 6291456
  224.9 9.7 %fusion = f32[192,2304]{1,0:T(8,128)} fusion(bf16[4096,768]{1,0:T(8,128)(2,1)} %get-tuple-element.60, bf16[4096,768]{1,0:T(8,128)(2,1)S(1)} %bitcast.135, bf16[4096,768]{1,0:T(8,128)(2,1)S(1)} %bitcast.127, f32[4096,192]{0,1:T(8,128)} %get-tuple-element.72, f32[4096,192]{0,1:T(8,128)} %bitcast.138, f32[4096]{0:T(1024)S(1)} %div.72), kind=kOutput, calls=%fused_computation | convolution fusion | flops 3689152512 | bytes 26951680 | tf_op jit(solution)/shard_map/dot_general | solution.py:215
  238.6 2.8 copy.51
  241.5 8.6 %fusion.6 = f32[192,2304]{1,0:T(8,128)S(1)} fusion(bf16[4096,768]{1,0:T(8,128)(2,1)} %get-tuple-element.63, bf16[4096,768]{1,0:T(8,128)(2,1)S(1)} %bitcast.137, bf16[4096,768]{1,0:T(8,128)(2,1)S(1)} %bitcast.129, f32[4096,192]{0,1:T(8,128)S(1)} %copy-done.6, f32[4096,192]{0,1:T(8,128)S(1)} %bitcast.139, f32[4096]{0:T(1024)S(1)} %div.75), kind=kOutput, calls=%fused_computation.6 | convolution fusion | flops 3689152512 | bytes 26951680 | tf_op jit(solution)/shard_map/dot_general | solution.py:215
  255.9 20.6 %shard_map.166 = (bf16[16,48,192]{2,1,0:T(8,128)(2,1)}, bf16[16,48,192]{2,1,0:T(8,128)(2,1)}, f32[16,2,768]{2,1,0:T(2,128)}) custom-call(bf16[16,48,192]{2,1,0:T(8,128)(2,1)} %bitcast.144, bf16[16,48,192]{2,1,0:T(8,128)(2,1)} %bitcast.145, f32[2,768]{1,0:T(2,128)} %pad_maximum_fusion.refs_2_), custom_call_target="tpu_custom_call" | custom-call | tf_op jit(solution)/shard_map/pallas_call | solution.py:66
  281.3 22.9 %shard_map.167 = (bf16[16,48,192]{2,1,0:T(8,128)(2,1)}, bf16[16,48,192]{2,1,0:T(8,128)(2,1)}, f32[16,2,768]{2,1,0:T(2,128)}) custom-call(bf16[48,192]{1,0:T(8,128)(2,1)} %reduce_sum.192.refs_0_, bf16[48,192]{1,0:T(8,128)(2,1)} %reduce_sum.193.refs_1_, f32[2,768]{1,0:T(2,128)} %reduce_sum.194.refs_2_), custom_call_target="tpu_custom_call" | custom-call | tf_op jit(solution)/shard_map/pallas_call | solution.py:66
  (114 shorter events, 36.8 us)
Async XLA Ops:
  7.2 67.0 %copy-start = (bf16[192,768]{1,0:T(8,128)(2,1)S(1)}, bf16[192,768]{1,0:T(8,128)(2,1)}, u32[]{:S(2)}) copy-start(bf16[192,768]{1,0:T(8,128)(2,1)} %param.14) | copy-start | bytes 884740
  7.2 103.5 %all-gather.2.cloned.1.call-start = ((), (), s32[]{:S(2)}) async-start(), calls=%async_computation | async-start | bytes 6684672 | tf_op jit(solution)/shard_map/all_gather | solution.py:241
  53.6 5.1 %copy-start.2 = (bf16[16,256,768]{2,1,0:T(8,128)(2,1)S(1)}, bf16[16,256,768]{2,1,0:T(8,128)(2,1)}, u32[]{:S(2)}) copy-start(bf16[16,256,768]{2,1,0:T(8,128)(2,1)} %shard_map.162) | copy-start | bytes 18874372
  60.7 6.5 %copy-start.10 = (bf16[768,192]{0,1:T(8,128)(2,1)S(1)}, bf16[768,192]{0,1:T(8,128)(2,1)}, u32[]{:S(2)}) copy-start(bf16[768,192]{0,1:T(8,128)(2,1)} %param.13) | copy-start | bytes 884740
  67.2 3.7 %copy-start.4 = (bf16[4096,768]{1,0:T(8,128)(2,1)}, bf16[4096,768]{1,0:T(8,128)(2,1)S(1)}, u32[]{:S(2)}) copy-start(bf16[4096,768]{1,0:T(8,128)(2,1)S(1)} %get-tuple-element.61) | copy-start | bytes 18874372
  107.0 8.0 %copy-start.16 = (f32[768]{0:T(1024)S(1)}, f32[768]{0:T(1024)}, u32[]{:S(2)}) copy-start(f32[768]{0:T(1024)} %param.20) | copy-start | bytes 9220
  110.7 4.6 %copy-start.3 = (bf16[1,16,256,768]{3,2,0,1:T(8,128)(2,1)S(1)}, bf16[1,16,256,768]{3,2,0,1:T(8,128)(2,1)}, u32[]{:S(2)}) copy-start(bf16[1,16,256,768]{3,2,0,1:T(8,128)(2,1)} %all-gather.2.cloned.1.call-done) | copy-start | bytes 18874372
  115.3 5.8 %copy-start.12 = (bf16[768,192]{0,1:T(8,128)(2,1)S(1)}, bf16[768,192]{0,1:T(8,128)(2,1)}, u32[]{:S(2)}) copy-start(bf16[768,192]{0,1:T(8,128)(2,1)} %param.18) | copy-start | bytes 884740
  121.1 3.8 %copy-start.5 = (bf16[4096,768]{1,0:T(8,128)(2,1)}, bf16[4096,768]{1,0:T(8,128)(2,1)S(1)}, u32[]{:S(2)}) copy-start(bf16[4096,768]{1,0:T(8,128)(2,1)S(1)} %get-tuple-element.64) | copy-start | bytes 18874372
  124.9 3.3 %copy-start.9 = (bf16[192,768]{1,0:T(8,128)(2,1)S(1)}, bf16[192,768]{1,0:T(8,128)(2,1)}, u32[]{:S(2)}) copy-start(bf16[192,768]{1,0:T(8,128)(2,1)} %param.19) | copy-start | bytes 884740
  124.9 99.9 %slice-start.4 = ((s8[6291456]{0:T(1024)(128)(4,1)}), s8[2097152]{0:T(1024)(128)(4,1)S(1)}, s32[]{:S(2)}) async-start(s8[6291456]{0:T(1024)(128)(4,1)} %bitcast.134), calls=%async_computation.5 | async-start | bytes 4194304
  211.7 5.7 %copy-start.8 = (f32[16,16,768]{2,1,0:T(8,128)S(1)}, f32[16,16,768]{2,1,0:T(8,128)}, u32[]{:S(2)}) copy-start(f32[16,16,768]{2,1,0:T(8,128)} %get-tuple-element.18) | copy-start | bytes 2359300
  214.1 10.7 %slice-start.5 = ((s8[6291456]{0:T(1024)(128)(4,1)}), s8[4194304]{0:T(1024)(128)(4,1)S(1)}, s32[]{:S(2)}) async-start(s8[6291456]{0:T(1024)(128)(4,1)} %bitcast.134), calls=%async_computation.6 | async-start | bytes 8388608
  215.0 9.8 %slice-start = ((s8[6291456]{0:T(1024)(128)(4,1)}), s8[4194304]{0:T(1024)(128)(4,1)S(1)}, s32[]{:S(2)}) async-start(s8[6291456]{0:T(1024)(128)(4,1)} %bitcast.126), calls=%async_computation.1 | async-start | bytes 8388608
  219.7 5.2 %slice-start.1 = ((s8[6291456]{0:T(1024)(128)(4,1)}), s8[2097152]{0:T(1024)(128)(4,1)S(1)}, s32[]{:S(2)}) async-start(s8[6291456]{0:T(1024)(128)(4,1)} %bitcast.126), calls=%async_computation.2 | async-start | bytes 4194304
  220.2 21.2 %slice-start.2 = ((s8[6291456]{0:T(1024)(128)(4,1)}), s8[4194304]{0:T(1024)(128)(4,1)S(1)}, s32[]{:S(2)}) async-start(s8[6291456]{0:T(1024)(128)(4,1)} %bitcast.128), calls=%async_computation.3 | async-start | bytes 8388608
  220.2 21.2 %slice-start.6 = ((s8[6291456]{0:T(1024)(128)(4,1)}), s8[2097152]{0:T(1024)(128)(4,1)S(1)}, s32[]{:S(2)}) async-start(s8[6291456]{0:T(1024)(128)(4,1)} %bitcast.136), calls=%async_computation.7 | async-start | bytes 4194304
  224.8 9.7 %copy-start.11 = (bf16[768,192]{0,1:T(8,128)(2,1)S(1)}, bf16[768,192]{0,1:T(8,128)(2,1)}, u32[]{:S(2)}) copy-start(bf16[768,192]{0,1:T(8,128)(2,1)} %param.13) | copy-start | bytes 884740
  224.9 16.6 %slice-start.3 = ((s8[6291456]{0:T(1024)(128)(4,1)}), s8[2097152]{0:T(1024)(128)(4,1)S(1)}, s32[]{:S(2)}) async-start(s8[6291456]{0:T(1024)(128)(4,1)} %bitcast.128), calls=%async_computation.4 | async-start | bytes 4194304
  224.9 16.6 %slice-start.7 = ((s8[6291456]{0:T(1024)(128)(4,1)}), s8[4194304]{0:T(1024)(128)(4,1)S(1)}, s32[]{:S(2)}) async-start(s8[6291456]{0:T(1024)(128)(4,1)} %bitcast.136), calls=%async_computation.8 | async-start | bytes 8388608
  241.5 8.7 %copy-start.13 = (bf16[768,192]{0,1:T(8,128)(2,1)S(1)}, bf16[768,192]{0,1:T(8,128)(2,1)}, u32[]{:S(2)}) copy-start(bf16[768,192]{0,1:T(8,128)(2,1)} %param.18) | copy-start | bytes 884740
  241.5 8.8 %copy-start.7 = (f32[256,768]{1,0:T(8,128)S(1)}, f32[256,768]{1,0:T(8,128)}, u32[]{:S(2)}) copy-start(f32[256,768]{1,0:T(8,128)} %convolution_multiply_fusion) | copy-start | bytes 2359300
  241.5 8.8 %copy-start.15 = (f32[16,16,192]{2,1,0:T(8,128)S(1)}, f32[16,16,192]{2,1,0:T(8,128)}, u32[]{:S(2)}) copy-start(f32[16,16,192]{2,1,0:T(8,128)} %get-tuple-element.28) | copy-start | bytes 589828
  255.9 55.4 %copy-start.1 = (bf16[192,768]{1,0:T(8,128)(2,1)S(1)}, bf16[192,768]{1,0:T(8,128)(2,1)}, u32[]{:S(2)}) copy-start(bf16[192,768]{1,0:T(8,128)(2,1)} %param.14) | copy-start | bytes 884740
  (3 other events, 6.5 us)
Sparse Core Ops, SparseCore 0:
  10.5 100.1 all-gather.1

commit v8 on v7

--- a/solution.py
+++ b/solution.py
@@ -254,16 +254,22 @@
     (s_terms,) = exchange([(jnp.dot(s_pooled, s_outer_f, precision=HIGH), "pb", False)], 6)
     q_block = jnp.sum(q_terms, axis=0) + q_resid
     s_block = jnp.sum(s_terms, axis=0) + s_resid
-    q_embed, q_pooled_all, s_embed, s_pooled_all, positive_all = exchange(
+    q_embed, q_pooled_all, positive_all = exchange(
         [
             (q_block, "pb", False),
             (q_pooled, "pb", False),
-            (s_block, "sa", False),
-            (s_pooled, "sa", False),
             (positive_column.reshape(1, -1), "pb", False),
         ],
         2,
     )
+    s_width = s_pooled.shape[-1]
+    s_pack = jnp.concatenate(
+        [s_block, s_pooled, jnp.zeros((s_block.shape[0], 128 - (D + s_width) % 128), jnp.float32)],
+        axis=1,
+    )
+    s_pack = plane_gather(s_pack, 7)
+    s_embed = s_pack[:, :, :D]
+    s_pooled_all = s_pack[:, :, D : D + s_width]
     positive_all = positive_all.reshape(-1)
     q_embed = q_embed.reshape(-1, D)
     s_embed = s_embed.reshape(-1, D)

time: 324 us -> 321 us (level)
  waiting for transfers between devices: 4.41 us -> 0.68 us
    pallas_call x2 -> x3, Pallas kernels: 68.3 us -> 98.1 us  [plane_gather(): pl.pallas_call(kernel, out_shape=jax.ShapeDtypeStruct((n,) + block.shape,...]
    pallas_call x4, Pallas kernels: 117 us -> 88.8 us  [exchange(): pl.pallas_call(kernel, out_shape=out_shape, in_specs=[anywhere] * count,...]
    all_gather x1, waiting for transfers between devices: 3.73 us -> 0.01 us  [per_device(): s_tokens = lax.all_gather(sql_states, 'pb', axis=1, tiled=True)[0]]
    unnamed x63 -> x67, local copies, waits for them, and re-layouts: 11.2 us -> 11.2 us
  transfers between devices with their start and end apart: 1 -> 1, of which waited for: 1 -> 0; matrix products, arithmetic and copies ran while one was open for 9% -> 10% of each run, Pallas kernels for 21% -> 31%
where the time goes in v8:
time: 321 us; the launch traced here: 316 us
  Pallas kernels  187 us (58%)
  matrix products  51.7 us (16%)
  other arithmetic  41.6 us (13%)
  local copies, waits for them, and re-layouts  18.3 us (6%)
  between operations  17.2 us (5%)
    pallas_call x3, Pallas kernels, plane_gather(): pl.pallas_call(kernel, out_shape=jax.ShapeDtypeStruct((n,) + block.shape,...  98.1 us
    pallas_call x4, Pallas kernels, exchange(): pl.pallas_call(kernel, out_shape=out_shape, in_specs=[anywhere] * count,...  88.8 us
    dot_general x2, matrix products, tower_backward(): lax.dot_general(dpre, rows, (((0,), (0,)), ((), ())), preferred_element_t...  18.2 us
    convert_element_type x2, other arithmetic, tower_backward(): high.astype(jnp.bfloat16)  12.5 us
    unnamed x67, local copies, waits for them, and re-layouts  11.2 us
    dot_general x2, matrix products, tower_forward(): jnp.einsum('nt,ntd->nd', weights, input_float.reshape(count, length, widt...  10.7 us
    dot_general x2, matrix products, tower_forward(): pre = jnp.dot(normalized_rows, inner, preferred_element_type=jnp.float32)  7.39 us
  transfers between devices with their start and end apart: 1, of which 0 were waited for; matrix products, arithmetic and copies ran while one was open for 10% of the time, Pallas kernels for 31%

profile of v8, /device:TPU:1, one launch (start us, length us, event | category | flops | bytes accessed | tf_op | source)
XLA Modules:
  0.0 316.5 jit_solution(10182527595856143461)
XLA Ops:
  9.8 43.7 %shard_map.162 = bf16[16,256,768]{2,1,0:T(8,128)(2,1)} custom-call(bf16[256,768]{1,0:T(8,128)(2,1)} %bitcast.147), custom_call_target="tpu_custom_call" | custom-call | tf_op jit(solution)/shard_map/pallas_call | solution.py:134
  53.6 3.9 %convert_reduce_fusion = f32[16,256]{1,0:T(8,128)S(1)} fusion(bf16[16,256,768]{2,1,0:T(8,128)(2,1)} %shard_map.162), kind=kLoop, calls=%fused_computation.25 | loop fusion | flops 6287360 | bytes 6307840 | tf_op jit(solution)/shard_map/reduce_sum | solution.py:165
  58.7 1.9 multiply_reduce_fusion.1
  60.7 6.6 %reduce-precision_convert_fusion.1 = (bf16[4096,768]{1,0:T(8,128)(2,1)}, bf16[4096,768]{1,0:T(8,128)(2,1)}, bf16[4096,768]{1,0:T(8,128)(2,1)S(1)}) fusion(bf16[16,256,768]{2,1,0:T(8,128)(2,1)S(1)} %copy-done.2, f32[4096]{0:T(1024)S(1)} %bitcast.158, f32[4096]{0:T(1024)S(1)} %bitcast.157, f32[768]{0:T(1024)S(1)} %copy-done.19), kind=kLoop, calls=%fused_computation.15 | loop fusion | flops 28311552 | bytes 25201664 | tf_op jit(solution)/shard_map/convert_element_type | solution.py:213
  67.3 3.7 %multiply_multiply_fusion.3 = (f32[4096,192]{0,1:T(8,128)S(1)}, f32[4096,192]{0,1:T(8,128)}) fusion(bf16[4096,768]{1,0:T(8,128)(2,1)S(1)} %get-tuple-element.57, bf16[768,192]{0,1:T(8,128)(2,1)S(1)} %copy-done.11), kind=kOutput, calls=%fused_computation.51 | convolution fusion | flops 1211105280 | bytes 12877824 | tf_op jit(solution)/shard_map/dot_general | solution.py:191
  70.9 2.7 fusion.32
  75.1 27.3 %shard_map.163 = f32[16,16,768]{2,1,0:T(8,128)} custom-call(f32[16,768]{1,0:T(8,128)} %fusion.78.src), custom_call_target="tpu_custom_call" | custom-call | tf_op jit(solution)/shard_map/pallas_call | solution.py:134
  103.7 5.3 %fusion.64 = f32[16,1,768]{2,1,0:T(1,128)S(1)} fusion(bf16[16,256,768]{2,1,0:T(8,128)(2,1)} %shard_map.162, f32[16,256,1]{1,0,2:T(8,128)S(1)} %get-tuple-element.66), kind=kOutput, calls=%fused_computation.105 | convolution fusion | flops 37748736 | bytes 6356992 | tf_op jit(solution)/shard_map/nt,ntd->nd/dot_general | solution.py:195
  109.6 27.9 %shard_map.164 = (f32[16,16,768]{2,1,0:T(8,128)}, f32[16,16,192]{2,1,0:T(8,128)}, s32[16,1,16]{2,1,0:T(1,128)}) custom-call(f32[16,768]{1,0:T(8,128)} %bitcast_add_fusion.1.refs_0_, f32[16,192]{1,0:T(8,128)} %bitcast.156, s32[1,16]{1,0:T(1,128)} %bitcast.159), custom_call_target="tpu_custom_call" | custom-call | tf_op jit(solution)/shard_map/pallas_call | solution.py:66
  140.9 4.2 %multiply_reduce_fusion = f32[16,256]{1,0:T(8,128)S(1)} fusion(bf16[1,16,256,768]{3,2,0,1:T(8,128)(2,1)} %all-gather.2.cloned.1.call-done), kind=kLoop, calls=%fused_computation.22 | loop fusion | flops 9433088 | bytes 6307840 | tf_op jit(solution)/shard_map/reduce_sum | solution.py:162
  145.5 5.9 %reduce-precision_convert_fusion = (bf16[4096,768]{1,0:T(8,128)(2,1)}, bf16[4096,768]{1,0:T(8,128)(2,1)}, bf16[4096,768]{1,0:T(8,128)(2,1)S(1)}) fusion(bf16[1,16,256,768]{3,2,0,1:T(8,128)(2,1)S(1)} %copy-done.3, f32[4096]{0:T(1024)S(1)} %bitcast.150, f32[768]{0:T(1024)S(1)} %copy-done.18), kind=kLoop, calls=%fused_computation.13 | loop fusion | flops 25165824 | bytes 25185280 | tf_op jit(solution)/shard_map/convert_element_type | solution.py:213
  151.4 3.7 %multiply_multiply_fusion.2 = (f32[4096,192]{0,1:T(8,128)S(1)}, f32[4096,192]{0,1:T(8,128)}) fusion(bf16[4096,768]{1,0:T(8,128)(2,1)S(1)} %get-tuple-element.60, bf16[768,192]{0,1:T(8,128)(2,1)S(1)} %copy-done.13), kind=kOutput, calls=%fused_computation.49 | convolution fusion | flops 1211105280 | bytes 12877824 | tf_op jit(solution)/shard_map/dot_general | solution.py:191
  155.2 2.7 fusion.29
  158.7 15.7 %shard_map.165 = f32[16,16,768]{2,1,0:T(8,128)} custom-call(f32[16,768]{1,0:T(8,128)} %fusion.79.refs_0_), custom_call_target="tpu_custom_call" | custom-call | tf_op jit(solution)/shard_map/pallas_call | solution.py:66
  175.6 5.3 %fusion.15 = f32[16,1,768]{2,1,0:T(1,128)S(1)} fusion(bf16[1,16,256,768]{3,2,0,1:T(8,128)(2,1)} %all-gather.2.cloned.1.call-done, f32[16,256,1]{1,0,2:T(8,128)S(1)} %get-tuple-element.64), kind=kOutput, calls=%fused_computation.26 | convolution fusion | flops 37748736 | bytes 6356992 | tf_op jit(solution)/shard_map/nt,ntd->nd/dot_general | solution.py:195
  181.6 27.1 %shard_map.166 = f32[16,16,1024]{2,1,0:T(8,128)} custom-call(f32[16,1024]{1,0:T(8,128)} %maximum_maximum_fusion.src), custom_call_target="tpu_custom_call" | custom-call | tf_op jit(solution)/shard_map/pallas_call | solution.py:134
  212.7 1.9 convolution_multiply_fusion
  215.5 4.7 %copy.48 = f32[24,8,16,256]{3,1,2,0:T(8,128)} copy(f32[24,8,16,256]{3,2,1,0:T(8,128)S(1)} %bitcast.132) | data formatting | bytes 6291456
  220.2 9.6 %fusion = f32[192,2304]{1,0:T(8,128)} fusion(bf16[4096,768]{1,0:T(8,128)(2,1)} %get-tuple-element.56, bf16[4096,768]{1,0:T(8,128)(2,1)S(1)} %bitcast.137, bf16[4096,768]{1,0:T(8,128)(2,1)S(1)} %bitcast.127, f32[4096,192]{0,1:T(8,128)} %get-tuple-element.68, f32[4096,192]{0,1:T(8,128)} %bitcast.141, f32[4096]{0:T(1024)S(1)} %copy-done.17), kind=kOutput, calls=%fused_computation | convolution fusion | flops 3689152512 | bytes 26951680 | tf_op jit(solution)/shard_map/dot_general | solution.py:215
  234.0 2.8 copy.51
  236.8 8.6 %fusion.6 = f32[192,2304]{1,0:T(8,128)S(1)} fusion(bf16[4096,768]{1,0:T(8,128)(2,1)} %get-tuple-element.59, bf16[4096,768]{1,0:T(8,128)(2,1)S(1)} %bitcast.139, bf16[4096,768]{1,0:T(8,128)(2,1)S(1)} %bitcast.129, f32[4096,192]{0,1:T(8,128)S(1)} %copy-done.6, f32[4096,192]{0,1:T(8,128)S(1)} %bitcast.142, f32[4096]{0:T(1024)S(1)} %copy-done.16), kind=kOutput, calls=%fused_computation.6 | convolution fusion | flops 3689152512 | bytes 26951680 | tf_op jit(solution)/shard_map/dot_general | solution.py:215
  251.2 22.0 %shard_map.167 = (bf16[16,48,192]{2,1,0:T(8,128)(2,1)}, bf16[16,48,192]{2,1,0:T(8,128)(2,1)}, f32[16,2,768]{2,1,0:T(2,128)}) custom-call(bf16[16,48,192]{2,1,0:T(8,128)(2,1)} %bitcast.145, bf16[16,48,192]{2,1,0:T(8,128)(2,1)} %bitcast.146, f32[2,768]{1,0:T(2,128)} %pad_maximum_fusion.refs_2_), custom_call_target="tpu_custom_call" | custom-call | tf_op jit(solution)/shard_map/pallas_call | solution.py:66
  273.2 1.7 reduce_sum.192.refs_0_
  278.1 23.1 %shard_map.168 = (bf16[16,48,192]{2,1,0:T(8,128)(2,1)}, bf16[16,48,192]{2,1,0:T(8,128)(2,1)}, f32[16,2,768]{2,1,0:T(2,128)}) custom-call(bf16[48,192]{1,0:T(8,128)(2,1)} %reduce_sum.192.refs_0_, bf16[48,192]{1,0:T(8,128)(2,1)} %reduce_sum.193.refs_1_, f32[2,768]{1,0:T(2,128)} %reduce_sum.194.refs_2_), custom_call_target="tpu_custom_call" | custom-call | tf_op jit(solution)/shard_map/pallas_call | solution.py:66
  (125 shorter events, 37.1 us)
Async XLA Ops:
  7.2 67.1 %copy-start = (bf16[192,768]{1,0:T(8,128)(2,1)S(1)}, bf16[192,768]{1,0:T(8,128)(2,1)}, u32[]{:S(2)}) copy-start(bf16[192,768]{1,0:T(8,128)(2,1)} %param.14) | copy-start | bytes 884740
  7.2 133.7 %all-gather.2.cloned.1.call-start = ((), (), s32[]{:S(2)}) async-start(), calls=%async_computation | async-start | bytes 6684672 | tf_op jit(solution)/shard_map/all_gather | solution.py:241
  53.6 5.1 %copy-start.2 = (bf16[16,256,768]{2,1,0:T(8,128)(2,1)S(1)}, bf16[16,256,768]{2,1,0:T(8,128)(2,1)}, u32[]{:S(2)}) copy-start(bf16[16,256,768]{2,1,0:T(8,128)(2,1)} %shard_map.162) | copy-start | bytes 18874372
  60.7 6.6 %copy-start.11 = (bf16[768,192]{0,1:T(8,128)(2,1)S(1)}, bf16[768,192]{0,1:T(8,128)(2,1)}, u32[]{:S(2)}) copy-start(bf16[768,192]{0,1:T(8,128)(2,1)} %param.13) | copy-start | bytes 884740
  140.8 4.3 %copy-start.18 = (f32[768]{0:T(1024)S(1)}, f32[768]{0:T(1024)}, u32[]{:S(2)}) copy-start(f32[768]{0:T(1024)} %param.20) | copy-start | bytes 9220
  140.8 4.6 %copy-start.3 = (bf16[1,16,256,768]{3,2,0,1:T(8,128)(2,1)S(1)}, bf16[1,16,256,768]{3,2,0,1:T(8,128)(2,1)}, u32[]{:S(2)}) copy-start(bf16[1,16,256,768]{3,2,0,1:T(8,128)(2,1)} %all-gather.2.cloned.1.call-done) | copy-start | bytes 18874372
  145.5 5.9 %copy-start.13 = (bf16[768,192]{0,1:T(8,128)(2,1)S(1)}, bf16[768,192]{0,1:T(8,128)(2,1)}, u32[]{:S(2)}) copy-start(bf16[768,192]{0,1:T(8,128)(2,1)} %param.18) | copy-start | bytes 884740
  151.4 3.7 %copy-start.5 = (bf16[4096,768]{1,0:T(8,128)(2,1)}, bf16[4096,768]{1,0:T(8,128)(2,1)S(1)}, u32[]{:S(2)}) copy-start(bf16[4096,768]{1,0:T(8,128)(2,1)S(1)} %get-tuple-element.60) | copy-start | bytes 18874372
  155.2 65.0 %slice-start.4 = ((s8[6291456]{0:T(1024)(128)(4,1)}), s8[2097152]{0:T(1024)(128)(4,1)S(1)}, s32[]{:S(2)}) async-start(s8[6291456]{0:T(1024)(128)(4,1)} %bitcast.136), calls=%async_computation.5 | async-start | bytes 4194304
  181.0 29.0 %copy-start.8 = (f32[16,16,768]{2,1,0:T(8,128)S(1)}, f32[16,16,768]{2,1,0:T(8,128)}, u32[]{:S(2)}) copy-start(f32[16,16,768]{2,1,0:T(8,128)} %get-tuple-element.16) | copy-start | bytes 2359300
  208.7 4.0 %copy-start.9 = (f32[16,16,768]{2,1,0:T(8,128)S(1)}, f32[16,16,768]{2,1,0:T(8,128)}, u32[]{:S(2)}) copy-start(f32[16,16,768]{2,1,0:T(8,128)} %get-tuple-element.16) | copy-start | bytes 2359300
  210.0 10.2 %slice-start.5 = ((s8[6291456]{0:T(1024)(128)(4,1)}), s8[4194304]{0:T(1024)(128)(4,1)S(1)}, s32[]{:S(2)}) async-start(s8[6291456]{0:T(1024)(128)(4,1)} %bitcast.136), calls=%async_computation.6 | async-start | bytes 8388608
  211.8 8.4 %slice-start = ((s8[6291456]{0:T(1024)(128)(4,1)}), s8[4194304]{0:T(1024)(128)(4,1)S(1)}, s32[]{:S(2)}) async-start(s8[6291456]{0:T(1024)(128)(4,1)} %bitcast.126), calls=%async_computation.1 | async-start | bytes 8388608
  215.0 5.2 %slice-start.1 = ((s8[6291456]{0:T(1024)(128)(4,1)}), s8[2097152]{0:T(1024)(128)(4,1)S(1)}, s32[]{:S(2)}) async-start(s8[6291456]{0:T(1024)(128)(4,1)} %bitcast.126), calls=%async_computation.2 | async-start | bytes 4194304
  215.0 5.2 %copy-start.17 = (f32[4096]{0:T(1024)S(1)}, f32[4096]{0:T(1024)}, u32[]{:S(2)}) copy-start(f32[4096]{0:T(1024)} %div.72) | copy-start | bytes 49156
  215.5 21.2 %slice-start.2 = ((s8[6291456]{0:T(1024)(128)(4,1)}), s8[4194304]{0:T(1024)(128)(4,1)S(1)}, s32[]{:S(2)}) async-start(s8[6291456]{0:T(1024)(128)(4,1)} %bitcast.128), calls=%async_computation.3 | async-start | bytes 8388608
  215.5 21.2 %slice-start.6 = ((s8[6291456]{0:T(1024)(128)(4,1)}), s8[2097152]{0:T(1024)(128)(4,1)S(1)}, s32[]{:S(2)}) async-start(s8[6291456]{0:T(1024)(128)(4,1)} %bitcast.138), calls=%async_computation.7 | async-start | bytes 4194304
  220.2 9.6 %copy-start.12 = (bf16[768,192]{0,1:T(8,128)(2,1)S(1)}, bf16[768,192]{0,1:T(8,128)(2,1)}, u32[]{:S(2)}) copy-start(bf16[768,192]{0,1:T(8,128)(2,1)} %param.13) | copy-start | bytes 884740
  220.2 16.5 %slice-start.3 = ((s8[6291456]{0:T(1024)(128)(4,1)}), s8[2097152]{0:T(1024)(128)(4,1)S(1)}, s32[]{:S(2)}) async-start(s8[6291456]{0:T(1024)(128)(4,1)} %bitcast.128), calls=%async_computation.4 | async-start | bytes 4194304
  220.2 16.5 %slice-start.7 = ((s8[6291456]{0:T(1024)(128)(4,1)}), s8[4194304]{0:T(1024)(128)(4,1)S(1)}, s32[]{:S(2)}) async-start(s8[6291456]{0:T(1024)(128)(4,1)} %bitcast.138), calls=%async_computation.8 | async-start | bytes 8388608
  236.8 8.7 %copy-start.14 = (bf16[768,192]{0,1:T(8,128)(2,1)S(1)}, bf16[768,192]{0,1:T(8,128)(2,1)}, u32[]{:S(2)}) copy-start(bf16[768,192]{0,1:T(8,128)(2,1)} %param.18) | copy-start | bytes 884740
  236.8 8.8 %slice-start.8 = ((f32[16,16,1024]{2,1,0:T(8,128)}), f32[16,16,192]{2,1,0:T(8,128)S(1)}, s32[]{:S(2)}) async-start(f32[16,16,1024]{2,1,0:T(8,128)} %shard_map.166), calls=%async_computation.9 | async-start | bytes 524288 | tf_op jit(solution)/shard_map/slice | solution.py:272
  236.8 8.8 %copy-start.7 = (f32[256,768]{1,0:T(8,128)S(1)}, f32[256,768]{1,0:T(8,128)}, u32[]{:S(2)}) copy-start(f32[256,768]{1,0:T(8,128)} %convolution_multiply_fusion) | copy-start | bytes 2359300
  251.2 57.1 %copy-start.1 = (bf16[192,768]{1,0:T(8,128)(2,1)S(1)}, bf16[192,768]{1,0:T(8,128)(2,1)}, u32[]{:S(2)}) copy-start(bf16[192,768]{1,0:T(8,128)(2,1)} %param.14) | copy-start | bytes 884740
  (6 other events, 15.7 us)
Sparse Core Ops, SparseCore 0:
  10.5 100.1 all-gather.1

commit v9 on v8

--- a/solution.py
+++ b/solution.py
@@ -251,17 +251,17 @@
     q_outer_f = q_outer_weight.astype(jnp.float32)
     s_outer_f = s_outer_weight.astype(jnp.float32)
     q_terms = plane_gather(jnp.dot(q_pooled, q_outer_f, precision=HIGH), 1)
-    (s_terms,) = exchange([(jnp.dot(s_pooled, s_outer_f, precision=HIGH), "pb", False)], 6)
     q_block = jnp.sum(q_terms, axis=0) + q_resid
-    s_block = jnp.sum(s_terms, axis=0) + s_resid
-    q_embed, q_pooled_all, positive_all = exchange(
+    q_embed, q_pooled_all, positive_all, s_terms = exchange(
         [
             (q_block, "pb", False),
             (q_pooled, "pb", False),
             (positive_column.reshape(1, -1), "pb", False),
+            (jnp.dot(s_pooled, s_outer_f, precision=HIGH), "pb", False),
         ],
         2,
     )
+    s_block = jnp.sum(s_terms, axis=0) + s_resid
     s_width = s_pooled.shape[-1]
     s_pack = jnp.concatenate(
         [s_block, s_pooled, jnp.zeros((s_block.shape[0], 128 - (D + s_width) % 128), jnp.float32)],

time: 321 us -> 317 us (0.988)
  Pallas kernels: 187 us -> 180 us
    pallas_call x3, Pallas kernels: 98.1 us -> 93.3 us  [plane_gather(): pl.pallas_call(kernel, out_shape=jax.ShapeDtypeStruct((n,) + block.shape,...]
    pallas_call x4 -> x3, Pallas kernels: 88.8 us -> 86.9 us  [exchange(): pl.pallas_call(kernel, out_shape=out_shape, in_specs=[anywhere] * count,...]
    unnamed x67 -> x63, local copies, waits for them, and re-layouts: 11.2 us -> 11 us
  transfers between devices with their start and end apart: 1 -> 1, of which waited for: 0 -> 1; matrix products, arithmetic and copies ran while one was open for 10% -> 10% of each run, Pallas kernels for 31% -> 22%
where the time goes in v9:
time: 317 us; the launch traced here: 313 us
  Pallas kernels  180 us (57%)
  matrix products  51.1 us (16%)
  other arithmetic  41.4 us (13%)
  local copies, waits for them, and re-layouts  19.8 us (6%)
  between operations  17.2 us (5%)
  waiting for transfers between devices  3.72 us (1%)
    pallas_call x3, Pallas kernels, plane_gather(): pl.pallas_call(kernel, out_shape=jax.ShapeDtypeStruct((n,) + block.shape,...  93.3 us
    pallas_call x3, Pallas kernels, exchange(): pl.pallas_call(kernel, out_shape=out_shape, in_specs=[anywhere] * count,...  86.9 us
    dot_general x2, matrix products, tower_backward(): lax.dot_general(dpre, rows, (((0,), (0,)), ((), ())), preferred_element_t...  17.7 us
    convert_element_type x2, other arithmetic, tower_backward(): high.astype(jnp.bfloat16)  12.3 us
    unnamed x63, local copies, waits for them, and re-layouts  11 us
    dot_general x2, matrix products, tower_forward(): jnp.einsum('nt,ntd->nd', weights, input_float.reshape(count, length, widt...  10.8 us
    dot_general x2, matrix products, tower_forward(): pre = jnp.dot(normalized_rows, inner, preferred_element_type=jnp.float32)  7.43 us
  transfers between devices with their start and end apart: 1, of which 1 were waited for; matrix products, arithmetic and copies ran while one was open for 10% of the time, Pallas kernels for 22%

profile of v9, /device:TPU:1, one launch (start us, length us, event | category | flops | bytes accessed | tf_op | source)
XLA Modules:
  0.0 313.4 jit_solution(9456553274398557805)
XLA Ops:
  9.8 43.7 %shard_map.162 = bf16[16,256,768]{2,1,0:T(8,128)(2,1)} custom-call(bf16[256,768]{1,0:T(8,128)(2,1)} %bitcast.147), custom_call_target="tpu_custom_call" | custom-call | tf_op jit(solution)/shard_map/pallas_call | solution.py:134
  53.6 3.9 %convert_reduce_fusion = f32[16,256]{1,0:T(8,128)S(1)} fusion(bf16[16,256,768]{2,1,0:T(8,128)(2,1)} %shard_map.162), kind=kLoop, calls=%fused_computation.25 | loop fusion | flops 6287360 | bytes 6307840 | tf_op jit(solution)/shard_map/reduce_sum | solution.py:165
  58.7 1.9 multiply_reduce_fusion.1
  60.7 6.5 %reduce-precision_convert_fusion.1 = (bf16[4096,768]{1,0:T(8,128)(2,1)}, bf16[4096,768]{1,0:T(8,128)(2,1)}, bf16[4096,768]{1,0:T(8,128)(2,1)S(1)}) fusion(bf16[16,256,768]{2,1,0:T(8,128)(2,1)S(1)} %copy-done.2, f32[4096]{0:T(1024)S(1)} %bitcast.158, f32[4096]{0:T(1024)S(1)} %bitcast.157, f32[768]{0:T(1024)S(1)} %copy-done.17), kind=kLoop, calls=%fused_computation.15 | loop fusion | flops 28311552 | bytes 25201664 | tf_op jit(solution)/shard_map/convert_element_type | solution.py:213
  67.2 3.7 %multiply_multiply_fusion.3 = (f32[4096,192]{0,1:T(8,128)S(1)}, f32[4096,192]{0,1:T(8,128)}) fusion(bf16[4096,768]{1,0:T(8,128)(2,1)S(1)} %get-tuple-element.59, bf16[768,192]{0,1:T(8,128)(2,1)S(1)} %copy-done.10), kind=kOutput, calls=%fused_computation.51 | convolution fusion | flops 1211105280 | bytes 12877824 | tf_op jit(solution)/shard_map/dot_general | solution.py:191
  70.9 2.7 fusion.32
  75.1 24.6 %shard_map.163 = f32[16,16,768]{2,1,0:T(8,128)} custom-call(f32[16,768]{1,0:T(8,128)} %fusion.78.src), custom_call_target="tpu_custom_call" | custom-call | tf_op jit(solution)/shard_map/pallas_call | solution.py:134
  101.6 5.5 %fusion.64 = f32[16,1,768]{2,1,0:T(1,128)S(1)} fusion(bf16[16,256,768]{2,1,0:T(8,128)(2,1)} %shard_map.162, f32[16,256,1]{1,0,2:T(8,128)S(1)} %get-tuple-element.68), kind=kOutput, calls=%fused_computation.105 | convolution fusion | flops 37748736 | bytes 6356992 | tf_op jit(solution)/shard_map/nt,ntd->nd/dot_general | solution.py:195
  107.7 3.0 all-gather.2.cloned.1.call-done
  110.7 4.2 %multiply_reduce_fusion = f32[16,256]{1,0:T(8,128)S(1)} fusion(bf16[1,16,256,768]{3,2,0,1:T(8,128)(2,1)} %all-gather.2.cloned.1.call-done), kind=kLoop, calls=%fused_computation.22 | loop fusion | flops 9433088 | bytes 6307840 | tf_op jit(solution)/shard_map/reduce_sum | solution.py:162
  115.3 5.8 %reduce-precision_convert_fusion = (bf16[4096,768]{1,0:T(8,128)(2,1)}, bf16[4096,768]{1,0:T(8,128)(2,1)}, bf16[4096,768]{1,0:T(8,128)(2,1)S(1)}) fusion(bf16[1,16,256,768]{3,2,0,1:T(8,128)(2,1)S(1)} %copy-done.3, f32[4096]{0:T(1024)S(1)} %bitcast.150, f32[768]{0:T(1024)S(1)} %copy-done.16), kind=kLoop, calls=%fused_computation.13 | loop fusion | flops 25165824 | bytes 25185280 | tf_op jit(solution)/shard_map/convert_element_type | solution.py:213
  121.1 3.8 %multiply_multiply_fusion.2 = (f32[4096,192]{0,1:T(8,128)S(1)}, f32[4096,192]{0,1:T(8,128)}) fusion(bf16[4096,768]{1,0:T(8,128)(2,1)S(1)} %get-tuple-element.62, bf16[768,192]{0,1:T(8,128)(2,1)S(1)} %copy-done.12), kind=kOutput, calls=%fused_computation.49 | convolution fusion | flops 1211105280 | bytes 12877824 | tf_op jit(solution)/shard_map/dot_general | solution.py:191
  124.9 2.7 fusion.29
  128.4 39.7 %shard_map.164 = (f32[16,16,768]{2,1,0:T(8,128)}, f32[16,16,192]{2,1,0:T(8,128)}, s32[16,1,16]{2,1,0:T(1,128)}, f32[16,16,768]{2,1,0:T(8,128)}) custom-call(f32[16,768]{1,0:T(8,128)} %bitcast_add_fusion.1.refs_0_, f32[16,192]{1,0:T(8,128)} %bitcast.154, s32[1,16]{1,0:T(1,128)} %bitcast.159, f32[16,768]{1,0:T(8,128)} %fusion.79.refs_3_), custom_call_target="tpu_custom_call" | custom-call | tf_op jit(solution)/shard_map/pallas_call | solution.py:66
  169.3 5.3 %fusion.15 = f32[16,1,768]{2,1,0:T(1,128)S(1)} fusion(bf16[1,16,256,768]{3,2,0,1:T(8,128)(2,1)} %all-gather.2.cloned.1.call-done, f32[16,256,1]{1,0,2:T(8,128)S(1)} %get-tuple-element.66), kind=kOutput, calls=%fused_computation.26 | convolution fusion | flops 37748736 | bytes 6356992 | tf_op jit(solution)/shard_map/nt,ntd->nd/dot_general | solution.py:195
  175.3 24.9 %shard_map.165 = f32[16,16,1024]{2,1,0:T(8,128)} custom-call(f32[16,1024]{1,0:T(8,128)} %maximum_maximum_fusion.src), custom_call_target="tpu_custom_call" | custom-call | tf_op jit(solution)/shard_map/pallas_call | solution.py:134
  205.5 2.4 convolution_multiply_fusion
  208.8 4.5 %copy.48 = f32[24,8,16,256]{3,1,2,0:T(8,128)} copy(f32[24,8,16,256]{3,2,1,0:T(8,128)S(1)} %bitcast.132) | data formatting | bytes 6291456
  213.3 11.7 %fusion = f32[192,2304]{1,0:T(8,128)} fusion(bf16[4096,768]{1,0:T(8,128)(2,1)} %get-tuple-element.58, bf16[4096,768]{1,0:T(8,128)(2,1)} %get-tuple-element.57, bf16[4096,768]{1,0:T(8,128)(2,1)S(1)} %bitcast.127, f32[4096,192]{0,1:T(8,128)} %get-tuple-element.70, f32[4096,192]{0,1:T(8,128)} %bitcast.141, f32[4096]{0:T(1024)} %div.72), kind=kOutput, calls=%fused_computation | convolution fusion | flops 3689152512 | bytes 26951680 | tf_op jit(solution)/shard_map/dot_general | solution.py:215
  226.4 1.8 fusion.49
  229.0 2.8 copy.51
  231.9 6.0 %fusion.6 = f32[192,2304]{1,0:T(8,128)} fusion(bf16[4096,768]{1,0:T(8,128)(2,1)S(1)} %bitcast.139, bf16[4096,768]{1,0:T(8,128)(2,1)S(1)} %bitcast.137, bf16[4096,768]{1,0:T(8,128)(2,1)S(1)} %bitcast.129, f32[4096,192]{0,1:T(8,128)S(1)} %copy-done.6, f32[4096,192]{0,1:T(8,128)S(1)} %bitcast.142, f32[4096]{0:T(1024)S(1)} %div.75), kind=kOutput, calls=%fused_computation.6 | convolution fusion | flops 3689152512 | bytes 26951680 | tf_op jit(solution)/shard_map/dot_general | solution.py:215
  246.0 23.7 %shard_map.166 = (bf16[16,48,192]{2,1,0:T(8,128)(2,1)}, bf16[16,48,192]{2,1,0:T(8,128)(2,1)}, f32[16,2,768]{2,1,0:T(2,128)}) custom-call(bf16[16,48,192]{2,1,0:T(8,128)(2,1)} %bitcast.145, bf16[16,48,192]{2,1,0:T(8,128)(2,1)} %bitcast.146, f32[2,768]{1,0:T(2,128)} %pad_maximum_fusion.refs_2_), custom_call_target="tpu_custom_call" | custom-call | tf_op jit(solution)/shard_map/pallas_call | solution.py:66
  274.6 23.5 %shard_map.167 = (bf16[16,48,192]{2,1,0:T(8,128)(2,1)}, bf16[16,48,192]{2,1,0:T(8,128)(2,1)}, f32[16,2,768]{2,1,0:T(2,128)}) custom-call(bf16[48,192]{1,0:T(8,128)(2,1)} %reduce_sum.192.refs_0_, bf16[48,192]{1,0:T(8,128)(2,1)} %reduce_sum.193.refs_1_, f32[2,768]{1,0:T(2,128)} %reduce_sum.194.refs_2_), custom_call_target="tpu_custom_call" | custom-call | tf_op jit(solution)/shard_map/pallas_call | solution.py:66
  (120 shorter events, 37.9 us)
Async XLA Ops:
  7.2 67.0 %copy-start = (bf16[192,768]{1,0:T(8,128)(2,1)S(1)}, bf16[192,768]{1,0:T(8,128)(2,1)}, u32[]{:S(2)}) copy-start(bf16[192,768]{1,0:T(8,128)(2,1)} %param.14) | copy-start | bytes 884740
  7.2 103.5 %all-gather.2.cloned.1.call-start = ((), (), s32[]{:S(2)}) async-start(), calls=%async_computation | async-start | bytes 6684672 | tf_op jit(solution)/shard_map/all_gather | solution.py:241
  53.6 5.1 %copy-start.2 = (bf16[16,256,768]{2,1,0:T(8,128)(2,1)S(1)}, bf16[16,256,768]{2,1,0:T(8,128)(2,1)}, u32[]{:S(2)}) copy-start(bf16[16,256,768]{2,1,0:T(8,128)(2,1)} %shard_map.162) | copy-start | bytes 18874372
  60.7 6.5 %copy-start.10 = (bf16[768,192]{0,1:T(8,128)(2,1)S(1)}, bf16[768,192]{0,1:T(8,128)(2,1)}, u32[]{:S(2)}) copy-start(bf16[768,192]{0,1:T(8,128)(2,1)} %param.13) | copy-start | bytes 884740
  107.6 7.3 %copy-start.16 = (f32[768]{0:T(1024)S(1)}, f32[768]{0:T(1024)}, u32[]{:S(2)}) copy-start(f32[768]{0:T(1024)} %param.20) | copy-start | bytes 9220
  110.7 4.6 %copy-start.3 = (bf16[1,16,256,768]{3,2,0,1:T(8,128)(2,1)S(1)}, bf16[1,16,256,768]{3,2,0,1:T(8,128)(2,1)}, u32[]{:S(2)}) copy-start(bf16[1,16,256,768]{3,2,0,1:T(8,128)(2,1)} %all-gather.2.cloned.1.call-done) | copy-start | bytes 18874372
  115.3 5.8 %copy-start.12 = (bf16[768,192]{0,1:T(8,128)(2,1)S(1)}, bf16[768,192]{0,1:T(8,128)(2,1)}, u32[]{:S(2)}) copy-start(bf16[768,192]{0,1:T(8,128)(2,1)} %param.18) | copy-start | bytes 884740
  121.1 3.8 %copy-start.5 = (bf16[4096,768]{1,0:T(8,128)(2,1)}, bf16[4096,768]{1,0:T(8,128)(2,1)S(1)}, u32[]{:S(2)}) copy-start(bf16[4096,768]{1,0:T(8,128)(2,1)S(1)} %get-tuple-element.62) | copy-start | bytes 18874372
  174.6 27.3 %copy-start.15 = (s32[16,1,16]{2,1,0:T(1,128)S(1)}, s32[16,1,16]{2,1,0:T(1,128)}, u32[]{:S(2)}) copy-start(s32[16,1,16]{2,1,0:T(1,128)} %get-tuple-element.19) | copy-start | bytes 3076
  174.6 28.1 %copy-start.7 = (f32[16,16,768]{2,1,0:T(8,128)S(1)}, f32[16,16,768]{2,1,0:T(8,128)}, u32[]{:S(2)}) copy-start(f32[16,16,768]{2,1,0:T(8,128)} %get-tuple-element.17) | copy-start | bytes 2359300
  204.6 8.7 %slice-start = ((s8[6291456]{0:T(1024)(128)(4,1)}), s8[4194304]{0:T(1024)(128)(4,1)S(1)}, s32[]{:S(2)}) async-start(s8[6291456]{0:T(1024)(128)(4,1)} %bitcast.126), calls=%async_computation.1 | async-start | bytes 8388608
  208.3 5.0 %slice-start.1 = ((s8[6291456]{0:T(1024)(128)(4,1)}), s8[2097152]{0:T(1024)(128)(4,1)S(1)}, s32[]{:S(2)}) async-start(s8[6291456]{0:T(1024)(128)(4,1)} %bitcast.126), calls=%async_computation.2 | async-start | bytes 4194304
  208.8 23.0 %slice-start.2 = ((s8[6291456]{0:T(1024)(128)(4,1)}), s8[4194304]{0:T(1024)(128)(4,1)S(1)}, s32[]{:S(2)}) async-start(s8[6291456]{0:T(1024)(128)(4,1)} %bitcast.128), calls=%async_computation.3 | async-start | bytes 8388608
  208.8 23.0 %slice-start.4 = ((s8[6291456]{0:T(1024)(128)(4,1)}), s8[4194304]{0:T(1024)(128)(4,1)S(1)}, s32[]{:S(2)}) async-start(s8[6291456]{0:T(1024)(128)(4,1)} %bitcast.136), calls=%async_computation.5 | async-start | bytes 8388608
  208.8 23.0 %slice-start.6 = ((s8[6291456]{0:T(1024)(128)(4,1)}), s8[4194304]{0:T(1024)(128)(4,1)S(1)}, s32[]{:S(2)}) async-start(s8[6291456]{0:T(1024)(128)(4,1)} %bitcast.138), calls=%async_computation.7 | async-start | bytes 8388608
  213.3 11.7 %copy-start.11 = (bf16[768,192]{0,1:T(8,128)(2,1)S(1)}, bf16[768,192]{0,1:T(8,128)(2,1)}, u32[]{:S(2)}) copy-start(bf16[768,192]{0,1:T(8,128)(2,1)} %param.13) | copy-start | bytes 884740
  213.3 18.5 %slice-start.3 = ((s8[6291456]{0:T(1024)(128)(4,1)}), s8[2097152]{0:T(1024)(128)(4,1)S(1)}, s32[]{:S(2)}) async-start(s8[6291456]{0:T(1024)(128)(4,1)} %bitcast.128), calls=%async_computation.4 | async-start | bytes 4194304
  213.3 18.5 %slice-start.5 = ((s8[6291456]{0:T(1024)(128)(4,1)}), s8[2097152]{0:T(1024)(128)(4,1)S(1)}, s32[]{:S(2)}) async-start(s8[6291456]{0:T(1024)(128)(4,1)} %bitcast.136), calls=%async_computation.6 | async-start | bytes 4194304
  213.3 18.5 %slice-start.7 = ((s8[6291456]{0:T(1024)(128)(4,1)}), s8[2097152]{0:T(1024)(128)(4,1)S(1)}, s32[]{:S(2)}) async-start(s8[6291456]{0:T(1024)(128)(4,1)} %bitcast.138), calls=%async_computation.8 | async-start | bytes 4194304
  231.9 6.0 %copy-start.13 = (bf16[768,192]{0,1:T(8,128)(2,1)S(1)}, bf16[768,192]{0,1:T(8,128)(2,1)}, u32[]{:S(2)}) copy-start(bf16[768,192]{0,1:T(8,128)(2,1)} %param.18) | copy-start | bytes 884740
  231.9 8.5 %slice-start.8 = ((f32[16,16,1024]{2,1,0:T(8,128)}), f32[16,16,192]{2,1,0:T(8,128)S(1)}, s32[]{:S(2)}) async-start(f32[16,16,1024]{2,1,0:T(8,128)} %shard_map.165), calls=%async_computation.9 | async-start | bytes 524288 | tf_op jit(solution)/shard_map/slice | solution.py:272
  237.9 4.1 %copy-start.14 = (f32[16,16,192]{2,1,0:T(8,128)S(1)}, f32[16,16,192]{2,1,0:T(8,128)}, u32[]{:S(2)}) copy-start(f32[16,16,192]{2,1,0:T(8,128)} %get-tuple-element.24) | copy-start | bytes 589828
  237.9 5.6 %copy-start.9 = (bf16[768,192]{0,1:T(8,128)(2,1)S(1)}, bf16[768,192]{0,1:T(8,128)(2,1)}, u32[]{:S(2)}) copy-start(bf16[768,192]{0,1:T(8,128)(2,1)} %fusion.49) | copy-start | bytes 884740
  246.0 59.2 %copy-start.1 = (bf16[192,768]{1,0:T(8,128)(2,1)S(1)}, bf16[192,768]{1,0:T(8,128)(2,1)}, u32[]{:S(2)}) copy-start(bf16[192,768]{1,0:T(8,128)(2,1)} %param.14) | copy-start | bytes 884740
  (4 other events, 11.2 us)
Sparse Core Ops, SparseCore 0:
  10.5 100.1 all-gather.1

commit v10 on v9

--- a/solution.py
+++ b/solution.py
@@ -309,8 +309,8 @@
     s_inner_part, s_gain_part = tower_backward(
         s_hat, s_normed, s_pre, s_weights, s_inner_weight, s_hidden_grad
     )
-    q_pieces = q_inner_part.reshape(lax.axis_size("pb"), -1, q_inner_part.shape[-1])
-    s_pieces = s_inner_part.reshape(lax.axis_size("sa"), -1, s_inner_part.shape[-1])
+    q_pieces = q_inner_part.reshape(lax.axis_size("pb"), -1, 128)
+    s_pieces = s_inner_part.reshape(lax.axis_size("sa"), -1, 128)
     gains = jnp.stack([q_gain_part, s_gain_part])
     q_pieces, s_pieces, gains = exchange(
         [

time: 317 us -> 312 us (0.984)
  Pallas kernels: 180 us -> 174 us
  local copies, waits for them, and re-layouts: 19.8 us -> 23 us
    pallas_call x3, Pallas kernels: 86.9 us -> 80.5 us  [exchange(): pl.pallas_call(kernel, out_shape=out_shape, in_specs=[anywhere] * count,...]
where the time goes in v10:
time: 312 us; the launch traced here: 308 us
  Pallas kernels  174 us (56%)
  matrix products  51.1 us (16%)
  other arithmetic  39.2 us (13%)
  local copies, waits for them, and re-layouts  23 us (7%)
  between operations  17.2 us (6%)
  waiting for transfers between devices  3.72 us (1%)
    pallas_call x3, Pallas kernels, plane_gather(): pl.pallas_call(kernel, out_shape=jax.ShapeDtypeStruct((n,) + block.shape,...  93.3 us
    pallas_call x3, Pallas kernels, exchange(): pl.pallas_call(kernel, out_shape=out_shape, in_specs=[anywhere] * count,...  80.5 us
    dot_general x2, matrix products, tower_backward(): lax.dot_general(dpre, rows, (((0,), (0,)), ((), ())), preferred_element_t...  17.7 us
    convert_element_type x2, other arithmetic, tower_backward(): high.astype(jnp.bfloat16)  12.3 us
    unnamed x63, local copies, waits for them, and re-layouts  11 us
    dot_general x2, matrix products, tower_forward(): jnp.einsum('nt,ntd->nd', weights, input_float.reshape(count, length, widt...  10.8 us
    dot_general x2, matrix products, tower_forward(): pre = jnp.dot(normalized_rows, inner, preferred_element_type=jnp.float32)  7.43 us
  transfers between devices with their start and end apart: 1, of which 1 were waited for; matrix products, arithmetic and copies ran while one was open for 10% of the time, Pallas kernels for 22%

profile of v10, /device:TPU:1, one launch (start us, length us, event | category | flops | bytes accessed | tf_op | source)
XLA Modules:
  0.0 308.0 jit_solution(389068705940323019)
XLA Ops:
  9.8 43.7 %shard_map.162 = bf16[16,256,768]{2,1,0:T(8,128)(2,1)} custom-call(bf16[256,768]{1,0:T(8,128)(2,1)} %bitcast.137), custom_call_target="tpu_custom_call" | custom-call | tf_op jit(solution)/shard_map/pallas_call | solution.py:134
  53.6 3.9 %convert_reduce_fusion = f32[16,256]{1,0:T(8,128)S(1)} fusion(bf16[16,256,768]{2,1,0:T(8,128)(2,1)} %shard_map.162), kind=kLoop, calls=%fused_computation.25 | loop fusion | flops 6287360 | bytes 6307840 | tf_op jit(solution)/shard_map/reduce_sum | solution.py:165
  58.7 1.9 multiply_reduce_fusion.1
  60.7 6.5 %reduce-precision_convert_fusion.1 = (bf16[4096,768]{1,0:T(8,128)(2,1)}, bf16[4096,768]{1,0:T(8,128)(2,1)}, bf16[4096,768]{1,0:T(8,128)(2,1)S(1)}) fusion(bf16[16,256,768]{2,1,0:T(8,128)(2,1)S(1)} %copy-done.2, f32[4096]{0:T(1024)S(1)} %bitcast.148, f32[4096]{0:T(1024)S(1)} %bitcast.147, f32[768]{0:T(1024)S(1)} %copy-done.17), kind=kLoop, calls=%fused_computation.15 | loop fusion | flops 28311552 | bytes 25201664 | tf_op jit(solution)/shard_map/convert_element_type | solution.py:213
  67.2 3.7 %multiply_multiply_fusion.3 = (f32[4096,192]{0,1:T(8,128)S(1)}, f32[4096,192]{0,1:T(8,128)}) fusion(bf16[4096,768]{1,0:T(8,128)(2,1)S(1)} %get-tuple-element.66, bf16[768,192]{0,1:T(8,128)(2,1)S(1)} %copy-done.10), kind=kOutput, calls=%fused_computation.51 | convolution fusion | flops 1211105280 | bytes 12877824 | tf_op jit(solution)/shard_map/dot_general | solution.py:191
  70.9 2.7 fusion.32
  75.1 24.6 %shard_map.163 = f32[16,16,768]{2,1,0:T(8,128)} custom-call(f32[16,768]{1,0:T(8,128)} %fusion.78.src), custom_call_target="tpu_custom_call" | custom-call | tf_op jit(solution)/shard_map/pallas_call | solution.py:134
  101.6 5.5 %fusion.64 = f32[16,1,768]{2,1,0:T(1,128)S(1)} fusion(bf16[16,256,768]{2,1,0:T(8,128)(2,1)} %shard_map.162, f32[16,256,1]{1,0,2:T(8,128)S(1)} %get-tuple-element.75), kind=kOutput, calls=%fused_computation.103 | convolution fusion | flops 37748736 | bytes 6356992 | tf_op jit(solution)/shard_map/nt,ntd->nd/dot_general | solution.py:195
  107.7 3.0 all-gather.2.cloned.1.call-done
  110.7 4.2 %multiply_reduce_fusion = f32[16,256]{1,0:T(8,128)S(1)} fusion(bf16[1,16,256,768]{3,2,0,1:T(8,128)(2,1)} %all-gather.2.cloned.1.call-done), kind=kLoop, calls=%fused_computation.22 | loop fusion | flops 9433088 | bytes 6307840 | tf_op jit(solution)/shard_map/reduce_sum | solution.py:162
  115.3 5.8 %reduce-precision_convert_fusion = (bf16[4096,768]{1,0:T(8,128)(2,1)}, bf16[4096,768]{1,0:T(8,128)(2,1)}, bf16[4096,768]{1,0:T(8,128)(2,1)S(1)}) fusion(bf16[1,16,256,768]{3,2,0,1:T(8,128)(2,1)S(1)} %copy-done.3, f32[4096]{0:T(1024)S(1)} %bitcast.140, f32[768]{0:T(1024)S(1)} %copy-done.16), kind=kLoop, calls=%fused_computation.13 | loop fusion | flops 25165824 | bytes 25185280 | tf_op jit(solution)/shard_map/convert_element_type | solution.py:213
  121.1 3.8 %multiply_multiply_fusion.2 = (f32[4096,192]{0,1:T(8,128)S(1)}, f32[4096,192]{0,1:T(8,128)}) fusion(bf16[4096,768]{1,0:T(8,128)(2,1)S(1)} %get-tuple-element.69, bf16[768,192]{0,1:T(8,128)(2,1)S(1)} %copy-done.12), kind=kOutput, calls=%fused_computation.49 | convolution fusion | flops 1211105280 | bytes 12877824 | tf_op jit(solution)/shard_map/dot_general | solution.py:191
  124.9 2.7 fusion.29
  128.4 39.7 %shard_map.164 = (f32[16,16,768]{2,1,0:T(8,128)}, f32[16,16,192]{2,1,0:T(8,128)}, s32[16,1,16]{2,1,0:T(1,128)}, f32[16,16,768]{2,1,0:T(8,128)}) custom-call(f32[16,768]{1,0:T(8,128)} %bitcast_add_fusion.1.refs_0_, f32[16,192]{1,0:T(8,128)} %bitcast.144, s32[1,16]{1,0:T(1,128)} %bitcast.149, f32[16,768]{1,0:T(8,128)} %fusion.79.refs_3_), custom_call_target="tpu_custom_call" | custom-call | tf_op jit(solution)/shard_map/pallas_call | solution.py:66
  169.3 5.3 %fusion.15 = f32[16,1,768]{2,1,0:T(1,128)S(1)} fusion(bf16[1,16,256,768]{3,2,0,1:T(8,128)(2,1)} %all-gather.2.cloned.1.call-done, f32[16,256,1]{1,0,2:T(8,128)S(1)} %get-tuple-element.73), kind=kOutput, calls=%fused_computation.26 | convolution fusion | flops 37748736 | bytes 6356992 | tf_op jit(solution)/shard_map/nt,ntd->nd/dot_general | solution.py:195
  175.3 24.9 %shard_map.165 = f32[16,16,1024]{2,1,0:T(8,128)} custom-call(f32[16,1024]{1,0:T(8,128)} %maximum_maximum_fusion.src), custom_call_target="tpu_custom_call" | custom-call | tf_op jit(solution)/shard_map/pallas_call | solution.py:134
  205.5 2.4 convolution_multiply_fusion
  208.8 4.5 %copy.54 = f32[24,8,16,256]{3,1,2,0:T(8,128)} copy(f32[24,8,16,256]{3,2,1,0:T(8,128)S(1)} %bitcast.124) | data formatting | bytes 6291456
  213.3 11.7 %fusion = f32[192,2304]{1,0:T(8,128)} fusion(bf16[4096,768]{1,0:T(8,128)(2,1)} %get-tuple-element.65, bf16[4096,768]{1,0:T(8,128)(2,1)} %get-tuple-element.64, bf16[4096,768]{1,0:T(8,128)(2,1)S(1)} %bitcast.119, f32[4096,192]{0,1:T(8,128)} %get-tuple-element.77, f32[4096,192]{0,1:T(8,128)} %bitcast.133, f32[4096]{0:T(1024)} %div.72), kind=kOutput, calls=%fused_computation | convolution fusion | flops 3689152512 | bytes 26951680 | tf_op jit(solution)/shard_map/dot_general | solution.py:215
  226.4 1.8 fusion.49
  229.0 2.8 copy.57
  231.9 6.0 %fusion.6 = f32[192,2304]{1,0:T(8,128)} fusion(bf16[4096,768]{1,0:T(8,128)(2,1)S(1)} %bitcast.131, bf16[4096,768]{1,0:T(8,128)(2,1)S(1)} %bitcast.129, bf16[4096,768]{1,0:T(8,128)(2,1)S(1)} %bitcast.121, f32[4096,192]{0,1:T(8,128)S(1)} %copy-done.6, f32[4096,192]{0,1:T(8,128)S(1)} %bitcast.134, f32[4096]{0:T(1024)S(1)} %div.75), kind=kOutput, calls=%fused_computation.6 | convolution fusion | flops 3689152512 | bytes 26951680 | tf_op jit(solution)/shard_map/dot_general | solution.py:215
  246.8 20.5 %shard_map.166 = (bf16[16,72,128]{2,1,0:T(8,128)(2,1)}, bf16[16,72,128]{2,1,0:T(8,128)(2,1)}, f32[16,2,768]{2,1,0:T(2,128)}) custom-call(bf16[16,72,128]{2,1,0:T(8,128)(2,1)} %convert_element_type.104.refs_0_, bf16[16,72,128]{2,1,0:T(8,128)(2,1)} %convert_element_type.111.refs_1_, f32[2,768]{1,0:T(2,128)} %pad_maximum_fusion.refs_2_), custom_call_target="tpu_custom_call" | custom-call | tf_op jit(solution)/shard_map/pallas_call | solution.py:66
  272.1 20.3 %shard_map.167 = (bf16[16,72,128]{2,1,0:T(8,128)(2,1)}, bf16[16,72,128]{2,1,0:T(8,128)(2,1)}, f32[16,2,768]{2,1,0:T(2,128)}) custom-call(bf16[72,128]{1,0:T(8,128)(2,1)} %reduce_sum.192.refs_0_, bf16[72,128]{1,0:T(8,128)(2,1)} %reduce_sum.193.refs_1_, f32[2,768]{1,0:T(2,128)} %reduce_sum.194.refs_2_), custom_call_target="tpu_custom_call" | custom-call | tf_op jit(solution)/shard_map/pallas_call | solution.py:66
  (122 shorter events, 38.9 us)
Async XLA Ops:
  7.2 67.0 %copy-start = (bf16[192,768]{1,0:T(8,128)(2,1)S(1)}, bf16[192,768]{1,0:T(8,128)(2,1)}, u32[]{:S(2)}) copy-start(bf16[192,768]{1,0:T(8,128)(2,1)} %param.14) | copy-start | bytes 884740
  7.2 103.5 %all-gather.2.cloned.1.call-start = ((), (), s32[]{:S(2)}) async-start(), calls=%async_computation | async-start | bytes 6684672 | tf_op jit(solution)/shard_map/all_gather | solution.py:241
  53.6 5.1 %copy-start.2 = (bf16[16,256,768]{2,1,0:T(8,128)(2,1)S(1)}, bf16[16,256,768]{2,1,0:T(8,128)(2,1)}, u32[]{:S(2)}) copy-start(bf16[16,256,768]{2,1,0:T(8,128)(2,1)} %shard_map.162) | copy-start | bytes 18874372
  60.7 6.5 %copy-start.10 = (bf16[768,192]{0,1:T(8,128)(2,1)S(1)}, bf16[768,192]{0,1:T(8,128)(2,1)}, u32[]{:S(2)}) copy-start(bf16[768,192]{0,1:T(8,128)(2,1)} %param.13) | copy-start | bytes 884740
  107.6 7.3 %copy-start.16 = (f32[768]{0:T(1024)S(1)}, f32[768]{0:T(1024)}, u32[]{:S(2)}) copy-start(f32[768]{0:T(1024)} %param.20) | copy-start | bytes 9220
  110.7 4.6 %copy-start.3 = (bf16[1,16,256,768]{3,2,0,1:T(8,128)(2,1)S(1)}, bf16[1,16,256,768]{3,2,0,1:T(8,128)(2,1)}, u32[]{:S(2)}) copy-start(bf16[1,16,256,768]{3,2,0,1:T(8,128)(2,1)} %all-gather.2.cloned.1.call-done) | copy-start | bytes 18874372
  115.3 5.8 %copy-start.12 = (bf16[768,192]{0,1:T(8,128)(2,1)S(1)}, bf16[768,192]{0,1:T(8,128)(2,1)}, u32[]{:S(2)}) copy-start(bf16[768,192]{0,1:T(8,128)(2,1)} %param.18) | copy-start | bytes 884740
  121.1 3.8 %copy-start.5 = (bf16[4096,768]{1,0:T(8,128)(2,1)}, bf16[4096,768]{1,0:T(8,128)(2,1)S(1)}, u32[]{:S(2)}) copy-start(bf16[4096,768]{1,0:T(8,128)(2,1)S(1)} %get-tuple-element.69) | copy-start | bytes 18874372
  174.6 27.3 %copy-start.15 = (s32[16,1,16]{2,1,0:T(1,128)S(1)}, s32[16,1,16]{2,1,0:T(1,128)}, u32[]{:S(2)}) copy-start(s32[16,1,16]{2,1,0:T(1,128)} %get-tuple-element.19) | copy-start | bytes 3076
  174.6 28.1 %copy-start.7 = (f32[16,16,768]{2,1,0:T(8,128)S(1)}, f32[16,16,768]{2,1,0:T(8,128)}, u32[]{:S(2)}) copy-start(f32[16,16,768]{2,1,0:T(8,128)} %get-tuple-element.17) | copy-start | bytes 2359300
  204.6 8.7 %slice-start = ((s8[6291456]{0:T(1024)(128)(4,1)}), s8[4194304]{0:T(1024)(128)(4,1)S(1)}, s32[]{:S(2)}) async-start(s8[6291456]{0:T(1024)(128)(4,1)} %bitcast.118), calls=%async_computation.1 | async-start | bytes 8388608
  208.3 5.0 %slice-start.1 = ((s8[6291456]{0:T(1024)(128)(4,1)}), s8[2097152]{0:T(1024)(128)(4,1)S(1)}, s32[]{:S(2)}) async-start(s8[6291456]{0:T(1024)(128)(4,1)} %bitcast.118), calls=%async_computation.2 | async-start | bytes 4194304
  208.8 23.0 %slice-start.2 = ((s8[6291456]{0:T(1024)(128)(4,1)}), s8[4194304]{0:T(1024)(128)(4,1)S(1)}, s32[]{:S(2)}) async-start(s8[6291456]{0:T(1024)(128)(4,1)} %bitcast.120), calls=%async_computation.3 | async-start | bytes 8388608
  208.8 23.0 %slice-start.4 = ((s8[6291456]{0:T(1024)(128)(4,1)}), s8[4194304]{0:T(1024)(128)(4,1)S(1)}, s32[]{:S(2)}) async-start(s8[6291456]{0:T(1024)(128)(4,1)} %bitcast.128), calls=%async_computation.5 | async-start | bytes 8388608
  208.8 23.0 %slice-start.6 = ((s8[6291456]{0:T(1024)(128)(4,1)}), s8[4194304]{0:T(1024)(128)(4,1)S(1)}, s32[]{:S(2)}) async-start(s8[6291456]{0:T(1024)(128)(4,1)} %bitcast.130), calls=%async_computation.7 | async-start | bytes 8388608
  213.3 11.7 %copy-start.11 = (bf16[768,192]{0,1:T(8,128)(2,1)S(1)}, bf16[768,192]{0,1:T(8,128)(2,1)}, u32[]{:S(2)}) copy-start(bf16[768,192]{0,1:T(8,128)(2,1)} %param.13) | copy-start | bytes 884740
  213.3 18.5 %slice-start.3 = ((s8[6291456]{0:T(1024)(128)(4,1)}), s8[2097152]{0:T(1024)(128)(4,1)S(1)}, s32[]{:S(2)}) async-start(s8[6291456]{0:T(1024)(128)(4,1)} %bitcast.120), calls=%async_computation.4 | async-start | bytes 4194304
  213.3 18.5 %slice-start.5 = ((s8[6291456]{0:T(1024)(128)(4,1)}), s8[2097152]{0:T(1024)(128)(4,1)S(1)}, s32[]{:S(2)}) async-start(s8[6291456]{0:T(1024)(128)(4,1)} %bitcast.128), calls=%async_computation.6 | async-start | bytes 4194304
  213.3 18.5 %slice-start.7 = ((s8[6291456]{0:T(1024)(128)(4,1)}), s8[2097152]{0:T(1024)(128)(4,1)S(1)}, s32[]{:S(2)}) async-start(s8[6291456]{0:T(1024)(128)(4,1)} %bitcast.130), calls=%async_computation.8 | async-start | bytes 4194304
  231.9 6.0 %copy-start.13 = (bf16[768,192]{0,1:T(8,128)(2,1)S(1)}, bf16[768,192]{0,1:T(8,128)(2,1)}, u32[]{:S(2)}) copy-start(bf16[768,192]{0,1:T(8,128)(2,1)} %param.18) | copy-start | bytes 884740
  231.9 8.5 %slice-start.8 = ((f32[16,16,1024]{2,1,0:T(8,128)}), f32[16,16,192]{2,1,0:T(8,128)S(1)}, s32[]{:S(2)}) async-start(f32[16,16,1024]{2,1,0:T(8,128)} %shard_map.165), calls=%async_computation.9 | async-start | bytes 524288 | tf_op jit(solution)/shard_map/slice | solution.py:272
  237.9 4.1 %copy-start.14 = (f32[16,16,192]{2,1,0:T(8,128)S(1)}, f32[16,16,192]{2,1,0:T(8,128)}, u32[]{:S(2)}) copy-start(f32[16,16,192]{2,1,0:T(8,128)} %get-tuple-element.24) | copy-start | bytes 589828
  237.9 5.6 %copy-start.9 = (bf16[768,192]{0,1:T(8,128)(2,1)S(1)}, bf16[768,192]{0,1:T(8,128)(2,1)}, u32[]{:S(2)}) copy-start(bf16[768,192]{0,1:T(8,128)(2,1)} %fusion.49) | copy-start | bytes 884740
  246.2 53.6 %copy-start.1 = (bf16[192,768]{1,0:T(8,128)(2,1)S(1)}, bf16[192,768]{1,0:T(8,128)(2,1)}, u32[]{:S(2)}) copy-start(bf16[192,768]{1,0:T(8,128)(2,1)} %param.14) | copy-start | bytes 884740
  (4 other events, 11.2 us)
Sparse Core Ops, SparseCore 0:
  10.5 100.1 all-gather.1

commit v11 on v10

--- a/solution.py
+++ b/solution.py
@@ -255,7 +255,7 @@
     q_embed, q_pooled_all, positive_all, s_terms = exchange(
         [
             (q_block, "pb", False),
-            (q_pooled, "pb", False),
+            (q_pooled.reshape(-1, 128), "pb", False),
             (positive_column.reshape(1, -1), "pb", False),
             (jnp.dot(s_pooled, s_outer_f, precision=HIGH), "pb", False),
         ],

time: 312 us -> 312 us (level)
  Pallas kernels: 174 us -> 164 us
  waiting for transfers between devices: 3.72 us -> 12.2 us
    all_gather x1, waiting for transfers between devices: 3.04 us -> 11.5 us  [per_device(): s_tokens = lax.all_gather(sql_states, 'pb', axis=1, tiled=True)[0]]
    pallas_call x3, Pallas kernels: 93.3 us -> 86 us  [plane_gather(): pl.pallas_call(kernel, out_shape=jax.ShapeDtypeStruct((n,) + block.shape,...]
    unnamed x63 -> x61, local copies, waits for them, and re-layouts: 11 us -> 11 us
  transfers between devices with their start and end apart: 1 -> 1, of which waited for: 1 -> 1; matrix products, arithmetic and copies ran while one was open for 10% -> 10% of each run, Pallas kernels for 22% -> 20%
where the time goes in v11:
time: 312 us; the launch traced here: 308 us
  Pallas kernels  164 us (53%)
  matrix products  51.1 us (16%)
  other arithmetic  38.9 us (12%)
  local copies, waits for them, and re-layouts  24.1 us (8%)
  between operations  17.2 us (6%)
  waiting for transfers between devices  12.2 us (4%)
    pallas_call x3, Pallas kernels, plane_gather(): pl.pallas_call(kernel, out_shape=jax.ShapeDtypeStruct((n,) + block.shape,...  86 us
    pallas_call x3, Pallas kernels, exchange(): pl.pallas_call(kernel, out_shape=out_shape, in_specs=[anywhere] * count,...  78.1 us
    dot_general x2, matrix products, tower_backward(): lax.dot_general(dpre, rows, (((0,), (0,)), ((), ())), preferred_element_t...  17.7 us
    convert_element_type x2, other arithmetic, tower_backward(): high.astype(jnp.bfloat16)  12 us
    all_gather x1, waiting for transfers between devices, per_device(): s_tokens = lax.all_gather(sql_states, 'pb', axis=1, tiled=True)[0]  11.5 us
    unnamed x61, local copies, waits for them, and re-layouts  11 us
    dot_general x2, matrix products, tower_forward(): jnp.einsum('nt,ntd->nd', weights, input_float.reshape(count, length, widt...  10.7 us
    dot_general x2, matrix products, tower_forward(): pre = jnp.dot(normalized_rows, inner, preferred_element_type=jnp.float32)  7.65 us
  transfers between devices with their start and end apart: 1, of which 1 were waited for; matrix products, arithmetic and copies ran while one was open for 10% of the time, Pallas kernels for 20%

profile of v11, /device:TPU:1, one launch (start us, length us, event | category | flops | bytes accessed | tf_op | source)
XLA Modules:
  0.0 307.7 jit_solution(13129743952892013464)
XLA Ops:
  9.8 43.7 %shard_map.162 = bf16[16,256,768]{2,1,0:T(8,128)(2,1)} custom-call(bf16[256,768]{1,0:T(8,128)(2,1)} %bitcast.136), custom_call_target="tpu_custom_call" | custom-call | tf_op jit(solution)/shard_map/pallas_call | solution.py:134
  53.6 3.9 %convert_reduce_fusion = f32[16,256]{1,0:T(8,128)S(1)} fusion(bf16[16,256,768]{2,1,0:T(8,128)(2,1)} %shard_map.162), kind=kLoop, calls=%fused_computation.25 | loop fusion | flops 6287360 | bytes 6307840 | tf_op jit(solution)/shard_map/reduce_sum | solution.py:165
  58.7 1.9 multiply_reduce_fusion.1
  60.7 6.2 %reduce-precision_convert_fusion.1 = (bf16[4096,768]{1,0:T(8,128)(2,1)}, bf16[4096,768]{1,0:T(8,128)(2,1)}, bf16[4096,768]{1,0:T(8,128)(2,1)S(1)}) fusion(bf16[16,256,768]{2,1,0:T(8,128)(2,1)S(1)} %copy-done.2, f32[4096]{0:T(1024)S(1)} %bitcast.146, f32[4096]{0:T(1024)S(1)} %bitcast.145, f32[768]{0:T(1024)S(1)} %copy-done.16), kind=kLoop, calls=%fused_computation.15 | loop fusion | flops 28311552 | bytes 25201664 | tf_op jit(solution)/shard_map/convert_element_type | solution.py:213
  66.9 3.7 %multiply_multiply_fusion.3 = (f32[4096,192]{0,1:T(8,128)S(1)}, f32[4096,192]{0,1:T(8,128)}) fusion(bf16[4096,768]{1,0:T(8,128)(2,1)S(1)} %get-tuple-element.66, bf16[768,192]{0,1:T(8,128)(2,1)S(1)} %copy-done.10), kind=kOutput, calls=%fused_computation.51 | convolution fusion | flops 1211105280 | bytes 12877824 | tf_op jit(solution)/shard_map/dot_general | solution.py:191
  70.6 2.7 fusion.32
  74.8 16.8 %shard_map.163 = f32[16,16,768]{2,1,0:T(8,128)} custom-call(f32[16,768]{1,0:T(8,128)} %fusion.78.src), custom_call_target="tpu_custom_call" | custom-call | tf_op jit(solution)/shard_map/pallas_call | solution.py:134
  93.5 5.3 %fusion.64 = f32[16,1,768]{2,1,0:T(1,128)S(1)} fusion(bf16[16,256,768]{2,1,0:T(8,128)(2,1)} %shard_map.162, f32[16,256,1]{1,0,2:T(8,128)S(1)} %get-tuple-element.75), kind=kOutput, calls=%fused_computation.103 | convolution fusion | flops 37748736 | bytes 6356992 | tf_op jit(solution)/shard_map/nt,ntd->nd/dot_general | solution.py:195
  99.4 11.5 %all-gather.2.cloned.1.call-done = bf16[1,16,256,768]{3,2,0,1:T(8,128)(2,1)} async-done(((bf16[1,1,256,768]{3,2,0,1:T(8,128)(2,1)}), bf16[1,16,256,768]{3,2,0,1:T(8,128)(2,1)}) %all-gather.2.cloned.1.call-update) | async-done | bytes 6291472 | tf_op jit(solution)/shard_map/all_gather | solution.py:241
  111.0 4.2 %multiply_reduce_fusion = f32[16,256]{1,0:T(8,128)S(1)} fusion(bf16[1,16,256,768]{3,2,0,1:T(8,128)(2,1)} %all-gather.2.cloned.1.call-done), kind=kLoop, calls=%fused_computation.22 | loop fusion | flops 9433088 | bytes 6307840 | tf_op jit(solution)/shard_map/reduce_sum | solution.py:162
  115.6 5.8 %reduce-precision_convert_fusion = (bf16[4096,768]{1,0:T(8,128)(2,1)}, bf16[4096,768]{1,0:T(8,128)(2,1)}, bf16[4096,768]{1,0:T(8,128)(2,1)S(1)}) fusion(bf16[1,16,256,768]{3,2,0,1:T(8,128)(2,1)S(1)} %copy-done.3, f32[4096]{0:T(1024)S(1)} %bitcast.138, f32[768]{0:T(1024)S(1)} %copy-done.15), kind=kLoop, calls=%fused_computation.13 | loop fusion | flops 25165824 | bytes 25185280 | tf_op jit(solution)/shard_map/convert_element_type | solution.py:213
  121.4 4.0 %multiply_multiply_fusion.2 = (f32[4096,192]{0,1:T(8,128)S(1)}, f32[4096,192]{0,1:T(8,128)}) fusion(bf16[4096,768]{1,0:T(8,128)(2,1)S(1)} %get-tuple-element.69, bf16[768,192]{0,1:T(8,128)(2,1)S(1)} %copy-done.12), kind=kOutput, calls=%fused_computation.49 | convolution fusion | flops 1211105280 | bytes 12877824 | tf_op jit(solution)/shard_map/dot_general | solution.py:191
  125.4 2.7 fusion.29
  128.9 38.0 %shard_map.164 = (f32[16,16,768]{2,1,0:T(8,128)}, f32[16,24,128]{2,1,0:T(8,128)}, s32[16,1,16]{2,1,0:T(1,128)}, f32[16,16,768]{2,1,0:T(8,128)}) custom-call(f32[16,768]{1,0:T(8,128)} %bitcast_add_fusion.1.refs_0_, f32[24,128]{1,0:T(8,128)} %reshape.191.refs_1_, s32[1,16]{1,0:T(1,128)} %bitcast.147, f32[16,768]{1,0:T(8,128)} %fusion.79.refs_3_), custom_call_target="tpu_custom_call" | custom-call | tf_op jit(solution)/shard_map/pallas_call | solution.py:66
  168.2 5.3 %fusion.15 = f32[16,1,768]{2,1,0:T(1,128)S(1)} fusion(bf16[1,16,256,768]{3,2,0,1:T(8,128)(2,1)} %all-gather.2.cloned.1.call-done, f32[16,256,1]{1,0,2:T(8,128)S(1)} %get-tuple-element.73), kind=kOutput, calls=%fused_computation.26 | convolution fusion | flops 37748736 | bytes 6356992 | tf_op jit(solution)/shard_map/nt,ntd->nd/dot_general | solution.py:195
  174.2 25.6 %shard_map.165 = f32[16,16,1024]{2,1,0:T(8,128)} custom-call(f32[16,1024]{1,0:T(8,128)} %maximum_maximum_fusion.src), custom_call_target="tpu_custom_call" | custom-call | tf_op jit(solution)/shard_map/pallas_call | solution.py:134
  205.0 2.4 convolution_multiply_fusion
  208.3 4.5 %copy.54 = f32[24,8,16,256]{3,1,2,0:T(8,128)} copy(f32[24,8,16,256]{3,2,1,0:T(8,128)S(1)} %bitcast.123) | data formatting | bytes 6291456
  212.8 11.7 %fusion = f32[192,2304]{1,0:T(8,128)} fusion(bf16[4096,768]{1,0:T(8,128)(2,1)} %get-tuple-element.65, bf16[4096,768]{1,0:T(8,128)(2,1)} %get-tuple-element.64, bf16[4096,768]{1,0:T(8,128)(2,1)S(1)} %bitcast.118, f32[4096,192]{0,1:T(8,128)} %get-tuple-element.77, f32[4096,192]{0,1:T(8,128)} %bitcast.132, f32[4096]{0:T(1024)} %div.72), kind=kOutput, calls=%fused_computation | convolution fusion | flops 3689152512 | bytes 26951680 | tf_op jit(solution)/shard_map/dot_general | solution.py:215
  225.8 1.8 fusion.49
  228.5 2.8 copy.57
  231.4 6.0 %fusion.6 = f32[192,2304]{1,0:T(8,128)} fusion(bf16[4096,768]{1,0:T(8,128)(2,1)S(1)} %bitcast.130, bf16[4096,768]{1,0:T(8,128)(2,1)S(1)} %bitcast.128, bf16[4096,768]{1,0:T(8,128)(2,1)S(1)} %bitcast.120, f32[4096,192]{0,1:T(8,128)S(1)} %copy-done.6, f32[4096,192]{0,1:T(8,128)S(1)} %bitcast.133, f32[4096]{0:T(1024)S(1)} %div.75), kind=kOutput, calls=%fused_computation.6 | convolution fusion | flops 3689152512 | bytes 26951680 | tf_op jit(solution)/shard_map/dot_general | solution.py:215
  247.3 19.7 %shard_map.166 = (bf16[16,72,128]{2,1,0:T(8,128)(2,1)}, bf16[16,72,128]{2,1,0:T(8,128)(2,1)}, f32[16,2,768]{2,1,0:T(2,128)}) custom-call(bf16[16,72,128]{2,1,0:T(8,128)(2,1)} %convert_element_type.104.refs_0_, bf16[16,72,128]{2,1,0:T(8,128)(2,1)} %convert_element_type.111.refs_1_, f32[2,768]{1,0:T(2,128)} %pad_maximum_fusion.refs_2_), custom_call_target="tpu_custom_call" | custom-call | tf_op jit(solution)/shard_map/pallas_call | solution.py:66
  271.7 20.4 %shard_map.167 = (bf16[16,72,128]{2,1,0:T(8,128)(2,1)}, bf16[16,72,128]{2,1,0:T(8,128)(2,1)}, f32[16,2,768]{2,1,0:T(2,128)}) custom-call(bf16[72,128]{1,0:T(8,128)(2,1)} %reduce_sum.192.refs_0_, bf16[72,128]{1,0:T(8,128)(2,1)} %reduce_sum.193.refs_1_, f32[2,768]{1,0:T(2,128)} %reduce_sum.194.refs_2_), custom_call_target="tpu_custom_call" | custom-call | tf_op jit(solution)/shard_map/pallas_call | solution.py:66
  (122 shorter events, 40.0 us)
Async XLA Ops:
  7.2 66.8 %copy-start = (bf16[192,768]{1,0:T(8,128)(2,1)S(1)}, bf16[192,768]{1,0:T(8,128)(2,1)}, u32[]{:S(2)}) copy-start(bf16[192,768]{1,0:T(8,128)(2,1)} %param.14) | copy-start | bytes 884740
  7.2 103.8 %all-gather.2.cloned.1.call-start = ((), (), s32[]{:S(2)}) async-start(), calls=%async_computation | async-start | bytes 6684672 | tf_op jit(solution)/shard_map/all_gather | solution.py:241
  53.6 5.1 %copy-start.2 = (bf16[16,256,768]{2,1,0:T(8,128)(2,1)S(1)}, bf16[16,256,768]{2,1,0:T(8,128)(2,1)}, u32[]{:S(2)}) copy-start(bf16[16,256,768]{2,1,0:T(8,128)(2,1)} %shard_map.162) | copy-start | bytes 18874372
  60.7 6.2 %copy-start.10 = (bf16[768,192]{0,1:T(8,128)(2,1)S(1)}, bf16[768,192]{0,1:T(8,128)(2,1)}, u32[]{:S(2)}) copy-start(bf16[768,192]{0,1:T(8,128)(2,1)} %param.13) | copy-start | bytes 884740
  66.9 3.7 %copy-start.4 = (bf16[4096,768]{1,0:T(8,128)(2,1)}, bf16[4096,768]{1,0:T(8,128)(2,1)S(1)}, u32[]{:S(2)}) copy-start(bf16[4096,768]{1,0:T(8,128)(2,1)S(1)} %get-tuple-element.66) | copy-start | bytes 18874372
  99.4 15.8 %copy-start.15 = (f32[768]{0:T(1024)S(1)}, f32[768]{0:T(1024)}, u32[]{:S(2)}) copy-start(f32[768]{0:T(1024)} %param.20) | copy-start | bytes 9220
  111.0 4.6 %copy-start.3 = (bf16[1,16,256,768]{3,2,0,1:T(8,128)(2,1)S(1)}, bf16[1,16,256,768]{3,2,0,1:T(8,128)(2,1)}, u32[]{:S(2)}) copy-start(bf16[1,16,256,768]{3,2,0,1:T(8,128)(2,1)} %all-gather.2.cloned.1.call-done) | copy-start | bytes 18874372
  115.6 5.8 %copy-start.12 = (bf16[768,192]{0,1:T(8,128)(2,1)S(1)}, bf16[768,192]{0,1:T(8,128)(2,1)}, u32[]{:S(2)}) copy-start(bf16[768,192]{0,1:T(8,128)(2,1)} %param.18) | copy-start | bytes 884740
  121.3 4.0 %copy-start.5 = (bf16[4096,768]{1,0:T(8,128)(2,1)}, bf16[4096,768]{1,0:T(8,128)(2,1)S(1)}, u32[]{:S(2)}) copy-start(bf16[4096,768]{1,0:T(8,128)(2,1)S(1)} %get-tuple-element.69) | copy-start | bytes 18874372
  173.5 27.9 %copy-start.14 = (s32[16,1,16]{2,1,0:T(1,128)S(1)}, s32[16,1,16]{2,1,0:T(1,128)}, u32[]{:S(2)}) copy-start(s32[16,1,16]{2,1,0:T(1,128)} %get-tuple-element.19) | copy-start | bytes 3076
  173.5 28.7 %copy-start.7 = (f32[16,16,768]{2,1,0:T(8,128)S(1)}, f32[16,16,768]{2,1,0:T(8,128)}, u32[]{:S(2)}) copy-start(f32[16,16,768]{2,1,0:T(8,128)} %get-tuple-element.17) | copy-start | bytes 2359300
  204.0 8.7 %slice-start = ((s8[6291456]{0:T(1024)(128)(4,1)}), s8[4194304]{0:T(1024)(128)(4,1)S(1)}, s32[]{:S(2)}) async-start(s8[6291456]{0:T(1024)(128)(4,1)} %bitcast.117), calls=%async_computation.1 | async-start | bytes 8388608
  207.8 5.0 %slice-start.1 = ((s8[6291456]{0:T(1024)(128)(4,1)}), s8[2097152]{0:T(1024)(128)(4,1)S(1)}, s32[]{:S(2)}) async-start(s8[6291456]{0:T(1024)(128)(4,1)} %bitcast.117), calls=%async_computation.2 | async-start | bytes 4194304
  208.3 23.0 %slice-start.2 = ((s8[6291456]{0:T(1024)(128)(4,1)}), s8[4194304]{0:T(1024)(128)(4,1)S(1)}, s32[]{:S(2)}) async-start(s8[6291456]{0:T(1024)(128)(4,1)} %bitcast.119), calls=%async_computation.3 | async-start | bytes 8388608
  208.3 23.0 %slice-start.4 = ((s8[6291456]{0:T(1024)(128)(4,1)}), s8[4194304]{0:T(1024)(128)(4,1)S(1)}, s32[]{:S(2)}) async-start(s8[6291456]{0:T(1024)(128)(4,1)} %bitcast.127), calls=%async_computation.5 | async-start | bytes 8388608
  208.3 23.0 %slice-start.6 = ((s8[6291456]{0:T(1024)(128)(4,1)}), s8[4194304]{0:T(1024)(128)(4,1)S(1)}, s32[]{:S(2)}) async-start(s8[6291456]{0:T(1024)(128)(4,1)} %bitcast.129), calls=%async_computation.7 | async-start | bytes 8388608
  212.8 11.7 %copy-start.11 = (bf16[768,192]{0,1:T(8,128)(2,1)S(1)}, bf16[768,192]{0,1:T(8,128)(2,1)}, u32[]{:S(2)}) copy-start(bf16[768,192]{0,1:T(8,128)(2,1)} %param.13) | copy-start | bytes 884740
  212.8 18.5 %slice-start.3 = ((s8[6291456]{0:T(1024)(128)(4,1)}), s8[2097152]{0:T(1024)(128)(4,1)S(1)}, s32[]{:S(2)}) async-start(s8[6291456]{0:T(1024)(128)(4,1)} %bitcast.119), calls=%async_computation.4 | async-start | bytes 4194304
  212.8 18.5 %slice-start.5 = ((s8[6291456]{0:T(1024)(128)(4,1)}), s8[2097152]{0:T(1024)(128)(4,1)S(1)}, s32[]{:S(2)}) async-start(s8[6291456]{0:T(1024)(128)(4,1)} %bitcast.127), calls=%async_computation.6 | async-start | bytes 4194304
  212.8 18.5 %slice-start.7 = ((s8[6291456]{0:T(1024)(128)(4,1)}), s8[2097152]{0:T(1024)(128)(4,1)S(1)}, s32[]{:S(2)}) async-start(s8[6291456]{0:T(1024)(128)(4,1)} %bitcast.129), calls=%async_computation.8 | async-start | bytes 4194304
  231.4 6.0 %copy-start.13 = (bf16[768,192]{0,1:T(8,128)(2,1)S(1)}, bf16[768,192]{0,1:T(8,128)(2,1)}, u32[]{:S(2)}) copy-start(bf16[768,192]{0,1:T(8,128)(2,1)} %param.18) | copy-start | bytes 884740
  231.4 9.5 %slice-start.8 = ((f32[16,16,1024]{2,1,0:T(8,128)}), f32[16,16,192]{2,1,0:T(8,128)S(1)}, s32[]{:S(2)}) async-start(f32[16,16,1024]{2,1,0:T(8,128)} %shard_map.165), calls=%async_computation.9 | async-start | bytes 524288 | tf_op jit(solution)/shard_map/slice | solution.py:272
  237.4 6.6 %copy-start.9 = (bf16[768,192]{0,1:T(8,128)(2,1)S(1)}, bf16[768,192]{0,1:T(8,128)(2,1)}, u32[]{:S(2)}) copy-start(bf16[768,192]{0,1:T(8,128)(2,1)} %fusion.49) | copy-start | bytes 884740
  246.7 52.8 %copy-start.1 = (bf16[192,768]{1,0:T(8,128)(2,1)S(1)}, bf16[192,768]{1,0:T(8,128)(2,1)}, u32[]{:S(2)}) copy-start(bf16[192,768]{1,0:T(8,128)(2,1)} %param.14) | copy-start | bytes 884740
  (3 other events, 7.5 us)
Sparse Core Ops, SparseCore 0:
  10.5 100.4 all-gather.1
